TPU v7x, 128 devices: a whole 4x4x4 slice. The times are simulated.
128 devices in a mesh: patch: 32 (over y, z, core), visit: 4 (over x).
Axes of the slice: x: 4, y: 4, z: 4, core: 2. Of those that a mesh axis runs over, the one named last changes fastest.
Arguments:
- ccd_rows: float32 [32, 1024, 4096], P('visit', 'patch'), may hold values from -6 to 6
- tract_row: int32 [32, 1024], P('visit', 'patch'), may hold values from 0 to 1023, as said below
- warp_taps: float32 [32, 32, 8, 4096], P('visit', 'patch'), may hold values from -0.25 to 0.5
- warp_shift: int32 [32, 32, 4096], P('visit', 'patch'), may hold values from -64 to 56
- basis_rows: float32 [9, 21], replicated, may hold values from -1 to 1
- basis_cols: float32 [9, 21], replicated, may hold values from -1 to 1
- coef_table: float32 [32, 32, 9, 32], P('visit', 'patch'), may hold values from -2 to 2
- grid_index: int32 [32, 4096], P('patch'), may hold values from 0 to 31
- template: float32 [1024, 4096], P('patch'), may hold values from -6 to 6
- visit_weight: float32 [32], replicated, may hold values from 0.2 to 5
Outputs:
- difference: float32 [32, 1024, 4096], P('visit', 'patch')
- coadd: float32 [1024, 4096], P(('patch', 'visit'))
Inputs may be any that keep to these rules, and one draw needn't show every extreme that they name: In each visit, tract_row is a permutation of the tract rows. For visit q with group g = q // 8 and l = q % 8, a value v among the rows held by patch index s (rows s * 32 to s * 32 + 31) lies in patch v // 32 = s + o_g - l + (v % 32) // 2 modulo the patch axis's size, with o_g one integer for all visits of group g. So the rows of one visit held on one device reach a patch either 2 times or never, with distinct v % 2, and the rows of one device reach one patch at most min(8, 16) * 2 times, exactly that often for one patch.
All inputs are finite; a program needn't handle non-finite values.
Results may differ from a plain program's by a relative error of at most 0.0003.
Values sent between devices are 32-bit elements; how exact they have to be, the bound alone decides.
A program may use at most 128 MiB of HBM per device.

v0:
```python
import jax
import jax.numpy as jnp
from jax import lax
from jax.sharding import PartitionSpec as P

precise = lax.Precision.HIGHEST
tile_width = 128
edge_width = 16


def padded_2(cells, sides, width):
    for axis, dim in sides:
        count = lax.axis_size(axis)
        ends = count - 1
        head = lax.slice_in_dim(cells, 0, width, axis=dim)
        tail = lax.slice_in_dim(cells, cells.shape[dim] - width, cells.shape[dim], axis=dim)
        cells = jnp.concatenate(
            [
                lax.ppermute(tail, axis, [(i, (i + 1) % count) for i in range(ends)]),
                cells,
                lax.ppermute(head, axis, [((i + 1) % count, i) for i in range(ends)]),
            ],
            axis=dim,
        )
    return cells


def band_table(values, spread):
    table = jnp.zeros((values.shape[0],) + spread.shape, jnp.float32)
    for lag in range(values.shape[1]):
        table = table + jnp.where(
            (spread == lag)[None], values[:, lag].reshape((-1,) + (1,) * spread.ndim), 0.0
        )
    return table


def inverse_places(places, count):
    source_ids = jnp.arange(places.shape[0], dtype=jnp.int32)
    found = jnp.full((count + 1,), places.shape[0], jnp.int32).at[places].set(source_ids)[:count]
    return (found, found < places.shape[0])


def pick_rows(rows, found, valid):
    picked = jnp.take(rows, jnp.minimum(found, rows.shape[0] - 1), axis=0)
    return jnp.where(valid[:, None], picked, 0.0)


def warp_visit(pieces):
    images, taps, shift = pieces
    patch_rows, row_width = images.shape
    tiles = row_width // tile_width
    spread = (
        jnp.arange(3 * tile_width)[None, :, None]
        - tile_width
        - jnp.arange(tile_width)[None, None, :]
        - shift.reshape(tiles, 1, tile_width)
    )
    matrix = jnp.zeros((tiles, 3 * tile_width, tile_width), jnp.float32)
    for lag in range(taps.shape[0]):
        matrix = matrix + jnp.where(spread == lag, taps[lag].reshape(tiles, 1, tile_width), 0.0)
    padded = jnp.pad(images, ((0, 0), (tile_width, tile_width))).reshape(
        patch_rows, tiles + 2, tile_width
    )
    window = jnp.concatenate([padded[:, :-2], padded[:, 1:-1], padded[:, 2:]], axis=-1)
    return jnp.einsum("ytk,tki->yti", window, matrix, precision=precise).reshape(
        patch_rows, row_width
    )


def on_device(
    ccd_rows,
    tract_row,
    warp_taps,
    warp_shift,
    basis_rows,
    basis_cols,
    coef_table,
    grid_index,
    template,
    visit_weight,
):
    vis_dev, patch_rows, row_width = ccd_rows.shape
    patches = lax.axis_size("patch")
    run_rows = 2 * patch_rows // patches
    half_width = basis_rows.shape[1] // 2
    target_patch = tract_row // patch_rows
    patch_row = tract_row % patch_rows
    flat_rows = ccd_rows.reshape(-1, row_width)
    slot_in_visit = target_patch * run_rows + patch_row % run_rows
    slot_count = vis_dev * patches * run_rows
    flat_slot = (jnp.arange(vis_dev)[:, None] * (patches * run_rows) + slot_in_visit).reshape(-1)
    found, valid = inverse_places(flat_slot, slot_count)
    send_rows = pick_rows(flat_rows, found, valid).reshape(vis_dev, patches, run_rows, row_width)
    label_pick = jnp.take(patch_row.reshape(-1), jnp.minimum(found, flat_slot.shape[0] - 1))
    send_labels = jnp.where(valid, label_pick, -1).reshape(vis_dev, patches, run_rows)

    def place_one(row_data, labels):
        target = jnp.where(labels < 0, patch_rows, labels).astype(jnp.int32)
        where_from, present = inverse_places(target, patch_rows)
        return pick_rows(row_data, where_from, present)

    row_data = lax.all_to_all(send_rows, "patch", split_axis=1, concat_axis=1, tiled=True)
    labels = lax.all_to_all(send_labels, "patch", split_axis=1, concat_axis=1, tiled=True)
    item_count = row_data.shape[0]
    row_data = row_data.reshape(item_count, -1, row_width)
    labels = labels.reshape(item_count, -1)
    images = jax.vmap(place_one)(row_data, labels)
    warped = lax.map(warp_visit, (images, warp_taps[:, 0], warp_shift[:, 0]))
    margined = padded_2(warped, (("patch", 1),), half_width)
    grid_cells = coef_table.shape[3]
    one_hot = (grid_index[0][None, :] == jnp.arange(grid_cells)[:, None]).astype(jnp.float32)
    coef_cols = jnp.einsum("qbg,gx->qbx", coef_table[:, 0], one_hot, precision=precise)
    vert_table = band_table(
        basis_rows,
        jnp.arange(patch_rows + 2 * half_width)[None, :] - jnp.arange(patch_rows)[:, None],
    )
    out_cols = jnp.arange(tile_width)[None, :]
    mid_table = band_table(basis_cols, jnp.arange(tile_width)[:, None] - out_cols + half_width)
    left_table = band_table(
        basis_cols, jnp.arange(edge_width)[:, None] - edge_width - out_cols + half_width
    )
    right_table = band_table(
        basis_cols, jnp.arange(edge_width)[:, None] + tile_width - out_cols + half_width
    )
    tiles = row_width // tile_width

    def match_visit(pieces):
        padded, coefs = pieces
        vertical = jnp.einsum("bya,ax->byx", vert_table, padded, precision=precise)
        blocks = vertical.reshape(vertical.shape[0], patch_rows, tiles, tile_width)
        tails = jnp.pad(
            blocks[:, :, :-1, tile_width - edge_width :], ((0, 0), (0, 0), (1, 0), (0, 0))
        )
        heads = jnp.pad(blocks[:, :, 1:, :edge_width], ((0, 0), (0, 0), (0, 1), (0, 0)))
        smoothed = jnp.einsum("bytk,bkx->bytx", blocks, mid_table, precision=precise)
        smoothed = smoothed + jnp.einsum("bytk,bkx->bytx", tails, left_table, precision=precise)
        smoothed = smoothed + jnp.einsum("bytk,bkx->bytx", heads, right_table, precision=precise)
        return jnp.sum(coefs.reshape(-1, 1, tiles, tile_width) * smoothed, axis=0).reshape(
            patch_rows, row_width
        )

    matched = lax.map(match_visit, (margined, coef_cols))
    difference = matched - template[None]
    weight_total = jnp.sum(visit_weight)
    regrouped = lax.all_to_all(matched, "visit", split_axis=1, concat_axis=0, tiled=True)
    coadd = jnp.einsum("q,qyx->yx", visit_weight, regrouped, precision=precise) / weight_total
    return (difference, coadd)


def solution(mesh):
    placed = (
        P("visit", "patch", None),
        P("visit", "patch"),
        P("visit", "patch", None, None),
        P("visit", "patch", None),
        P(),
        P(),
        P("visit", "patch", None, None),
        P("patch", None),
        P("patch", None),
        P(),
    )
    return jax.shard_map(
        on_device,
        mesh=mesh,
        in_specs=placed,
        out_specs=(P("visit", "patch", None), P(("patch", "visit"), None)),
        check_vma=False,
    )
```

profile of v0, /device:TPU:8, one launch (start us, length us, event | category | flops | bytes accessed | tf_op | source)
XLA Modules:
  0.0 827.7 jit_solution(219253705411481193)
XLA Ops:
  7.9 8.6 %all-to-all-start = ((s32[8,32,2]{0,2,1:T(2,128)}), s32[8,32,2]{0,2,1:T(2,128)S(1)}, u32[]{:S(2)}, u32[]{:S(2)}) async-start(s32[8,32,2]{0,2,1:T(2,128)} %copy.42), calls=%async_computation | async-start | bytes 65536 | tf_op jit(solution)/shard_map/all_to_all | solution.py:103
  16.6 11.0 %gather_fusion.1 = f32[512,4096]{1,0:T(8,128)} fusion(f32[256,4096]{1,0:T(8,128)} %bitcast.122, s32[1024]{0:T(1024)S(1)} %pad_clamp_fusion), kind=kCustom, calls=%fused_computation.1 | custom fusion | bytes 16779264 | tf_op jit(solution)/shard_map/jit(_take)/gather | solution.py:44
  27.6 10.6 %gather.19 = f32[8,32,2,4096]{3,2,1,0:T(2,128)} reshape(f32[512,4096]{1,0:T(8,128)} %gather_fusion.1) | data formatting | bytes 16777216 | tf_op jit(solution)/shard_map/jit(_take)/gather | solution.py:44
  38.1 10.0 %fusion.415 = f32[8,32,2,4096]{3,2,0,1:T(2,128)} fusion(f32[8,32,2,4096]{3,2,1,0:T(2,128)} %gather.19, pred[8,32,2]{2,0,1:T(8,128)(4,1)S(1)} %copy.45, pred[8,32,2]{2,0,1:T(8,128)(4,1)S(1)} %copy.44), kind=kLoop, calls=%fused_computation.437 | loop fusion | flops 4194304 | bytes 16778240 | tf_op jit(solution)/shard_map/jit(_where)/select_n | solution.py:45
  48.2 8.0 all-to-all-start.1
  57.1 22.1 %scatter_fusion = s32[8,33]{1,0:T(8,128)S(1)} fusion(s32[8,33]{1,0:T(8,128)S(1)} %broadcast_in_dim.1295, s32[512]{0:T(512)S(1)} %reshape.1467, s32[512]{0:T(512)S(1)} %reshape.1469), kind=kCustom, calls=%fused_computation.4 | custom fusion | bytes 10240 | tf_op jit(solution)/shard_map/vmap()/scatter | solution.py:39
  79.3 82.1 %all-to-all-done.1 = f32[8,32,2,4096]{3,2,0,1:T(2,128)} async-done(((f32[8,32,2,4096]{3,2,0,1:T(2,128)}), f32[8,32,2,4096]{3,2,0,1:T(2,128)}, u32[]{:S(2)}, u32[]{:S(2)}) %all-to-all-start.1) | async-done | bytes 8388640 | tf_op jit(solution)/shard_map/all_to_all | solution.py:102
  161.4 7.4 copy.47
  168.8 10.9 %reshape.1436 = f32[8,64,4096]{2,1,0:T(8,128)} reshape(f32[8,32,2,4096]{3,2,1,0:T(2,128)} %copy.47) | data formatting | bytes 16777216 | tf_op jit(solution)/shard_map/reshape | solution.py:105
  179.7 7.6 gather_fusion.2
  194.8 116.6 %while.26 = (s32[]{:T(128)}, f32[8,32,4096]{2,1,0:T(8,128)}, s32[8,4096]{1,0:T(8,128)S(1)}, f32[8,8,4096]{2,1,0:T(8,128)}, f32[8,32,4096]{2,1,0:T(8,128)}, /*ind...) while((s32[]{:T(128)}, f32[8,32,4096]{2,1,0:T(8,128)}, ...), condition=%wide.region_3.4_spmd, body=%wide.region_2.3_spmd.sunk | while | flops 642564480 | bytes 15617805 | solution.py:108
  199.2 9.1 %fusion.541 = f32[32,32,128]{2,0,1:T(8,128)S(1)} fusion(f32[32,32,128]{2,0,1:T(8,128)S(1)} %copy.90, f32[32,32,128]{2,0,1:T(8,128)S(1)} %copy.91, f32[32,32,128]{2,0,1:T(8,128)S(1)} %copy.92, f32[32,128]{1,0:T(8,128)S(1)} %bitcast.135, f32[32,128]{1,0:T(8,128)S(1)} %bitcast.129, f32[32,128]{1,0:T(8,128)S(1)} %bitcast.130, ...), kind=kOutput, calls=%fused_computation.57.clone.1 | convolution fusion | flops 642514944 | bytes 2441216 | tf_op jit(solution)/shard_map/while/body/eval_jaxpr/ytk,tki->yti/dot_general | solution.py:65
  213.7 9.1 %fusion.541 = f32[32,32,128]{2,0,1:T(8,128)S(1)} fusion(f32[32,32,128]{2,0,1:T(8,128)S(1)} %copy.90, f32[32,32,128]{2,0,1:T(8,128)S(1)} %copy.91, f32[32,32,128]{2,0,1:T(8,128)S(1)} %copy.92, f32[32,128]{1,0:T(8,128)S(1)} %bitcast.135, f32[32,128]{1,0:T(8,128)S(1)} %bitcast.129, f32[32,128]{1,0:T(8,128)S(1)} %bitcast.130, ...), kind=kOutput, calls=%fused_computation.57.clone.1 | convolution fusion | flops 642514944 | bytes 2441216 | tf_op jit(solution)/shard_map/while/body/eval_jaxpr/ytk,tki->yti/dot_general | solution.py:65
  228.2 9.1 %fusion.541 = f32[32,32,128]{2,0,1:T(8,128)S(1)} fusion(f32[32,32,128]{2,0,1:T(8,128)S(1)} %copy.90, f32[32,32,128]{2,0,1:T(8,128)S(1)} %copy.91, f32[32,32,128]{2,0,1:T(8,128)S(1)} %copy.92, f32[32,128]{1,0:T(8,128)S(1)} %bitcast.135, f32[32,128]{1,0:T(8,128)S(1)} %bitcast.129, f32[32,128]{1,0:T(8,128)S(1)} %bitcast.130, ...), kind=kOutput, calls=%fused_computation.57.clone.1 | convolution fusion | flops 642514944 | bytes 2441216 | tf_op jit(solution)/shard_map/while/body/eval_jaxpr/ytk,tki->yti/dot_general | solution.py:65
  242.7 9.1 %fusion.541 = f32[32,32,128]{2,0,1:T(8,128)S(1)} fusion(f32[32,32,128]{2,0,1:T(8,128)S(1)} %copy.90, f32[32,32,128]{2,0,1:T(8,128)S(1)} %copy.91, f32[32,32,128]{2,0,1:T(8,128)S(1)} %copy.92, f32[32,128]{1,0:T(8,128)S(1)} %bitcast.135, f32[32,128]{1,0:T(8,128)S(1)} %bitcast.129, f32[32,128]{1,0:T(8,128)S(1)} %bitcast.130, ...), kind=kOutput, calls=%fused_computation.57.clone.1 | convolution fusion | flops 642514944 | bytes 2441216 | tf_op jit(solution)/shard_map/while/body/eval_jaxpr/ytk,tki->yti/dot_general | solution.py:65
  257.2 9.1 %fusion.541 = f32[32,32,128]{2,0,1:T(8,128)S(1)} fusion(f32[32,32,128]{2,0,1:T(8,128)S(1)} %copy.90, f32[32,32,128]{2,0,1:T(8,128)S(1)} %copy.91, f32[32,32,128]{2,0,1:T(8,128)S(1)} %copy.92, f32[32,128]{1,0:T(8,128)S(1)} %bitcast.135, f32[32,128]{1,0:T(8,128)S(1)} %bitcast.129, f32[32,128]{1,0:T(8,128)S(1)} %bitcast.130, ...), kind=kOutput, calls=%fused_computation.57.clone.1 | convolution fusion | flops 642514944 | bytes 2441216 | tf_op jit(solution)/shard_map/while/body/eval_jaxpr/ytk,tki->yti/dot_general | solution.py:65
  271.7 9.1 %fusion.541 = f32[32,32,128]{2,0,1:T(8,128)S(1)} fusion(f32[32,32,128]{2,0,1:T(8,128)S(1)} %copy.90, f32[32,32,128]{2,0,1:T(8,128)S(1)} %copy.91, f32[32,32,128]{2,0,1:T(8,128)S(1)} %copy.92, f32[32,128]{1,0:T(8,128)S(1)} %bitcast.135, f32[32,128]{1,0:T(8,128)S(1)} %bitcast.129, f32[32,128]{1,0:T(8,128)S(1)} %bitcast.130, ...), kind=kOutput, calls=%fused_computation.57.clone.1 | convolution fusion | flops 642514944 | bytes 2441216 | tf_op jit(solution)/shard_map/while/body/eval_jaxpr/ytk,tki->yti/dot_general | solution.py:65
  286.1 9.1 %fusion.541 = f32[32,32,128]{2,0,1:T(8,128)S(1)} fusion(f32[32,32,128]{2,0,1:T(8,128)S(1)} %copy.90, f32[32,32,128]{2,0,1:T(8,128)S(1)} %copy.91, f32[32,32,128]{2,0,1:T(8,128)S(1)} %copy.92, f32[32,128]{1,0:T(8,128)S(1)} %bitcast.135, f32[32,128]{1,0:T(8,128)S(1)} %bitcast.129, f32[32,128]{1,0:T(8,128)S(1)} %bitcast.130, ...), kind=kOutput, calls=%fused_computation.57.clone.1 | convolution fusion | flops 642514944 | bytes 2441216 | tf_op jit(solution)/shard_map/while/body/eval_jaxpr/ytk,tki->yti/dot_general | solution.py:65
  300.6 9.1 %fusion.541 = f32[32,32,128]{2,0,1:T(8,128)S(1)} fusion(f32[32,32,128]{2,0,1:T(8,128)S(1)} %copy.90, f32[32,32,128]{2,0,1:T(8,128)S(1)} %copy.91, f32[32,32,128]{2,0,1:T(8,128)S(1)} %copy.92, f32[32,128]{1,0:T(8,128)S(1)} %bitcast.135, f32[32,128]{1,0:T(8,128)S(1)} %bitcast.129, f32[32,128]{1,0:T(8,128)S(1)} %bitcast.130, ...), kind=kOutput, calls=%fused_computation.57.clone.1 | convolution fusion | flops 642514944 | bytes 2441216 | tf_op jit(solution)/shard_map/while/body/eval_jaxpr/ytk,tki->yti/dot_general | solution.py:65
  318.3 18.4 %collective-permute-start.1 = (f32[8,10,4096]{2,0,1:T(8,128)S(1)}, f32[8,10,4096]{2,0,1:T(8,128)S(1)}, u32[]{:S(2)}, u32[]{:S(2)}) collective-permute-start(f32[8,10,4096]{2,0,1:T(8,128)S(1)} %get-tuple-element.1302), channel_id=1, source_target_pairs={{4,0},{8,4},{12,8},{16,12},{20,16},{24,20},{28,24},{32,28},{36,32}... | collective-permute-start | bytes 3932168 | tf_op jit(solution)/shard_map/ppermute | solution.py:21
  340.5 9.6 %collective-permute-done = f32[8,10,4096]{2,0,1:T(8,128)S(1)} collective-permute-done((f32[8,10,4096]{2,0,1:T(8,128)S(1)}, f32[8,10,4096]{2,0,1:T(8,128)S(1)}, u32[]{:S(2)}, u32[]{:S(2)}) %collective-permute-start) | collective-permute-done | bytes 1310752 | tf_op jit(solution)/shard_map/ppermute | solution.py:19
  358.7 400.0 %while.27 = (s32[]{:T(128)}, f32[8,32,4096]{2,1,0:T(8,128)}, f32[8,9,4096]{2,1,0:T(8,128)}, f32[8,52,4096]{2,1,0:T(8,128)}, f32[9]{0:T(128)S(1)}, /*index=5*/pre...) while((s32[]{:T(128)}, f32[8,32,4096]{2,1,0:T(8,128)}, ...), condition=%wide.region_6.7_spmd.clone.clone, body=%wide.region_4.6_spmd.clone.clone.sunk | while | flops 3013783040 | bytes 81763536 | solution.py:142
  358.8 5.5 fusion.549
  365.2 5.2 fusion.550
  374.5 9.7 %fusion.551 = f32[9,32,32,128]{3,2,1,0:T(8,128)} fusion(f32[9,32,31,16]{2,3,1,0:T(8,128)S(1)} %copy.95, f32[9]{0:T(128)S(1)} %get-tuple-element.2645, f32[9]{0:T(128)S(1)} %get-tuple-element.2643, f32[9]{0:T(128)S(1)} %get-tuple-element.2641, f32[9]{0:T(128)S(1)} %get-tuple-element.2639, f32[9]{0:T(128)S(1)} %get-tuple-element.2637, ...), kind=kOutput, calls=%fused_computation.82.clone.1 | convolution fusion | flops 227248128 | bytes 5333748 | tf_op jit(solution)/shard_map/while/body/eval_jaxpr/bytk,bkx->bytx/dot_general | solution.py:137
  388.3 8.7 %fusion.552 = f32[9,32,32,128]{3,2,1,0:T(8,128)S(1)} fusion(f32[9,32,31,16]{2,3,1,0:T(8,128)S(1)} %copy.96, f32[9]{0:T(128)S(1)} %get-tuple-element.2645, f32[9]{0:T(128)S(1)} %get-tuple-element.2643, f32[9]{0:T(128)S(1)} %get-tuple-element.2641, f32[9]{0:T(128)S(1)} %get-tuple-element.2639, f32[9]{0:T(128)S(1)} %get-tuple-element.2637, ...), kind=kOutput, calls=%fused_computation.84.clone.1 | convolution fusion | flops 227248128 | bytes 5333748 | tf_op jit(solution)/shard_map/while/body/eval_jaxpr/bytk,bkx->bytx/dot_general | solution.py:136
  398.1 9.8 %multiply_reduce_fusion.2 = f32[32,32,128]{2,1,0:T(8,128)S(1)} fusion(f32[9,32,32,128]{3,2,1,0:T(8,128)} %fusion.551, f32[9,32,32,128]{3,2,1,0:T(8,128)S(1)} %fusion.552, f32[9,32,128]{2,1,0:T(8,128)S(1)} %slice.402, f32[9]{0:T(128)S(1)} %get-tuple-element.2645, f32[9]{0:T(128)S(1)} %get-tuple-element.2643, f32[9]{0:T(128)S(1)} %get-tuple-element.2641, ...), kind=kOutput, calls=%fused_computation.81.clone.1 | convolution fusion | flops 1822572544 | bytes 15172340 | tf_op jit(solution)/shard_map/while/body/eval_jaxpr/bytk,bkx->bytx/dot_general | solution.py:135
  408.8 5.4 fusion.549
  415.1 5.2 fusion.550
  424.4 9.7 %fusion.551 = f32[9,32,32,128]{3,2,1,0:T(8,128)} fusion(f32[9,32,31,16]{2,3,1,0:T(8,128)S(1)} %copy.95, f32[9]{0:T(128)S(1)} %get-tuple-element.2645, f32[9]{0:T(128)S(1)} %get-tuple-element.2643, f32[9]{0:T(128)S(1)} %get-tuple-element.2641, f32[9]{0:T(128)S(1)} %get-tuple-element.2639, f32[9]{0:T(128)S(1)} %get-tuple-element.2637, ...), kind=kOutput, calls=%fused_computation.82.clone.1 | convolution fusion | flops 227248128 | bytes 5333748 | tf_op jit(solution)/shard_map/while/body/eval_jaxpr/bytk,bkx->bytx/dot_general | solution.py:137
  438.2 8.7 %fusion.552 = f32[9,32,32,128]{3,2,1,0:T(8,128)S(1)} fusion(f32[9,32,31,16]{2,3,1,0:T(8,128)S(1)} %copy.96, f32[9]{0:T(128)S(1)} %get-tuple-element.2645, f32[9]{0:T(128)S(1)} %get-tuple-element.2643, f32[9]{0:T(128)S(1)} %get-tuple-element.2641, f32[9]{0:T(128)S(1)} %get-tuple-element.2639, f32[9]{0:T(128)S(1)} %get-tuple-element.2637, ...), kind=kOutput, calls=%fused_computation.84.clone.1 | convolution fusion | flops 227248128 | bytes 5333748 | tf_op jit(solution)/shard_map/while/body/eval_jaxpr/bytk,bkx->bytx/dot_general | solution.py:136
  448.0 9.8 %multiply_reduce_fusion.2 = f32[32,32,128]{2,1,0:T(8,128)S(1)} fusion(f32[9,32,32,128]{3,2,1,0:T(8,128)} %fusion.551, f32[9,32,32,128]{3,2,1,0:T(8,128)S(1)} %fusion.552, f32[9,32,128]{2,1,0:T(8,128)S(1)} %slice.402, f32[9]{0:T(128)S(1)} %get-tuple-element.2645, f32[9]{0:T(128)S(1)} %get-tuple-element.2643, f32[9]{0:T(128)S(1)} %get-tuple-element.2641, ...), kind=kOutput, calls=%fused_computation.81.clone.1 | convolution fusion | flops 1822572544 | bytes 15172340 | tf_op jit(solution)/shard_map/while/body/eval_jaxpr/bytk,bkx->bytx/dot_general | solution.py:135
  458.8 5.4 fusion.549
  465.1 5.2 fusion.550
  474.4 9.7 %fusion.551 = f32[9,32,32,128]{3,2,1,0:T(8,128)} fusion(f32[9,32,31,16]{2,3,1,0:T(8,128)S(1)} %copy.95, f32[9]{0:T(128)S(1)} %get-tuple-element.2645, f32[9]{0:T(128)S(1)} %get-tuple-element.2643, f32[9]{0:T(128)S(1)} %get-tuple-element.2641, f32[9]{0:T(128)S(1)} %get-tuple-element.2639, f32[9]{0:T(128)S(1)} %get-tuple-element.2637, ...), kind=kOutput, calls=%fused_computation.82.clone.1 | convolution fusion | flops 227248128 | bytes 5333748 | tf_op jit(solution)/shard_map/while/body/eval_jaxpr/bytk,bkx->bytx/dot_general | solution.py:137
  488.2 8.7 %fusion.552 = f32[9,32,32,128]{3,2,1,0:T(8,128)S(1)} fusion(f32[9,32,31,16]{2,3,1,0:T(8,128)S(1)} %copy.96, f32[9]{0:T(128)S(1)} %get-tuple-element.2645, f32[9]{0:T(128)S(1)} %get-tuple-element.2643, f32[9]{0:T(128)S(1)} %get-tuple-element.2641, f32[9]{0:T(128)S(1)} %get-tuple-element.2639, f32[9]{0:T(128)S(1)} %get-tuple-element.2637, ...), kind=kOutput, calls=%fused_computation.84.clone.1 | convolution fusion | flops 227248128 | bytes 5333748 | tf_op jit(solution)/shard_map/while/body/eval_jaxpr/bytk,bkx->bytx/dot_general | solution.py:136
  497.9 9.8 %multiply_reduce_fusion.2 = f32[32,32,128]{2,1,0:T(8,128)S(1)} fusion(f32[9,32,32,128]{3,2,1,0:T(8,128)} %fusion.551, f32[9,32,32,128]{3,2,1,0:T(8,128)S(1)} %fusion.552, f32[9,32,128]{2,1,0:T(8,128)S(1)} %slice.402, f32[9]{0:T(128)S(1)} %get-tuple-element.2645, f32[9]{0:T(128)S(1)} %get-tuple-element.2643, f32[9]{0:T(128)S(1)} %get-tuple-element.2641, ...), kind=kOutput, calls=%fused_computation.81.clone.1 | convolution fusion | flops 1822572544 | bytes 15172340 | tf_op jit(solution)/shard_map/while/body/eval_jaxpr/bytk,bkx->bytx/dot_general | solution.py:135
  508.7 5.4 fusion.549
  515.0 5.2 fusion.550
  524.3 9.7 %fusion.551 = f32[9,32,32,128]{3,2,1,0:T(8,128)} fusion(f32[9,32,31,16]{2,3,1,0:T(8,128)S(1)} %copy.95, f32[9]{0:T(128)S(1)} %get-tuple-element.2645, f32[9]{0:T(128)S(1)} %get-tuple-element.2643, f32[9]{0:T(128)S(1)} %get-tuple-element.2641, f32[9]{0:T(128)S(1)} %get-tuple-element.2639, f32[9]{0:T(128)S(1)} %get-tuple-element.2637, ...), kind=kOutput, calls=%fused_computation.82.clone.1 | convolution fusion | flops 227248128 | bytes 5333748 | tf_op jit(solution)/shard_map/while/body/eval_jaxpr/bytk,bkx->bytx/dot_general | solution.py:137
  538.1 8.7 %fusion.552 = f32[9,32,32,128]{3,2,1,0:T(8,128)S(1)} fusion(f32[9,32,31,16]{2,3,1,0:T(8,128)S(1)} %copy.96, f32[9]{0:T(128)S(1)} %get-tuple-element.2645, f32[9]{0:T(128)S(1)} %get-tuple-element.2643, f32[9]{0:T(128)S(1)} %get-tuple-element.2641, f32[9]{0:T(128)S(1)} %get-tuple-element.2639, f32[9]{0:T(128)S(1)} %get-tuple-element.2637, ...), kind=kOutput, calls=%fused_computation.84.clone.1 | convolution fusion | flops 227248128 | bytes 5333748 | tf_op jit(solution)/shard_map/while/body/eval_jaxpr/bytk,bkx->bytx/dot_general | solution.py:136
  547.9 9.8 %multiply_reduce_fusion.2 = f32[32,32,128]{2,1,0:T(8,128)S(1)} fusion(f32[9,32,32,128]{3,2,1,0:T(8,128)} %fusion.551, f32[9,32,32,128]{3,2,1,0:T(8,128)S(1)} %fusion.552, f32[9,32,128]{2,1,0:T(8,128)S(1)} %slice.402, f32[9]{0:T(128)S(1)} %get-tuple-element.2645, f32[9]{0:T(128)S(1)} %get-tuple-element.2643, f32[9]{0:T(128)S(1)} %get-tuple-element.2641, ...), kind=kOutput, calls=%fused_computation.81.clone.1 | convolution fusion | flops 1822572544 | bytes 15172340 | tf_op jit(solution)/shard_map/while/body/eval_jaxpr/bytk,bkx->bytx/dot_general | solution.py:135
  558.7 5.4 fusion.549
  565.0 5.2 fusion.550
  574.3 9.7 %fusion.551 = f32[9,32,32,128]{3,2,1,0:T(8,128)} fusion(f32[9,32,31,16]{2,3,1,0:T(8,128)S(1)} %copy.95, f32[9]{0:T(128)S(1)} %get-tuple-element.2645, f32[9]{0:T(128)S(1)} %get-tuple-element.2643, f32[9]{0:T(128)S(1)} %get-tuple-element.2641, f32[9]{0:T(128)S(1)} %get-tuple-element.2639, f32[9]{0:T(128)S(1)} %get-tuple-element.2637, ...), kind=kOutput, calls=%fused_computation.82.clone.1 | convolution fusion | flops 227248128 | bytes 5333748 | tf_op jit(solution)/shard_map/while/body/eval_jaxpr/bytk,bkx->bytx/dot_general | solution.py:137
  588.1 8.7 %fusion.552 = f32[9,32,32,128]{3,2,1,0:T(8,128)S(1)} fusion(f32[9,32,31,16]{2,3,1,0:T(8,128)S(1)} %copy.96, f32[9]{0:T(128)S(1)} %get-tuple-element.2645, f32[9]{0:T(128)S(1)} %get-tuple-element.2643, f32[9]{0:T(128)S(1)} %get-tuple-element.2641, f32[9]{0:T(128)S(1)} %get-tuple-element.2639, f32[9]{0:T(128)S(1)} %get-tuple-element.2637, ...), kind=kOutput, calls=%fused_computation.84.clone.1 | convolution fusion | flops 227248128 | bytes 5333748 | tf_op jit(solution)/shard_map/while/body/eval_jaxpr/bytk,bkx->bytx/dot_general | solution.py:136
  597.8 9.8 %multiply_reduce_fusion.2 = f32[32,32,128]{2,1,0:T(8,128)S(1)} fusion(f32[9,32,32,128]{3,2,1,0:T(8,128)} %fusion.551, f32[9,32,32,128]{3,2,1,0:T(8,128)S(1)} %fusion.552, f32[9,32,128]{2,1,0:T(8,128)S(1)} %slice.402, f32[9]{0:T(128)S(1)} %get-tuple-element.2645, f32[9]{0:T(128)S(1)} %get-tuple-element.2643, f32[9]{0:T(128)S(1)} %get-tuple-element.2641, ...), kind=kOutput, calls=%fused_computation.81.clone.1 | convolution fusion | flops 1822572544 | bytes 15172340 | tf_op jit(solution)/shard_map/while/body/eval_jaxpr/bytk,bkx->bytx/dot_general | solution.py:135
  608.6 5.4 fusion.549
  614.9 5.2 fusion.550
  624.2 9.7 %fusion.551 = f32[9,32,32,128]{3,2,1,0:T(8,128)} fusion(f32[9,32,31,16]{2,3,1,0:T(8,128)S(1)} %copy.95, f32[9]{0:T(128)S(1)} %get-tuple-element.2645, f32[9]{0:T(128)S(1)} %get-tuple-element.2643, f32[9]{0:T(128)S(1)} %get-tuple-element.2641, f32[9]{0:T(128)S(1)} %get-tuple-element.2639, f32[9]{0:T(128)S(1)} %get-tuple-element.2637, ...), kind=kOutput, calls=%fused_computation.82.clone.1 | convolution fusion | flops 227248128 | bytes 5333748 | tf_op jit(solution)/shard_map/while/body/eval_jaxpr/bytk,bkx->bytx/dot_general | solution.py:137
  638.0 8.7 %fusion.552 = f32[9,32,32,128]{3,2,1,0:T(8,128)S(1)} fusion(f32[9,32,31,16]{2,3,1,0:T(8,128)S(1)} %copy.96, f32[9]{0:T(128)S(1)} %get-tuple-element.2645, f32[9]{0:T(128)S(1)} %get-tuple-element.2643, f32[9]{0:T(128)S(1)} %get-tuple-element.2641, f32[9]{0:T(128)S(1)} %get-tuple-element.2639, f32[9]{0:T(128)S(1)} %get-tuple-element.2637, ...), kind=kOutput, calls=%fused_computation.84.clone.1 | convolution fusion | flops 227248128 | bytes 5333748 | tf_op jit(solution)/shard_map/while/body/eval_jaxpr/bytk,bkx->bytx/dot_general | solution.py:136
  647.8 9.8 %multiply_reduce_fusion.2 = f32[32,32,128]{2,1,0:T(8,128)S(1)} fusion(f32[9,32,32,128]{3,2,1,0:T(8,128)} %fusion.551, f32[9,32,32,128]{3,2,1,0:T(8,128)S(1)} %fusion.552, f32[9,32,128]{2,1,0:T(8,128)S(1)} %slice.402, f32[9]{0:T(128)S(1)} %get-tuple-element.2645, f32[9]{0:T(128)S(1)} %get-tuple-element.2643, f32[9]{0:T(128)S(1)} %get-tuple-element.2641, ...), kind=kOutput, calls=%fused_computation.81.clone.1 | convolution fusion | flops 1822572544 | bytes 15172340 | tf_op jit(solution)/shard_map/while/body/eval_jaxpr/bytk,bkx->bytx/dot_general | solution.py:135
  658.6 5.4 fusion.549
  664.9 5.2 fusion.550
  674.2 9.7 %fusion.551 = f32[9,32,32,128]{3,2,1,0:T(8,128)} fusion(f32[9,32,31,16]{2,3,1,0:T(8,128)S(1)} %copy.95, f32[9]{0:T(128)S(1)} %get-tuple-element.2645, f32[9]{0:T(128)S(1)} %get-tuple-element.2643, f32[9]{0:T(128)S(1)} %get-tuple-element.2641, f32[9]{0:T(128)S(1)} %get-tuple-element.2639, f32[9]{0:T(128)S(1)} %get-tuple-element.2637, ...), kind=kOutput, calls=%fused_computation.82.clone.1 | convolution fusion | flops 227248128 | bytes 5333748 | tf_op jit(solution)/shard_map/while/body/eval_jaxpr/bytk,bkx->bytx/dot_general | solution.py:137
  688.0 8.7 %fusion.552 = f32[9,32,32,128]{3,2,1,0:T(8,128)S(1)} fusion(f32[9,32,31,16]{2,3,1,0:T(8,128)S(1)} %copy.96, f32[9]{0:T(128)S(1)} %get-tuple-element.2645, f32[9]{0:T(128)S(1)} %get-tuple-element.2643, f32[9]{0:T(128)S(1)} %get-tuple-element.2641, f32[9]{0:T(128)S(1)} %get-tuple-element.2639, f32[9]{0:T(128)S(1)} %get-tuple-element.2637, ...), kind=kOutput, calls=%fused_computation.84.clone.1 | convolution fusion | flops 227248128 | bytes 5333748 | tf_op jit(solution)/shard_map/while/body/eval_jaxpr/bytk,bkx->bytx/dot_general | solution.py:136
  697.7 9.8 %multiply_reduce_fusion.2 = f32[32,32,128]{2,1,0:T(8,128)S(1)} fusion(f32[9,32,32,128]{3,2,1,0:T(8,128)} %fusion.551, f32[9,32,32,128]{3,2,1,0:T(8,128)S(1)} %fusion.552, f32[9,32,128]{2,1,0:T(8,128)S(1)} %slice.402, f32[9]{0:T(128)S(1)} %get-tuple-element.2645, f32[9]{0:T(128)S(1)} %get-tuple-element.2643, f32[9]{0:T(128)S(1)} %get-tuple-element.2641, ...), kind=kOutput, calls=%fused_computation.81.clone.1 | convolution fusion | flops 1822572544 | bytes 15172340 | tf_op jit(solution)/shard_map/while/body/eval_jaxpr/bytk,bkx->bytx/dot_general | solution.py:135
  708.5 5.4 fusion.549
  714.8 5.2 fusion.550
  724.1 9.7 %fusion.551 = f32[9,32,32,128]{3,2,1,0:T(8,128)} fusion(f32[9,32,31,16]{2,3,1,0:T(8,128)S(1)} %copy.95, f32[9]{0:T(128)S(1)} %get-tuple-element.2645, f32[9]{0:T(128)S(1)} %get-tuple-element.2643, f32[9]{0:T(128)S(1)} %get-tuple-element.2641, f32[9]{0:T(128)S(1)} %get-tuple-element.2639, f32[9]{0:T(128)S(1)} %get-tuple-element.2637, ...), kind=kOutput, calls=%fused_computation.82.clone.1 | convolution fusion | flops 227248128 | bytes 5333748 | tf_op jit(solution)/shard_map/while/body/eval_jaxpr/bytk,bkx->bytx/dot_general | solution.py:137
  737.9 8.7 %fusion.552 = f32[9,32,32,128]{3,2,1,0:T(8,128)S(1)} fusion(f32[9,32,31,16]{2,3,1,0:T(8,128)S(1)} %copy.96, f32[9]{0:T(128)S(1)} %get-tuple-element.2645, f32[9]{0:T(128)S(1)} %get-tuple-element.2643, f32[9]{0:T(128)S(1)} %get-tuple-element.2641, f32[9]{0:T(128)S(1)} %get-tuple-element.2639, f32[9]{0:T(128)S(1)} %get-tuple-element.2637, ...), kind=kOutput, calls=%fused_computation.84.clone.1 | convolution fusion | flops 227248128 | bytes 5333748 | tf_op jit(solution)/shard_map/while/body/eval_jaxpr/bytk,bkx->bytx/dot_general | solution.py:136
  747.7 9.8 %multiply_reduce_fusion.2 = f32[32,32,128]{2,1,0:T(8,128)S(1)} fusion(f32[9,32,32,128]{3,2,1,0:T(8,128)} %fusion.551, f32[9,32,32,128]{3,2,1,0:T(8,128)S(1)} %fusion.552, f32[9,32,128]{2,1,0:T(8,128)S(1)} %slice.402, f32[9]{0:T(128)S(1)} %get-tuple-element.2645, f32[9]{0:T(128)S(1)} %get-tuple-element.2643, f32[9]{0:T(128)S(1)} %get-tuple-element.2641, ...), kind=kOutput, calls=%fused_computation.81.clone.1 | convolution fusion | flops 1822572544 | bytes 15172340 | tf_op jit(solution)/shard_map/while/body/eval_jaxpr/bytk,bkx->bytx/dot_general | solution.py:135
  758.6 6.6 copy.52
  775.5 41.3 %all-to-all-done.2 = f32[8,32,4096]{2,0,1:T(8,128)} async-done(((f32[8,32,4096]{2,0,1:T(8,128)}), f32[8,32,4096]{2,0,1:T(8,128)}, u32[]{:S(2)}, u32[]{:S(2)}) %all-to-all-start.2) | async-done | bytes 4194336 | tf_op jit(solution)/shard_map/all_to_all | solution.py:145
  (322 shorter events, 185.8 us)
Async XLA Ops:
  7.9 40.2 %all-to-all-start = ((s32[8,32,2]{0,2,1:T(2,128)}), s32[8,32,2]{0,2,1:T(2,128)S(1)}, u32[]{:S(2)}, u32[]{:S(2)}) async-start(s32[8,32,2]{0,2,1:T(2,128)} %copy.42), calls=%async_computation | async-start | bytes 65536 | tf_op jit(solution)/shard_map/all_to_all | solution.py:103
  48.1 8.1 copy-start.5
  48.1 8.4 %copy-start.2 = (f32[9,21]{1,0:T(8,128)S(1)}, f32[9,21]{1,0:T(8,128)}, u32[]{:S(2)}) copy-start(f32[9,21]{1,0:T(8,128)} %param.18) | copy-start | bytes 2272
  48.1 8.4 %copy-start.3 = (f32[9,21]{1,0:T(8,128)S(1)}, f32[9,21]{1,0:T(8,128)}, u32[]{:S(2)}) copy-start(f32[9,21]{1,0:T(8,128)} %param.19) | copy-start | bytes 2272
  48.2 113.3 %all-to-all-start.1 = ((f32[8,32,2,4096]{3,2,0,1:T(2,128)}), f32[8,32,2,4096]{3,2,0,1:T(2,128)}, u32[]{:S(2)}, u32[]{:S(2)}) async-start(f32[8,32,2,4096]{3,2,0,1:T(2,128)} %fusion.415), calls=%async_computation.1 | async-start | bytes 16777216 | tf_op jit(solution)/shard_map/all_to_all | solution.py:102
  316.1 22.0 %copy-start.6 = (f32[8,1,9,32]{3,1,2,0:T(1,128)S(1)}, f32[8,1,9,32]{3,1,2,0:T(1,128)}, u32[]{:S(2)}) copy-start(f32[8,1,9,32]{3,1,2,0:T(1,128)} %param.20) | copy-start | bytes 27652
  316.1 22.0 %copy-start.7 = (s32[1,4096]{1,0:T(1,128)S(1)}, s32[1,4096]{1,0:T(1,128)}, u32[]{:S(2)}) copy-start(s32[1,4096]{1,0:T(1,128)} %param.21) | copy-start | bytes 49156
  316.4 33.7 %collective-permute-start = (f32[8,10,4096]{2,0,1:T(8,128)S(1)}, f32[8,10,4096]{2,0,1:T(8,128)S(1)}, u32[]{:S(2)}, u32[]{:S(2)}) collective-permute-start(f32[8,10,4096]{2,0,1:T(8,128)S(1)} %get-tuple-element.1301), channel_id=1, source_target_pairs={{0,4},{4,8},{8,12},{12,16},{16,20},{20,24},{24,28},{28,32},{32,36}... | collective-permute-start | bytes 3932168 | tf_op jit(solution)/shard_map/ppermute | solution.py:19
  318.3 33.5 %collective-permute-start.1 = (f32[8,10,4096]{2,0,1:T(8,128)S(1)}, f32[8,10,4096]{2,0,1:T(8,128)S(1)}, u32[]{:S(2)}, u32[]{:S(2)}) collective-permute-start(f32[8,10,4096]{2,0,1:T(8,128)S(1)} %get-tuple-element.1302), channel_id=1, source_target_pairs={{4,0},{8,4},{12,8},{16,12},{20,16},{24,20},{28,24},{32,28},{36,32}... | collective-permute-start | bytes 3932168 | tf_op jit(solution)/shard_map/ppermute | solution.py:21
  336.9 15.8 %copy-start.1 = (f32[8,32,4096]{2,1,0:T(8,128)S(1)}, f32[8,32,4096]{2,1,0:T(8,128)}, u32[]{:S(2)}) copy-start(f32[8,32,4096]{2,1,0:T(8,128)} %get-tuple-element.169) | copy-start | bytes 12582916
  365.2 5.3 copy-start
  388.3 9.7 %slice-start = ((s8[4718592]{0:T(1024)(128)(4,1)}), s8[4194304]{0:T(1024)(128)(4,1)S(1)}, s32[]{:S(2)}) async-start(s8[4718592]{0:T(1024)(128)(4,1)} %bitcast.119), calls=%async_computation.3 | async-start | bytes 8388608 | tf_op jit(solution)/shard_map/while
  388.3 9.7 %slice-start.1 = ((s8[4718592]{0:T(1024)(128)(4,1)}), s8[524288]{0:T(1024)(128)(4,1)S(1)}, s32[]{:S(2)}) async-start(s8[4718592]{0:T(1024)(128)(4,1)} %bitcast.119), calls=%async_computation.4 | async-start | bytes 1048576 | tf_op jit(solution)/shard_map/while
  415.1 5.3 copy-start
  438.2 9.7 %slice-start = ((s8[4718592]{0:T(1024)(128)(4,1)}), s8[4194304]{0:T(1024)(128)(4,1)S(1)}, s32[]{:S(2)}) async-start(s8[4718592]{0:T(1024)(128)(4,1)} %bitcast.119), calls=%async_computation.3 | async-start | bytes 8388608 | tf_op jit(solution)/shard_map/while
  438.2 9.7 %slice-start.1 = ((s8[4718592]{0:T(1024)(128)(4,1)}), s8[524288]{0:T(1024)(128)(4,1)S(1)}, s32[]{:S(2)}) async-start(s8[4718592]{0:T(1024)(128)(4,1)} %bitcast.119), calls=%async_computation.4 | async-start | bytes 1048576 | tf_op jit(solution)/shard_map/while
  465.1 5.3 copy-start
  488.2 9.7 %slice-start = ((s8[4718592]{0:T(1024)(128)(4,1)}), s8[4194304]{0:T(1024)(128)(4,1)S(1)}, s32[]{:S(2)}) async-start(s8[4718592]{0:T(1024)(128)(4,1)} %bitcast.119), calls=%async_computation.3 | async-start | bytes 8388608 | tf_op jit(solution)/shard_map/while
  488.2 9.7 %slice-start.1 = ((s8[4718592]{0:T(1024)(128)(4,1)}), s8[524288]{0:T(1024)(128)(4,1)S(1)}, s32[]{:S(2)}) async-start(s8[4718592]{0:T(1024)(128)(4,1)} %bitcast.119), calls=%async_computation.4 | async-start | bytes 1048576 | tf_op jit(solution)/shard_map/while
  515.0 5.3 copy-start
  538.1 9.7 %slice-start = ((s8[4718592]{0:T(1024)(128)(4,1)}), s8[4194304]{0:T(1024)(128)(4,1)S(1)}, s32[]{:S(2)}) async-start(s8[4718592]{0:T(1024)(128)(4,1)} %bitcast.119), calls=%async_computation.3 | async-start | bytes 8388608 | tf_op jit(solution)/shard_map/while
  538.1 9.7 %slice-start.1 = ((s8[4718592]{0:T(1024)(128)(4,1)}), s8[524288]{0:T(1024)(128)(4,1)S(1)}, s32[]{:S(2)}) async-start(s8[4718592]{0:T(1024)(128)(4,1)} %bitcast.119), calls=%async_computation.4 | async-start | bytes 1048576 | tf_op jit(solution)/shard_map/while
  565.0 5.3 copy-start
  588.1 9.7 %slice-start = ((s8[4718592]{0:T(1024)(128)(4,1)}), s8[4194304]{0:T(1024)(128)(4,1)S(1)}, s32[]{:S(2)}) async-start(s8[4718592]{0:T(1024)(128)(4,1)} %bitcast.119), calls=%async_computation.3 | async-start | bytes 8388608 | tf_op jit(solution)/shard_map/while
  588.1 9.7 %slice-start.1 = ((s8[4718592]{0:T(1024)(128)(4,1)}), s8[524288]{0:T(1024)(128)(4,1)S(1)}, s32[]{:S(2)}) async-start(s8[4718592]{0:T(1024)(128)(4,1)} %bitcast.119), calls=%async_computation.4 | async-start | bytes 1048576 | tf_op jit(solution)/shard_map/while
  614.9 5.3 copy-start
  638.0 9.7 %slice-start = ((s8[4718592]{0:T(1024)(128)(4,1)}), s8[4194304]{0:T(1024)(128)(4,1)S(1)}, s32[]{:S(2)}) async-start(s8[4718592]{0:T(1024)(128)(4,1)} %bitcast.119), calls=%async_computation.3 | async-start | bytes 8388608 | tf_op jit(solution)/shard_map/while
  638.0 9.7 %slice-start.1 = ((s8[4718592]{0:T(1024)(128)(4,1)}), s8[524288]{0:T(1024)(128)(4,1)S(1)}, s32[]{:S(2)}) async-start(s8[4718592]{0:T(1024)(128)(4,1)} %bitcast.119), calls=%async_computation.4 | async-start | bytes 1048576 | tf_op jit(solution)/shard_map/while
  664.8 5.3 copy-start
  688.0 9.7 %slice-start = ((s8[4718592]{0:T(1024)(128)(4,1)}), s8[4194304]{0:T(1024)(128)(4,1)S(1)}, s32[]{:S(2)}) async-start(s8[4718592]{0:T(1024)(128)(4,1)} %bitcast.119), calls=%async_computation.3 | async-start | bytes 8388608 | tf_op jit(solution)/shard_map/while
  688.0 9.7 %slice-start.1 = ((s8[4718592]{0:T(1024)(128)(4,1)}), s8[524288]{0:T(1024)(128)(4,1)S(1)}, s32[]{:S(2)}) async-start(s8[4718592]{0:T(1024)(128)(4,1)} %bitcast.119), calls=%async_computation.4 | async-start | bytes 1048576 | tf_op jit(solution)/shard_map/while
  714.8 5.3 copy-start
  737.9 9.7 %slice-start = ((s8[4718592]{0:T(1024)(128)(4,1)}), s8[4194304]{0:T(1024)(128)(4,1)S(1)}, s32[]{:S(2)}) async-start(s8[4718592]{0:T(1024)(128)(4,1)} %bitcast.119), calls=%async_computation.3 | async-start | bytes 8388608 | tf_op jit(solution)/shard_map/while
  737.9 9.7 %slice-start.1 = ((s8[4718592]{0:T(1024)(128)(4,1)}), s8[524288]{0:T(1024)(128)(4,1)S(1)}, s32[]{:S(2)}) async-start(s8[4718592]{0:T(1024)(128)(4,1)} %bitcast.119), calls=%async_computation.4 | async-start | bytes 1048576 | tf_op jit(solution)/shard_map/while
  765.2 5.0 copy-start.8
  765.2 5.6 copy-start.4
  765.2 51.6 %all-to-all-start.2 = ((f32[8,32,4096]{2,0,1:T(8,128)}), f32[8,32,4096]{2,0,1:T(8,128)}, u32[]{:S(2)}, u32[]{:S(2)}) async-start(f32[8,32,4096]{2,0,1:T(8,128)} %copy.52), calls=%async_computation.2 | async-start | bytes 8388608 | tf_op jit(solution)/shard_map/all_to_all | solution.py:145
where the time goes:
time: 843 us; the launch traced here: 828 us
  matrix products  349 us (41%)
  local copies, waits for them, and re-layouts  272 us (32%)
  waiting for transfers between devices  134 us (16%)
  starting transfers between devices  41.8 us (5%)
  other arithmetic  27.4 us (3%)
    all_to_all x1, waiting for transfers between devices, on_device(): lax.all_to_all(send_rows, 'patch', split_axis=1, concat_axis=1, tiled=True)  82.1 us
    while x104, local copies, waits for them, and re-layouts  80 us
    dot_general x8, matrix products, match_visit(): jnp.einsum('bytk,bkx->bytx', blocks, mid_table, precision=precise)  78.5 us
    dot_general x8, matrix products, match_visit(): jnp.einsum('bytk,bkx->bytx', heads, right_table, precision=precise)  77.9 us
    dot_general x8, matrix products, warp_visit(): jnp.einsum('ytk,tki->yti', window, matrix, precision=precise)  72.8 us
    dot_general x8, matrix products, match_visit(): jnp.einsum('bytk,bkx->bytx', tails, left_table, precision=precise)  69.3 us
    dot_general x8, matrix products, match_visit(): vertical = jnp.einsum('bya,ax->byx', vert_table, padded, precision=precise)  43.2 us
    slice x8, local copies, waits for them, and re-layouts, match_visit(): blocks[:, :, :-1, tile_width - edge_width:]  41.9 us
  transfers between devices with their start and end apart: 5, of which 4 were waited for; matrix products, arithmetic and copies ran while one was open for 8% of the time, Pallas kernels for 0%

commit v1 on v0

v1 whole, which is shorter than its diff:
```python
import functools

import jax
import jax.numpy as jnp
from jax import lax
from jax.experimental import pallas as pl
from jax.experimental.pallas import tpu as pltpu
from jax.sharding import PartitionSpec as P

lane = 128
half_lane = 64
group = 1024
chunks = (2, 2, 2, 2)
bf16 = jnp.bfloat16


def pack_kernel(first, places_ref, rows_ref, sent_ref, sem):
    count = sent_ref.shape[1]
    patch_rows = places_ref.shape[1]

    def step(item, carry):
        local = item // patch_rows
        row = item % patch_rows
        place = places_ref[first + local, row]
        pltpu.make_async_copy(
            rows_ref.at[first + local, row // 8, :, row % 8, :],
            sent_ref.at[place // patch_rows, local, :, place % 2, :],
            sem,
        ).start()
        return carry

    lax.fori_loop(0, count * patch_rows, step, 0)
    everything = rows_ref.at[pl.ds(first, count)]
    pltpu.make_async_copy(everything, everything, sem).wait()


def pack_rows(first, count, tract_row, tiled_rows, patches):
    return pl.pallas_call(
        functools.partial(pack_kernel, first),
        out_shape=jax.ShapeDtypeStruct(
            (patches, count, tiled_rows.shape[2], 2, lane), jnp.float32
        ),
        in_specs=[
            pl.BlockSpec(memory_space=pltpu.SMEM),
            pl.BlockSpec(memory_space=pl.ANY),
        ],
        out_specs=pl.BlockSpec(memory_space=pl.ANY),
        scratch_shapes=[pltpu.SemaphoreType.DMA],
        cost_estimate=pl.CostEstimate(flops=0, bytes_accessed=8 * count << 20, transcendentals=0),
        name="pack_rows",
    )(tract_row, tiled_rows)


def pick_lanes(cells, index):
    return jnp.take_along_axis(cells, index, axis=1, mode="promise_in_bounds")


def warp_kernel(
    first, turn_ref, got_ref, taps_ref, shift_ref, warped_ref, head_ref, tail_ref, image, sems
):
    patches, count, tiles = got_ref.shape[:3]
    pairs = warped_ref.shape[1] // 2
    for local in range(count):

        def fetch(pair, carry):
            source = (turn_ref[0] + first + local - pair + 2 * patches) % patches
            pltpu.make_async_copy(
                got_ref.at[source, local],
                image.at[local, pair // 4, pl.ds(1, tiles), pl.ds(2 * (pair % 4), 2), :],
                sems.at[local],
            ).start()
            return carry

        lax.fori_loop(0, pairs, fetch, 0)
    blank = jnp.zeros((8, lane), jnp.float32)
    groups = image.shape[1]
    for local in range(count):
        for g in range(groups):
            image[local, g, 0] = blank
            image[local, g, tiles + 1] = blank
    columns = lax.broadcasted_iota(jnp.int32, (8, lane), 1) + half_lane
    for local in range(count):
        whole = image.at[local, :, pl.ds(1, tiles)]
        pltpu.make_async_copy(whole, whole, sems.at[local]).wait()

        def tile_step(u, carry):
            window = pl.ds(pl.multiple_of(u * lane, lane), lane)
            base = columns + jnp.broadcast_to(shift_ref[local, :, window], (8, lane))
            totals = [blank] * groups
            lows = [image[local, g, u] for g in range(groups)]
            highs = [image[local, g, u + 1] for g in range(groups)]
            for k in range(taps_ref.shape[1]):
                spot = base + k
                index = spot & (lane - 1)
                upper = spot >= lane
                tap = jnp.broadcast_to(taps_ref[local, k : k + 1, window], (8, lane))
                for g in range(groups):
                    picked = jnp.where(
                        upper, pick_lanes(highs[g], index), pick_lanes(lows[g], index)
                    )
                    totals[g] = totals[g] + tap * picked
            for g in range(groups):
                warped_ref[local, 8 * g : 8 * g + 8, window] = totals[g]
            return carry

        lax.fori_loop(0, tiles + 1, tile_step, 0)
        edge = head_ref.shape[1]
        last = warped_ref.shape[1] - 2 * edge
        for i in range(edge):
            head_ref[local, i] = warped_ref[local, 2 * i : 2 * i + 2, :]
            tail_ref[local, i] = warped_ref[local, last + 2 * i : last + 2 * i + 2, :]


def warp_rows(first, turn, got, taps, shift, patch_rows, edge):
    patches, count, tiles = got.shape[:3]
    width = (tiles + 1) * lane
    shapes = (
        jax.ShapeDtypeStruct((count, patch_rows, width), jnp.float32),
        jax.ShapeDtypeStruct((count, edge, 2, width), jnp.float32),
        jax.ShapeDtypeStruct((count, edge, 2, width), jnp.float32),
    )
    part = first // count
    return pl.pallas_call(
        functools.partial(warp_kernel, first),
        out_shape=shapes,
        grid=(1,),
        in_specs=[
            pl.BlockSpec(memory_space=pltpu.SMEM),
            pl.BlockSpec(memory_space=pl.ANY),
            pl.BlockSpec((count,) + taps.shape[1:], lambda i: (part, 0, 0)),
            pl.BlockSpec((count,) + shift.shape[1:], lambda i: (part, 0, 0)),
        ],
        out_specs=[
            pl.BlockSpec(shapes[0].shape, lambda i: (0, 0, 0)),
            pl.BlockSpec(shapes[1].shape, lambda i: (0, 0, 0, 0)),
            pl.BlockSpec(shapes[2].shape, lambda i: (0, 0, 0, 0)),
        ],
        scratch_shapes=[
            pltpu.VMEM((count, patch_rows // 8, tiles + 2, 8, lane), jnp.float32),
            pltpu.SemaphoreType.DMA((count,)),
        ],
        compiler_params=pltpu.CompilerParams(vmem_limit_bytes=32 << 20),
        cost_estimate=pl.CostEstimate(flops=0, bytes_accessed=5 * count << 20, transcendentals=0),
        name="warp_rows",
    )(turn, got, taps, shift)


def two_parts(values):
    high = values.astype(bf16)
    low = (values - high.astype(jnp.float32)).astype(bf16)
    return high, low


def match_kernel(
    first,
    fresh,
    weight_ref,
    warped_ref,
    above_ref,
    below_ref,
    down_ref,
    across_ref,
    coef_ref,
    template_ref,
    before_ref,
    _,
    difference_ref,
    total_ref,
    stack,
    high_ref,
    low_ref,
):
    patch_rows = warped_ref.shape[1]
    edge = above_ref.shape[1]
    bases = coef_ref.shape[1]
    tiles = group // lane

    @pl.when(pl.program_id(1) == 0)
    def _():
        stack[:patch_rows, :] = warped_ref[0]
        for i in range(edge):
            at = patch_rows + 2 * i
            stack[at : at + 2, :] = above_ref[0, i]
            at = at + 2 * edge
            stack[at : at + 2, :] = below_ref[0, i]
        used = patch_rows + 4 * edge
        stack[used:, :] = jnp.zeros((stack.shape[0] - used, stack.shape[1]), jnp.float32)

    start = pl.multiple_of(pl.program_id(1) * group, group)
    high, low = two_parts(stack[:, pl.ds(start, group + lane)])
    vertical = jnp.dot(
        down_ref[...],
        jnp.concatenate([high, low, high], axis=0),
        preferred_element_type=jnp.float32,
    )
    high_ref[...], low_ref[...] = two_parts(vertical)

    def windows(ref, b):
        rows = slice(b * patch_rows, (b + 1) * patch_rows)
        return jnp.concatenate(
            [ref[rows, lane * i : lane * (i + 2)] for i in range(tiles)], axis=0
        )

    matched = jnp.zeros((tiles * patch_rows, lane), jnp.float32)
    for b in range(bases):
        both = jnp.dot(windows(high_ref, b), across_ref[b], preferred_element_type=jnp.float32)
        rest = jnp.dot(
            windows(low_ref, b), across_ref[b, :, :lane], preferred_element_type=jnp.float32
        )
        smoothed = both[:, :lane] + both[:, lane:] + rest
        scale = jnp.concatenate(
            [
                jnp.broadcast_to(
                    coef_ref[0, b : b + 1, lane * i : lane * (i + 1)], (patch_rows, lane)
                )
                for i in range(tiles)
            ],
            axis=0,
        )
        matched = matched + scale * smoothed
    weight = weight_ref[first + pl.program_id(0)]
    for i in range(tiles):
        piece = matched[i * patch_rows : (i + 1) * patch_rows]
        here = slice(lane * i, lane * (i + 1))
        columns = pl.ds(pl.multiple_of(start + lane * i, lane), lane)
        difference_ref[0, :, here] = piece - template_ref[:, columns]
        if fresh:

            @pl.when(pl.program_id(0) == 0)
            def _():
                total_ref[:, columns] = weight * piece

        else:

            @pl.when(pl.program_id(0) == 0)
            def _():
                total_ref[:, columns] = before_ref[:, columns] + weight * piece

        @pl.when(pl.program_id(0) > 0)
        def _():
            total_ref[:, columns] = total_ref[:, columns] + weight * piece


def match_rows(
    first, weights, warped, above, below, down, across, coefs, template, before, difference
):
    count, patch_rows, width = warped.shape
    edge = above.shape[1]
    visits, bases, row_width = coefs.shape
    fresh = before is None
    if fresh:
        before = template
    extra, aliases = [], {}
    if difference is not None:
        extra, aliases = [difference], {9: 0}
    kernel = functools.partial(match_kernel, first, fresh)
    if difference is None:

        def body(*refs):
            kernel(*refs[:9], None, *refs[9:])

    else:
        body = kernel
    rows_spec = pl.BlockSpec(template.shape, lambda q, c: (0, 0))
    return pl.pallas_call(
        body,
        out_shape=(
            jax.ShapeDtypeStruct((visits, patch_rows, row_width), jnp.float32),
            jax.ShapeDtypeStruct(template.shape, jnp.float32),
        ),
        grid=(count, row_width // group),
        in_specs=[
            pl.BlockSpec(memory_space=pltpu.SMEM),
            pl.BlockSpec((1, patch_rows, width), lambda q, c: (q, 0, 0)),
            pl.BlockSpec((1, edge, 2, width), lambda q, c: (q, 0, 0, 0)),
            pl.BlockSpec((1, edge, 2, width), lambda q, c: (q, 0, 0, 0)),
            pl.BlockSpec(down.shape, lambda q, c: (0, 0)),
            pl.BlockSpec(across.shape, lambda q, c: (0, 0, 0)),
            pl.BlockSpec((1, bases, group), lambda q, c: (q + first, 0, c)),
            rows_spec,
            rows_spec,
        ]
        + [pl.BlockSpec(memory_space=pl.ANY)] * len(extra),
        out_specs=[
            pl.BlockSpec((1, patch_rows, group), lambda q, c: (q + first, 0, c)),
            rows_spec,
        ],
        scratch_shapes=[
            pltpu.VMEM((down.shape[1] // 3, width), jnp.float32),
            pltpu.VMEM((down.shape[0], group + lane), bf16),
            pltpu.VMEM((down.shape[0], group + lane), bf16),
        ],
        input_output_aliases=aliases,
        compiler_params=pltpu.CompilerParams(vmem_limit_bytes=48 << 20),
        cost_estimate=pl.CostEstimate(flops=0, bytes_accessed=14 * count << 20, transcendentals=0),
        name="match_rows",
    )(weights, warped, above, below, down, across, coefs, template, before, *extra)


def split_table(values):
    high = lax.reduce_precision(values, 8, 7)
    return high.astype(bf16), (values - high).astype(bf16)


def taken(values, index):
    table = jnp.zeros((values.shape[0],) + index.shape, jnp.float32)
    for lag in range(values.shape[1]):
        table = jnp.where((index == lag)[None], values[:, lag].reshape(-1, 1, 1), table)
    return table


def on_device(
    ccd_rows,
    tract_row,
    warp_taps,
    warp_shift,
    basis_rows,
    basis_cols,
    coef_table,
    grid_index,
    template,
    visit_weight,
):
    visits, patch_rows, row_width = ccd_rows.shape
    patches = lax.axis_size("patch")
    here = lax.axis_index("patch")
    half = basis_rows.shape[1] // 2
    edge = half // 2
    tiles = row_width // lane

    tiled_rows = ccd_rows.reshape(visits, patch_rows // 8, 8, tiles, lane).transpose(0, 1, 3, 2, 4)
    place = tract_row[0, 0]
    offset = place // patch_rows - here - (place % patch_rows) // 2
    turn = ((here - offset) % patches).astype(jnp.int32).reshape(1)
    taps = jnp.pad(warp_taps[:, 0], ((0, 0), (0, 0), (half_lane, half_lane)))
    shift = jnp.pad(warp_shift, ((0, 0), (0, 0), (half_lane, half_lane)))

    one_hot = (grid_index[0][None, :] == jnp.arange(coef_table.shape[3])[:, None]).astype(
        jnp.float32
    )
    coefs = jnp.einsum(
        "qbg,gx->qbx", coef_table[:, 0], one_hot, precision=lax.Precision.HIGHEST
    )

    rows = jnp.arange(patch_rows)
    ends = jnp.arange(half)
    blank = jnp.full((64 - patch_rows - 2 * half,), 4 * patch_rows)
    inner = jnp.concatenate([rows, ends - half, ends + patch_rows, blank])
    down = taken(basis_rows, inner[None, :] - rows[:, None] + half).reshape(-1, inner.shape[0])
    down_high, down_low = split_table(down)
    down = jnp.concatenate([down_high, down_high, down_low], axis=1)
    across = taken(
        basis_cols, jnp.arange(2 * lane)[:, None] - half_lane - jnp.arange(lane)[None, :] + half
    )
    across = jnp.concatenate(split_table(across), axis=2)
    weights = lax.dynamic_slice_in_dim(
        visit_weight, lax.axis_index("visit") * visits, visits
    )

    starts = [sum(chunks[:i]) for i in range(len(chunks))]
    sent = [
        pack_rows(first, count, tract_row, tiled_rows, patches)
        for first, count in zip(starts, chunks)
    ]
    got = [lax.all_to_all(block, "patch", split_axis=0, concat_axis=0, tiled=True) for block in sent]
    total, difference = None, None
    down_pairs = [(i, i + 1) for i in range(patches - 1)]
    up_pairs = [(i + 1, i) for i in range(patches - 1)]
    for first, block in zip(starts, got):
        warped, head, tail = warp_rows(first, turn, block, taps, shift, patch_rows, edge)
        above = lax.ppermute(tail, "patch", down_pairs)
        below = lax.ppermute(head, "patch", up_pairs)
        difference, total = match_rows(
            first, weights, warped, above, below, down, across, coefs, template, total, difference
        )
    parts = lax.axis_size("visit")
    slices = lax.all_to_all(
        total.reshape(parts, patch_rows // parts, row_width),
        "visit",
        split_axis=0,
        concat_axis=0,
        tiled=True,
    )
    return difference, jnp.sum(slices, axis=0) / jnp.sum(visit_weight)


def solution(mesh):
    placed = (
        P("visit", "patch", None),
        P("visit", "patch"),
        P("visit", "patch", None, None),
        P("visit", "patch", None),
        P(),
        P(),
        P("visit", "patch", None, None),
        P("patch", None),
        P("patch", None),
        P(),
    )
    return jax.shard_map(
        on_device,
        mesh=mesh,
        in_specs=placed,
        out_specs=(P("visit", "patch", None), P(("patch", "visit"), None)),
        check_vma=False,
    )
```

time: 843 us -> 337 us (0.40); the launches traced: 828 us -> 336 us
  matrix products: 349 us -> 3.18 us
  local copies, waits for them, and re-layouts: 272 us -> 11.1 us
  Pallas kernels: 0 us -> 235 us
  waiting for transfers between devices: 134 us -> 7.43 us
  starting transfers between devices: 41.8 us -> 66.1 us
  other arithmetic: 27.4 us -> 8.63 us
    dot_general x42 -> x1, matrix products: 349 us -> 3.18 us  [on_device(): jnp.einsum('qbg,gx->qbx', coef_table[:, 0], one_hot, precision=lax.Precis...]
    pallas_call x0 -> x12, Pallas kernels: none -> 235 us  [the longest x4 135 us: pack_rows(): pl.pallas_call(functools.partial(pack_kernel, first), out_shape=jax.Shape...]
    all_to_all x3 -> x5, waiting for transfers between devices: 123 us -> 7.41 us  [the longest x1 7.4 us: on_device(): lax.all_to_all(total.reshape(parts, patch_rows // parts, row_width), 'vis...]
    while x106 -> x0, local copies, waits for them, and re-layouts: 91.2 us -> none
    slice x28 -> x5, local copies, waits for them, and re-layouts: 57.7 us -> 2.64 us  [the longest x4 1.44 us: taken(): values[:, lag].reshape(-1, 1, 1)]
    gather x6 -> x0, local copies, waits for them, and re-layouts: 32.9 us -> none  [the longest x4 29.3 us: pick_rows(): picked = jnp.take(rows, jnp.minimum(found, rows.shape[0] - 1), axis=0)]
    scatter x4 -> x0, local copies, waits for them, and re-layouts: 23.6 us -> none  [inverse_places(): jnp.full((count + 1,), places.shape[0], jnp.int32).at[places]]
    select_n x5 -> x0, other arithmetic: 15.8 us -> none  [the longest x2 15 us: pick_rows(): return jnp.where(valid[:, None], picked, 0.0)]
  transfers between devices with their start and end apart: 5 -> 13, of which waited for: 4 -> 1; matrix products, arithmetic and copies ran while one was open for 8% -> 5% of each run, Pallas kernels for 0% -> 56%
where the time goes in v1:
time: 337 us; the launch traced here: 336 us
  Pallas kernels  235 us (70%)
  starting transfers between devices  66.1 us (20%)
  local copies, waits for them, and re-layouts  11.1 us (3%)
  other arithmetic  8.63 us (3%)
  waiting for transfers between devices  7.43 us (2%)
  between operations  3.8 us (1%)
    pallas_call x4, Pallas kernels, pack_rows(): pl.pallas_call(functools.partial(pack_kernel, first), out_shape=jax.Shape...  135 us
    pallas_call x4, Pallas kernels, warp_rows(): pl.pallas_call(functools.partial(warp_kernel, first), out_shape=shapes, g...  51.1 us
    pallas_call x4, Pallas kernels, match_rows(): pl.pallas_call(body, out_shape=(jax.ShapeDtypeStruct((visits, patch_rows,...  49.6 us
    all_to_all x4, starting transfers between devices, on_device(): lax.all_to_all(block, 'patch', split_axis=0, concat_axis=0, tiled=True)  30.8 us
    ppermute x4, starting transfers between devices, on_device(): below = lax.ppermute(head, 'patch', up_pairs)  23.1 us
    ppermute x4, starting transfers between devices, on_device(): above = lax.ppermute(tail, 'patch', down_pairs)  7.94 us
    all_to_all x1, waiting for transfers between devices, on_device(): lax.all_to_all(total.reshape(parts, patch_rows // parts, row_width), 'vis...  7.4 us
  transfers between devices with their start and end apart: 13, of which 1 were waited for; matrix products, arithmetic and copies ran while one was open for 5% of the time, Pallas kernels for 56%

profile of v1, /device:TPU:8, one launch (start us, length us, event | category | flops | bytes accessed | tf_op | source)
XLA Modules:
  0.0 335.6 jit_solution(17164548947253070843)
XLA Ops:
  0.6 33.6 %pack_rows.7 = f32[32,2,32,2,128]{4,3,2,1,0:T(2,128)} custom-call(s32[8,32]{1,0:T(8,128)} %places_ref.7, f32[8,4,32,8,128]{4,3,2,1,0:T(8,128)} %bitcast.81), custom_call_target="tpu_custom_call" | custom-call | bytes 16777216 | tf_op jit(solution)/shard_map/pack_rows/pallas_call | solution.py:38
  34.3 8.6 %all-to-all-start.3 = ((f32[32,2,32,2,128]{4,3,2,1,0:T(2,128)}), f32[32,2,32,2,128]{4,3,2,1,0:T(2,128)S(1)}, u32[]{:S(2)}, u32[]{:S(2)}) async-start(f32[32,2,32,2,128]{4,3,2,1,0:T(2,128)} %pack_rows.7), calls=%async_computation.3 | async-start | bytes 4194304 | tf_op jit(solution)/shard_map/all_to_all | solution.py:365
  42.8 33.6 %pack_rows.6 = f32[32,2,32,2,128]{4,3,2,1,0:T(2,128)} custom-call(s32[8,32]{1,0:T(8,128)} %places_ref.7, f32[8,4,32,8,128]{4,3,2,1,0:T(8,128)} %bitcast.82), custom_call_target="tpu_custom_call" | custom-call | bytes 16777216 | tf_op jit(solution)/shard_map/pack_rows/pallas_call | solution.py:38
  76.5 1.3 copy-done.3
  77.8 7.4 %all-to-all-start.2 = ((f32[32,2,32,2,128]{4,3,2,1,0:T(2,128)}), f32[32,2,32,2,128]{4,3,2,1,0:T(2,128)S(1)}, u32[]{:S(2)}, u32[]{:S(2)}) async-start(f32[32,2,32,2,128]{4,3,2,1,0:T(2,128)} %pack_rows.6), calls=%async_computation.2 | async-start | bytes 4194304 | tf_op jit(solution)/shard_map/all_to_all | solution.py:365
  85.2 33.6 %pack_rows.5 = f32[32,2,32,2,128]{4,3,2,1,0:T(2,128)} custom-call(s32[8,32]{1,0:T(8,128)} %places_ref.7, f32[8,4,32,8,128]{4,3,2,1,0:T(8,128)} %bitcast.83), custom_call_target="tpu_custom_call" | custom-call | bytes 16777216 | tf_op jit(solution)/shard_map/pack_rows/pallas_call | solution.py:38
  118.8 1.3 copy-done.1
  120.2 7.4 %all-to-all-start.1 = ((f32[32,2,32,2,128]{4,3,2,1,0:T(2,128)}), f32[32,2,32,2,128]{4,3,2,1,0:T(2,128)}, u32[]{:S(2)}, u32[]{:S(2)}) async-start(f32[32,2,32,2,128]{4,3,2,1,0:T(2,128)} %pack_rows.5), calls=%async_computation.1 | async-start | bytes 4194304 | tf_op jit(solution)/shard_map/all_to_all | solution.py:365
  127.6 1.2 slice.129
  131.5 33.8 %pack_rows.4 = f32[32,2,32,2,128]{4,3,2,1,0:T(2,128)} custom-call(s32[8,32]{1,0:T(8,128)} %places_ref.7, f32[8,4,32,8,128]{4,3,2,1,0:T(8,128)} %bitcast.84), custom_call_target="tpu_custom_call" | custom-call | bytes 16777216 | tf_op jit(solution)/shard_map/pack_rows/pallas_call | solution.py:38
  165.3 0.3 pad.9.shift_ref
  165.6 0.5 slice_reduce_fusion.41
  166.2 0.1 broadcast_in_dim.699
  166.4 0.1 broadcast_in_dim.705
  166.5 0.1 broadcast_in_dim.711
  166.7 0.1 broadcast_in_dim.717
  166.8 0.1 broadcast_in_dim.723
  167.0 0.1 broadcast_in_dim.729
  167.1 0.1 broadcast_in_dim.735
  167.3 0.1 broadcast_in_dim.741
  167.4 0.1 broadcast_in_dim.747
  167.6 0.1 broadcast_in_dim.753
  167.7 0.1 broadcast_in_dim.759
  167.9 0.1 broadcast_in_dim.765
  168.0 0.1 broadcast_in_dim.771
  168.2 0.1 broadcast_in_dim.777
  168.3 0.1 broadcast_in_dim.783
  168.5 0.1 broadcast_in_dim.789
  168.8 0.1 broadcast_in_dim.801
  169.0 0.2 slice_reduce_fusion.22
  169.5 0.1 broadcast_in_dim.819
  169.5 0.4 pad.8.taps_ref
  169.9 7.4 %all-to-all-start = ((f32[32,2,32,2,128]{4,3,2,1,0:T(2,128)}), f32[32,2,32,2,128]{4,3,2,1,0:T(2,128)}, u32[]{:S(2)}, u32[]{:S(2)}) async-start(f32[32,2,32,2,128]{4,3,2,1,0:T(2,128)} %pack_rows.4), calls=%async_computation | async-start | bytes 4194304 | tf_op jit(solution)/shard_map/all_to_all | solution.py:365
  177.5 1.7 reduce-precision_convert_fusion.1
  179.2 0.2 slice_reduce_fusion.1
  179.4 0.5 slice_reduce_fusion.20
  179.9 0.5 fusion.25
  180.5 2.8 reduce-precision_convert_fusion
  183.3 0.1 fusion
  183.5 12.7 %warp_rows.7 = (f32[2,32,4224]{2,1,0:T(8,128)S(1)}, f32[2,5,2,4224]{3,2,1,0:T(2,128)}, f32[2,5,2,4224]{3,2,1,0:T(2,128)}) custom-call(s32[1]{0:T(128)} %bitcast.1.turn_ref, f32[32,2,32,2,128]{4,3,2,1,0:T(2,128)S(1)} %copy-done.4, f32[8,8,4224]{2,1,0:T(8,128)S(1)} %pad.8.taps_ref, s32[8,1,4224]{2,1,0:T(1,128)S(1)} %pad.9.shift_ref), custom_call_target="tpu_custom_call" | custom-call | bytes 10485760 | tf_op jit(solution)/shard_map/warp_rows/pallas_call | solution.py:123
  196.2 2.1 collective-permute-start.6
  198.2 5.6 %collective-permute-start.7 = (f32[2,5,2,4224]{3,2,1,0:T(2,128)}, f32[2,5,2,4224]{3,2,1,0:T(2,128)}, u32[]{:S(2)}, u32[]{:S(2)}) collective-permute-start(f32[2,5,2,4224]{3,2,1,0:T(2,128)} %get-tuple-element.33), channel_id=1, source_target_pairs={{4,0},{8,4},{12,8},{16,12},{20,16},{24,20},{28,24},{32,28},{36,32}... | collective-permute-start | bytes 1013768 | tf_op jit(solution)/shard_map/ppermute | solution.py:372
  203.9 12.7 %warp_rows.6 = (f32[2,32,4224]{2,1,0:T(8,128)S(1)}, f32[2,5,2,4224]{3,2,1,0:T(2,128)}, f32[2,5,2,4224]{3,2,1,0:T(2,128)}) custom-call(s32[1]{0:T(128)} %bitcast.1.turn_ref, f32[32,2,32,2,128]{4,3,2,1,0:T(2,128)S(1)} %copy-done.2, f32[8,8,4224]{2,1,0:T(8,128)S(1)} %pad.8.taps_ref, s32[8,1,4224]{2,1,0:T(1,128)S(1)} %pad.9.shift_ref), custom_call_target="tpu_custom_call" | custom-call | bytes 10485760 | tf_op jit(solution)/shard_map/warp_rows/pallas_call | solution.py:123
  216.6 1.9 collective-permute-start.4
  218.5 0.1 pad_maximum_fusion.refs_5_.across_ref
  218.7 5.8 %collective-permute-start.5 = (f32[2,5,2,4224]{3,2,1,0:T(2,128)}, f32[2,5,2,4224]{3,2,1,0:T(2,128)}, u32[]{:S(2)}, u32[]{:S(2)}) collective-permute-start(f32[2,5,2,4224]{3,2,1,0:T(2,128)} %get-tuple-element.30), channel_id=1, source_target_pairs={{4,0},{8,4},{12,8},{16,12},{20,16},{24,20},{28,24},{32,28},{36,32}... | collective-permute-start | bytes 1013768 | tf_op jit(solution)/shard_map/ppermute | solution.py:372
  224.4 12.9 %warp_rows.5 = (f32[2,32,4224]{2,1,0:T(8,128)S(1)}, f32[2,5,2,4224]{3,2,1,0:T(2,128)}, f32[2,5,2,4224]{3,2,1,0:T(2,128)}) custom-call(s32[1]{0:T(128)} %bitcast.1.turn_ref, f32[32,2,32,2,128]{4,3,2,1,0:T(2,128)} %all-to-all-done.1.got_ref, f32[8,8,4224]{2,1,0:T(8,128)S(1)} %pad.8.taps_ref, s32[8,1,4224]{2,1,0:T(1,128)S(1)} %pad.9.shift_ref), custom_call_target="tpu_custom_call" | custom-call | bytes 10485760 | tf_op jit(solution)/shard_map/warp_rows/pallas_call | solution.py:123
  237.4 1.0 copy-done.7
  238.4 2.0 collective-permute-start.2
  240.4 12.9 %warp_rows.4 = (f32[2,32,4224]{2,1,0:T(8,128)S(1)}, f32[2,5,2,4224]{3,2,1,0:T(2,128)}, f32[2,5,2,4224]{3,2,1,0:T(2,128)}) custom-call(s32[1]{0:T(128)} %bitcast.1.turn_ref, f32[32,2,32,2,128]{4,3,2,1,0:T(2,128)} %all-to-all-done.got_ref, f32[8,8,4224]{2,1,0:T(8,128)S(1)} %pad.8.taps_ref, s32[8,1,4224]{2,1,0:T(1,128)S(1)} %pad.9.shift_ref), custom_call_target="tpu_custom_call" | custom-call | bytes 10485760 | tf_op jit(solution)/shard_map/warp_rows/pallas_call | solution.py:123
  253.3 5.8 %collective-permute-start.3 = (f32[2,5,2,4224]{3,2,1,0:T(2,128)}, f32[2,5,2,4224]{3,2,1,0:T(2,128)}, u32[]{:S(2)}, u32[]{:S(2)}) collective-permute-start(f32[2,5,2,4224]{3,2,1,0:T(2,128)} %get-tuple-element.27), channel_id=1, source_target_pairs={{4,0},{8,4},{12,8},{16,12},{20,16},{24,20},{28,24},{32,28},{36,32}... | collective-permute-start | bytes 1013768 | tf_op jit(solution)/shard_map/ppermute | solution.py:372
  259.1 1.9 collective-permute-start
  261.0 5.9 %collective-permute-start.1 = (f32[2,5,2,4224]{3,2,1,0:T(2,128)}, f32[2,5,2,4224]{3,2,1,0:T(2,128)}, u32[]{:S(2)}, u32[]{:S(2)}) collective-permute-start(f32[2,5,2,4224]{3,2,1,0:T(2,128)} %get-tuple-element.24), channel_id=1, source_target_pairs={{4,0},{8,4},{12,8},{16,12},{20,16},{24,20},{28,24},{32,28},{36,32}... | collective-permute-start | bytes 1013768 | tf_op jit(solution)/shard_map/ppermute | solution.py:372
  267.0 1.1 pad_maximum_fusion.1.refs_4_.down_ref
  268.2 3.2 convolution_bitcast_fusion.refs_6_.coef_ref
  271.4 12.4 %match_rows.4 = (f32[8,32,4096]{2,1,0:T(8,128)}, f32[32,4096]{1,0:T(8,128)S(1)}) custom-call(f32[8]{0:T(128)S(1)} %dynamic_slice.3.refs_0_.weight_ref, f32[2,32,4224]{2,1,0:T(8,128)S(1)} %copy-done.10, f32[2,5,2,4224]{3,2,1,0:T(2,128)} %collective-permute-done.6.refs_2_, f32[2,5,2,4224]{3,2,1,0:T(2,128)} %collective-permute-done.7.refs_3_, ...), custom_call_target="tpu_custom_call" | custom-call | bytes 29360128 | tf_op jit(solution)/shard_map/match_rows/pallas_call | solution.py:265
  283.8 12.5 %match_rows.5 = (f32[8,32,4096]{2,1,0:T(8,128)}, f32[32,4096]{1,0:T(8,128)S(1)}) custom-call(f32[8]{0:T(128)S(1)} %dynamic_slice.3.refs_0_.weight_ref, f32[2,32,4224]{2,1,0:T(8,128)S(1)} %copy-done.6, f32[2,5,2,4224]{3,2,1,0:T(2,128)} %collective-permute-done.4.above_ref, ...), custom_call_target="tpu_custom_call", output_to_operand_aliasing={{0}: (9, {})} | custom-call | bytes 29360128 | tf_op jit(solution)/shard_map/match_rows/pallas_call | solution.py:265
  296.3 12.4 %match_rows.6 = (f32[8,32,4096]{2,1,0:T(8,128)}, f32[32,4096]{1,0:T(8,128)S(1)}) custom-call(f32[8]{0:T(128)S(1)} %dynamic_slice.3.refs_0_.weight_ref, f32[2,32,4224]{2,1,0:T(8,128)S(1)} %copy-done.8, f32[2,5,2,4224]{3,2,1,0:T(2,128)} %collective-permute-done.2.above_ref, ...), custom_call_target="tpu_custom_call", output_to_operand_aliasing={{0}: (9, {})} | custom-call | bytes 29360128 | tf_op jit(solution)/shard_map/match_rows/pallas_call | solution.py:265
  308.6 12.4 %match_rows.7 = (f32[8,32,4096]{2,1,0:T(8,128)}, f32[32,4096]{1,0:T(8,128)S(1)}) custom-call(f32[8]{0:T(128)S(1)} %dynamic_slice.3.refs_0_.weight_ref, f32[2,32,4224]{2,1,0:T(8,128)S(1)} %get-tuple-element.22.warped_ref, f32[2,5,2,4224]{3,2,1,0:T(2,128)} %collective-permute-done.above_ref, ...), custom_call_target="tpu_custom_call", output_to_operand_aliasing={{0}: (9, {})} | custom-call | bytes 29360128 | tf_op jit(solution)/shard_map/match_rows/pallas_call | solution.py:265
  321.0 0.8 copy-done.11
  321.8 4.3 %all-to-all-start.4 = ((f32[4,8,4096]{2,1,0:T(8,128)}), f32[4,8,4096]{2,1,0:T(8,128)S(1)}, u32[]{:S(2)}, u32[]{:S(2)}) async-start(f32[4,8,4096]{2,1,0:T(8,128)} %bitcast.80), calls=%async_computation.4 | async-start | bytes 1048576 | tf_op jit(solution)/shard_map/all_to_all | solution.py:377
  326.1 0.7 reduce_sum.19
  326.8 7.4 %all-to-all-done.4 = f32[4,8,4096]{2,1,0:T(8,128)S(1)} async-done(((f32[4,8,4096]{2,1,0:T(8,128)}), f32[4,8,4096]{2,1,0:T(8,128)S(1)}, u32[]{:S(2)}, u32[]{:S(2)}) %all-to-all-start.4) | async-done | bytes 524320 | tf_op jit(solution)/shard_map/all_to_all | solution.py:377
  334.2 1.4 broadcast_divide_fusion
  (75 shorter events, 2.1 us)
Async XLA Ops:
  34.3 42.2 %all-to-all-start.3 = ((f32[32,2,32,2,128]{4,3,2,1,0:T(2,128)}), f32[32,2,32,2,128]{4,3,2,1,0:T(2,128)S(1)}, u32[]{:S(2)}, u32[]{:S(2)}) async-start(f32[32,2,32,2,128]{4,3,2,1,0:T(2,128)} %pack_rows.7), calls=%async_computation.3 | async-start | bytes 4194304 | tf_op jit(solution)/shard_map/all_to_all | solution.py:365
  76.5 1.3 copy-start.3
  77.8 41.0 %all-to-all-start.2 = ((f32[32,2,32,2,128]{4,3,2,1,0:T(2,128)}), f32[32,2,32,2,128]{4,3,2,1,0:T(2,128)S(1)}, u32[]{:S(2)}, u32[]{:S(2)}) async-start(f32[32,2,32,2,128]{4,3,2,1,0:T(2,128)} %pack_rows.6), calls=%async_computation.2 | async-start | bytes 4194304 | tf_op jit(solution)/shard_map/all_to_all | solution.py:365
  118.8 1.3 copy-start.1
  120.2 49.8 %all-to-all-start.1 = ((f32[32,2,32,2,128]{4,3,2,1,0:T(2,128)}), f32[32,2,32,2,128]{4,3,2,1,0:T(2,128)}, u32[]{:S(2)}, u32[]{:S(2)}) async-start(f32[32,2,32,2,128]{4,3,2,1,0:T(2,128)} %pack_rows.5), calls=%async_computation.1 | async-start | bytes 4194304 | tf_op jit(solution)/shard_map/all_to_all | solution.py:365
  131.5 33.8 %copy-start.15 = (s32[8,1,4096]{2,1,0:T(1,128)S(1)}, s32[8,1,4096]{2,1,0:T(1,128)}, u32[]{:S(2)}) copy-start(s32[8,1,4096]{2,1,0:T(1,128)} %param.13) | copy-start | bytes 393220
  131.5 34.1 %copy-start.12 = (f32[9,21]{1,0:T(8,128)S(1)}, f32[9,21]{1,0:T(8,128)}, u32[]{:S(2)}) copy-start(f32[9,21]{1,0:T(8,128)} %param.14) | copy-start | bytes 2272
  131.5 38.1 %copy-start.14 = (f32[8,1,8,4096]{3,2,1,0:T(8,128)S(1)}, f32[8,1,8,4096]{3,2,1,0:T(8,128)}, u32[]{:S(2)}) copy-start(f32[8,1,8,4096]{3,2,1,0:T(8,128)} %param.12) | copy-start | bytes 3145732
  169.9 9.3 %copy-start.13 = (f32[9,21]{1,0:T(8,128)S(1)}, f32[9,21]{1,0:T(8,128)}, u32[]{:S(2)}) copy-start(f32[9,21]{1,0:T(8,128)} %param.15) | copy-start | bytes 2272
  169.9 70.5 %all-to-all-start = ((f32[32,2,32,2,128]{4,3,2,1,0:T(2,128)}), f32[32,2,32,2,128]{4,3,2,1,0:T(2,128)}, u32[]{:S(2)}, u32[]{:S(2)}) async-start(f32[32,2,32,2,128]{4,3,2,1,0:T(2,128)} %pack_rows.4), calls=%async_computation | async-start | bytes 4194304 | tf_op jit(solution)/shard_map/all_to_all | solution.py:365
  180.5 3.0 copy-start.4
  183.5 20.4 %copy-start.2 = (f32[32,2,32,2,128]{4,3,2,1,0:T(2,128)S(1)}, f32[32,2,32,2,128]{4,3,2,1,0:T(2,128)}, u32[]{:S(2)}) copy-start(f32[32,2,32,2,128]{4,3,2,1,0:T(2,128)} %copy-done.1) | copy-start | bytes 6291460
  196.1 20.4 %copy-start.9 = (f32[2,32,4224]{2,1,0:T(8,128)}, f32[2,32,4224]{2,1,0:T(8,128)S(1)}, u32[]{:S(2)}) copy-start(f32[2,32,4224]{2,1,0:T(8,128)S(1)} %get-tuple-element.31.refs_1_) | copy-start | bytes 3244036
  196.2 57.2 %collective-permute-start.6 = (f32[2,5,2,4224]{3,2,1,0:T(2,128)}, f32[2,5,2,4224]{3,2,1,0:T(2,128)}, u32[]{:S(2)}, u32[]{:S(2)}) collective-permute-start(f32[2,5,2,4224]{3,2,1,0:T(2,128)} %get-tuple-element.32), channel_id=1, source_target_pairs={{0,4},{4,8},{8,12},{12,16},{16,20},{20,24},{24,28},{28,32},{32,36}... | collective-permute-start | bytes 1013768 | tf_op jit(solution)/shard_map/ppermute | solution.py:371
  198.2 60.9 %collective-permute-start.7 = (f32[2,5,2,4224]{3,2,1,0:T(2,128)}, f32[2,5,2,4224]{3,2,1,0:T(2,128)}, u32[]{:S(2)}, u32[]{:S(2)}) collective-permute-start(f32[2,5,2,4224]{3,2,1,0:T(2,128)} %get-tuple-element.33), channel_id=1, source_target_pairs={{4,0},{8,4},{12,8},{16,12},{20,16},{24,20},{28,24},{32,28},{36,32}... | collective-permute-start | bytes 1013768 | tf_op jit(solution)/shard_map/ppermute | solution.py:372
  216.6 2.1 copy-start.5
  216.6 44.5 %collective-permute-start.4 = (f32[2,5,2,4224]{3,2,1,0:T(2,128)}, f32[2,5,2,4224]{3,2,1,0:T(2,128)}, u32[]{:S(2)}, u32[]{:S(2)}) collective-permute-start(f32[2,5,2,4224]{3,2,1,0:T(2,128)} %get-tuple-element.29), channel_id=1, source_target_pairs={{0,4},{4,8},{8,12},{12,16},{16,20},{20,24},{24,28},{28,32},{32,36}... | collective-permute-start | bytes 1013768 | tf_op jit(solution)/shard_map/ppermute | solution.py:371
  218.7 65.1 %collective-permute-start.5 = (f32[2,5,2,4224]{3,2,1,0:T(2,128)}, f32[2,5,2,4224]{3,2,1,0:T(2,128)}, u32[]{:S(2)}, u32[]{:S(2)}) collective-permute-start(f32[2,5,2,4224]{3,2,1,0:T(2,128)} %get-tuple-element.30), channel_id=1, source_target_pairs={{4,0},{8,4},{12,8},{16,12},{20,16},{24,20},{28,24},{32,28},{36,32}... | collective-permute-start | bytes 1013768 | tf_op jit(solution)/shard_map/ppermute | solution.py:372
  237.4 1.0 copy-start.7
  238.4 29.7 %copy-start.16 = (f32[32]{0:T(128)S(1)}, f32[32]{0:T(128)}, u32[]{:S(2)}) copy-start(f32[32]{0:T(128)} %param.19) | copy-start | bytes 388
  238.4 57.9 %collective-permute-start.2 = (f32[2,5,2,4224]{3,2,1,0:T(2,128)}, f32[2,5,2,4224]{3,2,1,0:T(2,128)}, u32[]{:S(2)}, u32[]{:S(2)}) collective-permute-start(f32[2,5,2,4224]{3,2,1,0:T(2,128)} %get-tuple-element.26), channel_id=1, source_target_pairs={{0,4},{4,8},{8,12},{12,16},{16,20},{20,24},{24,28},{28,32},{32,36}... | collective-permute-start | bytes 1013768 | tf_op jit(solution)/shard_map/ppermute | solution.py:371
  253.3 42.9 %collective-permute-start.3 = (f32[2,5,2,4224]{3,2,1,0:T(2,128)}, f32[2,5,2,4224]{3,2,1,0:T(2,128)}, u32[]{:S(2)}, u32[]{:S(2)}) collective-permute-start(f32[2,5,2,4224]{3,2,1,0:T(2,128)} %get-tuple-element.27), channel_id=1, source_target_pairs={{4,0},{8,4},{12,8},{16,12},{20,16},{24,20},{28,24},{32,28},{36,32}... | collective-permute-start | bytes 1013768 | tf_op jit(solution)/shard_map/ppermute | solution.py:372
  259.1 49.5 %collective-permute-start = (f32[2,5,2,4224]{3,2,1,0:T(2,128)}, f32[2,5,2,4224]{3,2,1,0:T(2,128)}, u32[]{:S(2)}, u32[]{:S(2)}) collective-permute-start(f32[2,5,2,4224]{3,2,1,0:T(2,128)} %get-tuple-element.23), channel_id=1, source_target_pairs={{0,4},{4,8},{8,12},{12,16},{16,20},{20,24},{24,28},{28,32},{32,36}... | collective-permute-start | bytes 1013768 | tf_op jit(solution)/shard_map/ppermute | solution.py:371
  261.0 47.6 %collective-permute-start.1 = (f32[2,5,2,4224]{3,2,1,0:T(2,128)}, f32[2,5,2,4224]{3,2,1,0:T(2,128)}, u32[]{:S(2)}, u32[]{:S(2)}) collective-permute-start(f32[2,5,2,4224]{3,2,1,0:T(2,128)} %get-tuple-element.24), channel_id=1, source_target_pairs={{4,0},{8,4},{12,8},{16,12},{20,16},{24,20},{28,24},{32,28},{36,32}... | collective-permute-start | bytes 1013768 | tf_op jit(solution)/shard_map/ppermute | solution.py:372
  267.0 4.4 %copy-start = (f32[32,4096]{1,0:T(8,128)S(1)}, f32[32,4096]{1,0:T(8,128)}, u32[]{:S(2)}) copy-start(f32[32,4096]{1,0:T(8,128)} %template_ref.5) | copy-start | bytes 1572868
  268.1 3.3 copy-start.10
  271.4 12.4 %copy-start.6 = (f32[2,32,4224]{2,1,0:T(8,128)S(1)}, f32[2,32,4224]{2,1,0:T(8,128)}, u32[]{:S(2)}) copy-start(f32[2,32,4224]{2,1,0:T(8,128)} %copy-done.5) | copy-start | bytes 3244036
  283.8 12.5 %copy-start.8 = (f32[2,32,4224]{2,1,0:T(8,128)S(1)}, f32[2,32,4224]{2,1,0:T(8,128)}, u32[]{:S(2)}) copy-start(f32[2,32,4224]{2,1,0:T(8,128)} %copy-done.7) | copy-start | bytes 3244036
  321.0 0.8 copy-start.11
  321.8 12.4 %all-to-all-start.4 = ((f32[4,8,4096]{2,1,0:T(8,128)}), f32[4,8,4096]{2,1,0:T(8,128)S(1)}, u32[]{:S(2)}, u32[]{:S(2)}) async-start(f32[4,8,4096]{2,1,0:T(8,128)} %bitcast.80), calls=%async_computation.4 | async-start | bytes 1048576 | tf_op jit(solution)/shard_map/all_to_all | solution.py:377

commit v2 on v1

--- a/solution.py
+++ b/solution.py
@@ -10,137 +10,137 @@
 lane = 128
 half_lane = 64
 group = 1024
-chunks = (2, 2, 2, 2)
+chunks = (4, 3, 1)
 bf16 = jnp.bfloat16
 
 
-def pack_kernel(first, places_ref, rows_ref, sent_ref, sem):
-    count = sent_ref.shape[1]
+def pack_kernel(first, places_ref, rows_ref, sent_ref):
+    tiles = sent_ref.shape[2] // 2
     patch_rows = places_ref.shape[1]
-
-    def step(item, carry):
-        local = item // patch_rows
-        row = item % patch_rows
-        place = places_ref[first + local, row]
-        pltpu.make_async_copy(
-            rows_ref.at[first + local, row // 8, :, row % 8, :],
-            sent_ref.at[place // patch_rows, local, :, place % 2, :],
-            sem,
-        ).start()
+    visit = first + pl.program_id(0)
+
+    def step(row, carry):
+        place = places_ref[visit, row]
+        start = (row // 8) * (8 * tiles) + row % 8
+        cells = rows_ref[0, pl.ds(start, tiles, stride=8), :]
+        at = pl.multiple_of((place % 2) * tiles, tiles)
+        sent_ref[place // patch_rows, pl.program_id(0), pl.ds(at, tiles), :] = cells
         return carry
 
-    lax.fori_loop(0, count * patch_rows, step, 0)
-    everything = rows_ref.at[pl.ds(first, count)]
-    pltpu.make_async_copy(everything, everything, sem).wait()
+    lax.fori_loop(0, patch_rows, step, 0, unroll=4)
 
 
 def pack_rows(first, count, tract_row, tiled_rows, patches):
+    visits, cells, _ = tiled_rows.shape
+    tiles = cells // tract_row.shape[1]
+    shape = (patches, count, 2 * tiles, lane)
     return pl.pallas_call(
         functools.partial(pack_kernel, first),
-        out_shape=jax.ShapeDtypeStruct(
-            (patches, count, tiled_rows.shape[2], 2, lane), jnp.float32
+        out_shape=jax.ShapeDtypeStruct(shape, jnp.float32),
+        grid=(count,),
+        in_specs=[
+            pl.BlockSpec(memory_space=pltpu.SMEM),
+            pl.BlockSpec((1, cells, lane), lambda q: (q + first, 0, 0)),
+        ],
+        out_specs=pl.BlockSpec(shape, lambda q: (0, 0, 0, 0)),
+        compiler_params=pltpu.CompilerParams(vmem_limit_bytes=32 << 20),
+        cost_estimate=pl.CostEstimate(flops=0, bytes_accessed=3 * count << 20, transcendentals=0),
+        name="pack_rows",
+    )(tract_row, tiled_rows)
+
+
+def pick_lanes(cells, index):
+    return jnp.take_along_axis(cells, index, axis=1, mode="promise_in_bounds")
+
+
+def warp_kernel(
+    first, turn_ref, got_ref, taps_ref, shift_ref, warped_ref, head_ref, tail_ref, rows, sems
+):
+    patches, count, depth = got_ref.shape[:3]
+    tiles = depth // 2
+    patch_rows = warped_ref.shape[1]
+    groups = patch_rows // 8
+    visit = pl.program_id(0)
+
+    @pl.when(visit == 0)
+    def _():
+        def fetch(item, carry):
+            local = item // (patch_rows // 2)
+            pair = item % (patch_rows // 2)
+            source = (turn_ref[0] + first + local - pair + 2 * patches) % patches
+            pltpu.make_async_copy(
+                got_ref.at[source, local],
+                rows.at[local, pl.ds(pl.multiple_of(pair * depth, depth), depth), :],
+                sems.at[local],
+            ).start()
+            return carry
+
+        lax.fori_loop(0, count * patch_rows // 2, fetch, 0)
+
+    pltpu.make_async_copy(rows.at[visit], rows.at[visit], sems.at[visit]).wait()
+    blank = jnp.zeros((8, lane), jnp.float32)
+    columns = lax.broadcasted_iota(jnp.int32, (8, lane), 1) + half_lane
+
+    def tile_step(u, carry):
+        window = pl.ds(pl.multiple_of(u * lane, lane), lane)
+        base = columns + jnp.broadcast_to(shift_ref[0, :, window], (8, lane))
+        totals = [blank] * groups
+        left, right = jnp.maximum(u - 1, 0), jnp.minimum(u, tiles - 1)
+        lows, highs = [], []
+        for g in range(groups):
+            low = rows[visit, pl.ds(8 * g * tiles + left, 8, stride=tiles), :]
+            high = rows[visit, pl.ds(8 * g * tiles + right, 8, stride=tiles), :]
+            lows.append(jnp.where(u > 0, low, 0.0))
+            highs.append(jnp.where(u < tiles, high, 0.0))
+        for k in range(taps_ref.shape[1]):
+            spot = base + k
+            index = spot & (lane - 1)
+            upper = spot >= lane
+            tap = jnp.broadcast_to(taps_ref[0, k : k + 1, window], (8, lane))
+            for g in range(groups):
+                picked = jnp.where(upper, pick_lanes(highs[g], index), pick_lanes(lows[g], index))
+                totals[g] = totals[g] + tap * picked
+        for g in range(groups):
+            warped_ref[0, 8 * g : 8 * g + 8, window] = totals[g]
+        return carry
+
+    lax.fori_loop(0, tiles + 1, tile_step, 0)
+    edge = head_ref.shape[1]
+    last = patch_rows - 2 * edge
+    for i in range(edge):
+        head_ref[0, i] = warped_ref[0, 2 * i : 2 * i + 2, :]
+        tail_ref[0, i] = warped_ref[0, last + 2 * i : last + 2 * i + 2, :]
+
+
+def warp_rows(first, turn, got, taps, shift, patch_rows, edge):
+    patches, count, depth = got.shape[:3]
+    width = (depth // 2 + 1) * lane
+    edges = jax.ShapeDtypeStruct((count, edge, 2, width), jnp.float32)
+    return pl.pallas_call(
+        functools.partial(warp_kernel, first),
+        out_shape=(
+            jax.ShapeDtypeStruct((count, patch_rows, width), jnp.float32),
+            edges,
+            edges,
         ),
+        grid=(count,),
         in_specs=[
             pl.BlockSpec(memory_space=pltpu.SMEM),
             pl.BlockSpec(memory_space=pl.ANY),
-        ],
-        out_specs=pl.BlockSpec(memory_space=pl.ANY),
-        scratch_shapes=[pltpu.SemaphoreType.DMA],
-        cost_estimate=pl.CostEstimate(flops=0, bytes_accessed=8 * count << 20, transcendentals=0),
-        name="pack_rows",
-    )(tract_row, tiled_rows)
-
-
-def pick_lanes(cells, index):
-    return jnp.take_along_axis(cells, index, axis=1, mode="promise_in_bounds")
-
-
-def warp_kernel(
-    first, turn_ref, got_ref, taps_ref, shift_ref, warped_ref, head_ref, tail_ref, image, sems
-):
-    patches, count, tiles = got_ref.shape[:3]
-    pairs = warped_ref.shape[1] // 2
-    for local in range(count):
-
-        def fetch(pair, carry):
-            source = (turn_ref[0] + first + local - pair + 2 * patches) % patches
-            pltpu.make_async_copy(
-                got_ref.at[source, local],
-                image.at[local, pair // 4, pl.ds(1, tiles), pl.ds(2 * (pair % 4), 2), :],
-                sems.at[local],
-            ).start()
-            return carry
-
-        lax.fori_loop(0, pairs, fetch, 0)
-    blank = jnp.zeros((8, lane), jnp.float32)
-    groups = image.shape[1]
-    for local in range(count):
-        for g in range(groups):
-            image[local, g, 0] = blank
-            image[local, g, tiles + 1] = blank
-    columns = lax.broadcasted_iota(jnp.int32, (8, lane), 1) + half_lane
-    for local in range(count):
-        whole = image.at[local, :, pl.ds(1, tiles)]
-        pltpu.make_async_copy(whole, whole, sems.at[local]).wait()
-
-        def tile_step(u, carry):
-            window = pl.ds(pl.multiple_of(u * lane, lane), lane)
-            base = columns + jnp.broadcast_to(shift_ref[local, :, window], (8, lane))
-            totals = [blank] * groups
-            lows = [image[local, g, u] for g in range(groups)]
-            highs = [image[local, g, u + 1] for g in range(groups)]
-            for k in range(taps_ref.shape[1]):
-                spot = base + k
-                index = spot & (lane - 1)
-                upper = spot >= lane
-                tap = jnp.broadcast_to(taps_ref[local, k : k + 1, window], (8, lane))
-                for g in range(groups):
-                    picked = jnp.where(
-                        upper, pick_lanes(highs[g], index), pick_lanes(lows[g], index)
-                    )
-                    totals[g] = totals[g] + tap * picked
-            for g in range(groups):
-                warped_ref[local, 8 * g : 8 * g + 8, window] = totals[g]
-            return carry
-
-        lax.fori_loop(0, tiles + 1, tile_step, 0)
-        edge = head_ref.shape[1]
-        last = warped_ref.shape[1] - 2 * edge
-        for i in range(edge):
-            head_ref[local, i] = warped_ref[local, 2 * i : 2 * i + 2, :]
-            tail_ref[local, i] = warped_ref[local, last + 2 * i : last + 2 * i + 2, :]
-
-
-def warp_rows(first, turn, got, taps, shift, patch_rows, edge):
-    patches, count, tiles = got.shape[:3]
-    width = (tiles + 1) * lane
-    shapes = (
-        jax.ShapeDtypeStruct((count, patch_rows, width), jnp.float32),
-        jax.ShapeDtypeStruct((count, edge, 2, width), jnp.float32),
-        jax.ShapeDtypeStruct((count, edge, 2, width), jnp.float32),
-    )
-    part = first // count
-    return pl.pallas_call(
-        functools.partial(warp_kernel, first),
-        out_shape=shapes,
-        grid=(1,),
-        in_specs=[
-            pl.BlockSpec(memory_space=pltpu.SMEM),
-            pl.BlockSpec(memory_space=pl.ANY),
-            pl.BlockSpec((count,) + taps.shape[1:], lambda i: (part, 0, 0)),
-            pl.BlockSpec((count,) + shift.shape[1:], lambda i: (part, 0, 0)),
+            pl.BlockSpec((1,) + taps.shape[1:], lambda q: (q + first, 0, 0)),
+            pl.BlockSpec((1,) + shift.shape[1:], lambda q: (q + first, 0, 0)),
         ],
         out_specs=[
-            pl.BlockSpec(shapes[0].shape, lambda i: (0, 0, 0)),
-            pl.BlockSpec(shapes[1].shape, lambda i: (0, 0, 0, 0)),
-            pl.BlockSpec(shapes[2].shape, lambda i: (0, 0, 0, 0)),
+            pl.BlockSpec((1, patch_rows, width), lambda q: (q, 0, 0)),
+            pl.BlockSpec((1, edge, 2, width), lambda q: (q, 0, 0, 0)),
+            pl.BlockSpec((1, edge, 2, width), lambda q: (q, 0, 0, 0)),
         ],
         scratch_shapes=[
-            pltpu.VMEM((count, patch_rows // 8, tiles + 2, 8, lane), jnp.float32),
+            pltpu.VMEM((count, patch_rows // 2 * depth, lane), jnp.float32),
             pltpu.SemaphoreType.DMA((count,)),
         ],
         compiler_params=pltpu.CompilerParams(vmem_limit_bytes=32 << 20),
-        cost_estimate=pl.CostEstimate(flops=0, bytes_accessed=5 * count << 20, transcendentals=0),
+        cost_estimate=pl.CostEstimate(flops=0, bytes_accessed=12 * count << 20, transcendentals=0),
         name="warp_rows",
     )(turn, got, taps, shift)
 
@@ -292,7 +292,7 @@
         ],
         input_output_aliases=aliases,
         compiler_params=pltpu.CompilerParams(vmem_limit_bytes=48 << 20),
-        cost_estimate=pl.CostEstimate(flops=0, bytes_accessed=14 * count << 20, transcendentals=0),
+        cost_estimate=pl.CostEstimate(flops=0, bytes_accessed=20 * count << 20, transcendentals=0),
         name="match_rows",
     )(weights, warped, above, below, down, across, coefs, template, before, *extra)
 
@@ -329,6 +329,7 @@
     tiles = row_width // lane
 
     tiled_rows = ccd_rows.reshape(visits, patch_rows // 8, 8, tiles, lane).transpose(0, 1, 3, 2, 4)
+    tiled_rows = tiled_rows.reshape(visits, patch_rows * tiles, lane)
     place = tract_row[0, 0]
     offset = place // patch_rows - here - (place % patch_rows) // 2
     turn = ((here - offset) % patches).astype(jnp.int32).reshape(1)
@@ -367,6 +368,8 @@
     down_pairs = [(i, i + 1) for i in range(patches - 1)]
     up_pairs = [(i + 1, i) for i in range(patches - 1)]
     for first, block in zip(starts, got):
+        if total is not None:
+            turn, total = lax.optimization_barrier((turn, total))
         warped, head, tail = warp_rows(first, turn, block, taps, shift, patch_rows, edge)
         above = lax.ppermute(tail, "patch", down_pairs)
         below = lax.ppermute(head, "patch", up_pairs)

time: 337 us -> 263 us (0.78)
  Pallas kernels: 235 us -> 108 us
  waiting for transfers between devices: 7.43 us -> 64.9 us
  starting transfers between devices: 66.1 us -> 52.1 us
  local copies, waits for them, and re-layouts: 11.1 us -> 22.5 us
    pallas_call x4 -> x3, Pallas kernels: 135 us -> 8.82 us  [pack_rows(): pl.pallas_call(functools.partial(pack_kernel, first), out_shape=jax.Shape...]
    all_to_all x4 -> x3, waiting for transfers between devices: 0.01 us -> 44.1 us  [on_device(): lax.all_to_all(block, 'patch', split_axis=0, concat_axis=0, tiled=True)]
    unnamed x34 -> x52, local copies, waits for them, and re-layouts: 4.51 us -> 16.6 us
    ppermute x4 -> x3, waiting for transfers between devices: 0.01 us -> 7.77 us  [on_device(): below = lax.ppermute(head, 'patch', up_pairs)]
    all_to_all x4 -> x3, starting transfers between devices: 30.8 us -> 23.2 us  [on_device(): lax.all_to_all(block, 'patch', split_axis=0, concat_axis=0, tiled=True)]
    ppermute x4 -> x3, waiting for transfers between devices: 0.01 us -> 5.67 us  [on_device(): above = lax.ppermute(tail, 'patch', down_pairs)]
    ppermute x4 -> x3, starting transfers between devices: 23.1 us -> 18.7 us  [on_device(): below = lax.ppermute(head, 'patch', up_pairs)]
    pallas_call x4 -> x3, Pallas kernels: 49.6 us -> 45.6 us  [match_rows(): pl.pallas_call(body, out_shape=(jax.ShapeDtypeStruct((visits, patch_rows,...]
  transfers between devices with their start and end apart: 13 -> 10, of which waited for: 1 -> 7; matrix products, arithmetic and copies ran while one was open for 5% -> 6% of each run, Pallas kernels for 56% -> 35%
where the time goes in v2:
time: 263 us; the launch traced here: 261 us
  Pallas kernels  108 us (41%)
  waiting for transfers between devices  64.9 us (25%)
  starting transfers between devices  52.1 us (20%)
  local copies, waits for them, and re-layouts  22.5 us (9%)
  other arithmetic  8.89 us (3%)
  between operations  3.67 us (1%)
    pallas_call x3, Pallas kernels, warp_rows(): pl.pallas_call(functools.partial(warp_kernel, first), out_shape=(jax.Shap...  53.7 us
    pallas_call x3, Pallas kernels, match_rows(): pl.pallas_call(body, out_shape=(jax.ShapeDtypeStruct((visits, patch_rows,...  45.6 us
    all_to_all x3, waiting for transfers between devices, on_device(): lax.all_to_all(block, 'patch', split_axis=0, concat_axis=0, tiled=True)  44.1 us
    all_to_all x3, starting transfers between devices, on_device(): lax.all_to_all(block, 'patch', split_axis=0, concat_axis=0, tiled=True)  23.2 us
    ppermute x3, starting transfers between devices, on_device(): below = lax.ppermute(head, 'patch', up_pairs)  18.7 us
    unnamed x52, local copies, waits for them, and re-layouts  16.6 us
    pallas_call x3, Pallas kernels, pack_rows(): pl.pallas_call(functools.partial(pack_kernel, first), out_shape=jax.Shape...  8.82 us
    ppermute x3, waiting for transfers between devices, on_device(): below = lax.ppermute(head, 'patch', up_pairs)  7.77 us
  transfers between devices with their start and end apart: 10, of which 7 were waited for; matrix products, arithmetic and copies ran while one was open for 6% of the time, Pallas kernels for 35%

profile of v2, /device:TPU:8, one launch (start us, length us, event | category | flops | bytes accessed | tf_op | source)
XLA Modules:
  0.0 261.1 jit_solution(11183120553700044978)
XLA Ops:
  0.6 2.2 copy-done
  2.8 0.7 copy-done.17
  3.5 2.8 %pack_rows.3 = f32[32,4,64,128]{3,2,1,0:T(8,128)S(1)} custom-call(s32[8,32]{1,0:T(8,128)S(1)} %copy-done.17, f32[8,1024,128]{2,1,0:T(8,128)S(1)} %bitcast.82), custom_call_target="tpu_custom_call" | custom-call | bytes 12582912 | tf_op jit(solution)/shard_map/pack_rows/pallas_call | solution.py:37
  6.3 2.0 copy-done.8
  8.3 8.7 %all-to-all-start = ((f32[32,4,64,128]{3,2,1,0:T(8,128)}), f32[32,4,64,128]{3,2,1,0:T(8,128)}, u32[]{:S(2)}, u32[]{:S(2)}) async-start(f32[32,4,64,128]{3,2,1,0:T(8,128)} %copy-done.8), calls=%async_computation | async-start | bytes 8388608 | tf_op jit(solution)/shard_map/all_to_all | solution.py:366
  17.1 2.2 copy-done.1
  19.3 4.0 %pack_rows.4 = f32[32,3,64,128]{3,2,1,0:T(8,128)} custom-call(s32[8,32]{1,0:T(8,128)S(1)} %copy-done.18, f32[8,1024,128]{2,1,0:T(8,128)S(1)} %bitcast.83), custom_call_target="tpu_custom_call" | custom-call | bytes 9437184 | tf_op jit(solution)/shard_map/pack_rows/pallas_call | solution.py:37
  23.2 44.1 %all-to-all-done.got_ref = f32[32,4,64,128]{3,2,1,0:T(8,128)} async-done(((f32[32,4,64,128]{3,2,1,0:T(8,128)}), f32[32,4,64,128]{3,2,1,0:T(8,128)}, u32[]{:S(2)}, u32[]{:S(2)}) %all-to-all-start) | async-done | bytes 4194336 | tf_op jit(solution)/shard_map/all_to_all | solution.py:366
  67.3 9.1 %all-to-all-start.1 = ((f32[32,3,64,128]{3,2,1,0:T(8,128)}), f32[32,3,64,128]{3,2,1,0:T(8,128)}, u32[]{:S(2)}, u32[]{:S(2)}) async-start(f32[32,3,64,128]{3,2,1,0:T(8,128)} %pack_rows.4), calls=%async_computation.1 | async-start | bytes 6291456 | tf_op jit(solution)/shard_map/all_to_all | solution.py:366
  76.5 0.5 slice.129
  79.6 2.2 copy-done.2
  81.8 2.1 pack_rows.5
  83.9 0.3 pad.9.shift_ref
  84.2 0.5 slice_reduce_fusion.41
  84.8 0.1 broadcast_in_dim.699
  85.0 0.1 broadcast_in_dim.705
  85.1 0.1 broadcast_in_dim.711
  85.3 0.1 broadcast_in_dim.717
  85.6 0.1 broadcast_in_dim.729
  85.9 0.1 broadcast_in_dim.741
  86.4 0.1 broadcast_in_dim.759
  86.5 0.1 broadcast_in_dim.765
  87.3 0.1 broadcast_in_dim.795
  87.6 0.2 slice_reduce_fusion.22
  87.9 0.1 broadcast_in_dim.813
  88.2 0.4 pad.8.taps_ref
  88.8 0.9 reduce-precision_convert_fusion.1
  89.7 0.2 slice_reduce_fusion.1
  89.9 0.5 slice_reduce_fusion.20
  90.5 0.5 fusion.25
  91.0 3.7 %reduce-precision_convert_fusion = (bf16[9,256,128]{2,1,0:T(8,128)(2,1)}, f32[9,256,128]{2,1,0:T(8,128)S(1)}) fusion(f32[9]{0:T(128)S(1)} %get-tuple-element.60, pred[256,128]{1,0:T(8,128)(4,1)S(1)} %get-tuple-element.87, f32[9]{0:T(128)S(1)} %get-tuple-element.59, pred[256,128]{1,0:T(8,128)(4,1)S(1)} %get-tuple-element.88, f32[9]{0:T(128)S(1)} %get-tuple-element.41, ...), kind=kLoop, calls=%fused_computation.2 | loop fusion | flops 6782976 | bytes 2458356 | tf_op jit(solution)/shard_map/convert_element_type | solution.py:302
  94.7 0.1 fusion
  94.9 26.7 %warp_rows.3 = (f32[4,32,4224]{2,1,0:T(8,128)S(1)}, f32[4,5,2,4224]{3,2,1,0:T(2,128)}, f32[4,5,2,4224]{3,2,1,0:T(2,128)}) custom-call(s32[1]{0:T(128)} %bitcast.1.turn_ref, f32[32,4,64,128]{3,2,1,0:T(8,128)} %all-to-all-done.got_ref, f32[8,8,4224]{2,1,0:T(8,128)S(1)} %pad.8.taps_ref, s32[8,1,4224]{2,1,0:T(1,128)S(1)} %pad.9.shift_ref), custom_call_target="tpu_custom_call" | custom-call | bytes 50331648 | tf_op jit(solution)/shard_map/warp_rows/pallas_call | solution.py:119
  121.6 1.3 copy-done.13
  123.0 2.0 collective-permute-start
  125.0 5.6 %collective-permute-start.1 = (f32[4,5,2,4224]{3,2,1,0:T(2,128)}, f32[4,5,2,4224]{3,2,1,0:T(2,128)S(1)}, u32[]{:S(2)}, u32[]{:S(2)}) collective-permute-start(f32[4,5,2,4224]{3,2,1,0:T(2,128)} %get-tuple-element.23), channel_id=1, source_target_pairs={{4,0},{8,4},{12,8},{16,12},{20,16},{24,20},{28,24},{32,28},{36,32}... | collective-permute-start | bytes 2027528 | tf_op jit(solution)/shard_map/ppermute | solution.py:375
  130.7 5.3 %all-to-all-start.2 = ((f32[32,1,64,128]{3,2,1,0:T(8,128)}), f32[32,1,64,128]{3,2,1,0:T(8,128)}, u32[]{:S(2)}, u32[]{:S(2)}) async-start(f32[32,1,64,128]{3,2,1,0:T(8,128)} %pack_rows.5), calls=%async_computation.2 | async-start | bytes 2097152 | tf_op jit(solution)/shard_map/all_to_all | solution.py:366
  136.0 0.1 pad_maximum_fusion.1.refs_4_.down_ref
  136.2 1.2 pad_maximum_fusion.refs_5_.across_ref
  137.4 1.0 convolution_bitcast_fusion.refs_6_.coef_ref
  138.4 4.3 %collective-permute-done.1.refs_3_ = f32[4,5,2,4224]{3,2,1,0:T(2,128)S(1)} collective-permute-done((f32[4,5,2,4224]{3,2,1,0:T(2,128)}, f32[4,5,2,4224]{3,2,1,0:T(2,128)S(1)}, u32[]{:S(2)}, u32[]{:S(2)}) %collective-permute-start.1) | collective-permute-done | bytes 675872 | tf_op jit(solution)/shard_map/ppermute | solution.py:375
  142.7 22.6 %match_rows.3 = (f32[8,32,4096]{2,1,0:T(8,128)}, f32[32,4096]{1,0:T(8,128)S(1)}) custom-call(f32[8]{0:T(128)S(1)} %dynamic_slice.3.refs_0_.weight_ref, f32[4,32,4224]{2,1,0:T(8,128)} %copy-done.13, f32[4,5,2,4224]{3,2,1,0:T(2,128)S(1)} %collective-permute-done.refs_2_, f32[4,5,2,4224]{3,2,1,0:T(2,128)S(1)} %collective-permute-done.1.refs_3_, ...), custom_call_target="tpu_custom_call" | custom-call | bytes 83886080 | tf_op jit(solution)/shard_map/match_rows/pallas_call | solution.py:265
  165.3 19.8 %warp_rows.4 = (f32[3,32,4224]{2,1,0:T(8,128)S(1)}, f32[3,5,2,4224]{3,2,1,0:T(2,128)S(1)}, f32[3,5,2,4224]{3,2,1,0:T(2,128)S(1)}) custom-call(s32[1]{0:T(128)} %bitcast.1.turn_ref, f32[32,3,64,128]{3,2,1,0:T(8,128)} %all-to-all-done.1.got_ref, f32[8,8,4224]{2,1,0:T(8,128)S(1)} %copy-done.6, s32[8,1,4224]{2,1,0:T(1,128)S(1)} %pad.9.shift_ref), custom_call_target="tpu_custom_call" | custom-call | bytes 37748736 | tf_op jit(solution)/shard_map/warp_rows/pallas_call | solution.py:119
  185.1 1.9 collective-permute-start.2
  187.0 7.2 %collective-permute-start.3 = (f32[3,5,2,4224]{3,2,1,0:T(2,128)S(1)}, f32[3,5,2,4224]{3,2,1,0:T(2,128)S(1)}, u32[]{:S(2)}, u32[]{:S(2)}) collective-permute-start(f32[3,5,2,4224]{3,2,1,0:T(2,128)S(1)} %get-tuple-element.28), channel_id=1, source_target_pairs={{4,0},{8,4},{12,8},{16,12},{20,16},{24,20},{28,24},{32,28},{36,32}... | collective-permute-start | bytes 1520648 | tf_op jit(solution)/shard_map/ppermute | solution.py:375
  194.2 4.6 %collective-permute-done.2.above_ref = f32[3,5,2,4224]{3,2,1,0:T(2,128)S(1)} collective-permute-done((f32[3,5,2,4224]{3,2,1,0:T(2,128)S(1)}, f32[3,5,2,4224]{3,2,1,0:T(2,128)S(1)}, u32[]{:S(2)}, u32[]{:S(2)}) %collective-permute-start.2) | collective-permute-done | bytes 506912 | tf_op jit(solution)/shard_map/ppermute | solution.py:374
  198.7 1.8 collective-permute-done.3.below_ref
  200.5 17.1 %match_rows.4 = (f32[8,32,4096]{2,1,0:T(8,128)}, f32[32,4096]{1,0:T(8,128)S(1)}) custom-call(f32[8]{0:T(128)S(1)} %dynamic_slice.3.refs_0_.weight_ref, f32[3,32,4224]{2,1,0:T(8,128)S(1)} %get-tuple-element.26.warped_ref, f32[3,5,2,4224]{3,2,1,0:T(2,128)S(1)} %collective-permute-done.2.above_ref, ...), custom_call_target="tpu_custom_call", output_to_operand_aliasing={{0}: (9, {})} | custom-call | bytes 62914560 | tf_op jit(solution)/shard_map/match_rows/pallas_call | solution.py:265
  217.6 0.8 copy-done.14
  218.4 1.4 copy-done.7
  219.8 0.9 copy-done.12
  220.7 7.2 %warp_rows.5 = (f32[1,32,4224]{2,1,0:T(8,128)S(1)}, f32[1,5,2,4224]{3,2,1,0:T(2,128)S(1)}, f32[1,5,2,4224]{3,2,1,0:T(2,128)S(1)}) custom-call(s32[1]{0:T(128)} %bitcast.1.turn_ref, f32[32,1,64,128]{3,2,1,0:T(8,128)} %all-to-all-done.2.got_ref, f32[8,8,4224]{2,1,0:T(8,128)S(1)} %copy-done.7, s32[8,1,4224]{2,1,0:T(1,128)S(1)} %copy-done.12), custom_call_target="tpu_custom_call" | custom-call | bytes 12582912 | tf_op jit(solution)/shard_map/warp_rows/pallas_call | solution.py:119
  227.9 1.9 collective-permute-start.4
  229.8 5.9 %collective-permute-start.5 = (f32[1,5,2,4224]{3,2,1,0:T(2,128)S(1)}, f32[1,5,2,4224]{3,2,1,0:T(2,128)S(1)}, u32[]{:S(2)}, u32[]{:S(2)}) collective-permute-start(f32[1,5,2,4224]{3,2,1,0:T(2,128)S(1)} %get-tuple-element.35), channel_id=1, source_target_pairs={{4,0},{8,4},{12,8},{16,12},{20,16},{24,20},{28,24},{32,28},{36,32}... | collective-permute-start | bytes 506888 | tf_op jit(solution)/shard_map/ppermute | solution.py:375
  235.7 1.1 collective-permute-done.4.above_ref
  236.8 1.8 collective-permute-done.5.below_ref
  238.6 1.0 copy-done.10
  239.6 1.0 copy-done.15
  240.7 5.9 %match_rows.5 = (f32[8,32,4096]{2,1,0:T(8,128)}, f32[32,4096]{1,0:T(8,128)S(1)}) custom-call(f32[8]{0:T(128)S(1)} %dynamic_slice.3.refs_0_.weight_ref, f32[1,32,4224]{2,1,0:T(8,128)S(1)} %get-tuple-element.33.warped_ref, f32[1,5,2,4224]{3,2,1,0:T(2,128)S(1)} %collective-permute-done.4.above_ref, ...), custom_call_target="tpu_custom_call", output_to_operand_aliasing={{0}: (9, {})} | custom-call | bytes 20971520 | tf_op jit(solution)/shard_map/match_rows/pallas_call | solution.py:265
  246.6 0.8 copy-done.16
  247.4 4.3 %all-to-all-start.3 = ((f32[4,8,4096]{2,1,0:T(8,128)}), f32[4,8,4096]{2,1,0:T(8,128)S(1)}, u32[]{:S(2)}, u32[]{:S(2)}) async-start(f32[4,8,4096]{2,1,0:T(8,128)} %bitcast.85), calls=%async_computation.3 | async-start | bytes 1048576 | tf_op jit(solution)/shard_map/all_to_all | solution.py:380
  251.6 0.7 reduce_sum.19
  252.3 7.4 %all-to-all-done.3 = f32[4,8,4096]{2,1,0:T(8,128)S(1)} async-done(((f32[4,8,4096]{2,1,0:T(8,128)}), f32[4,8,4096]{2,1,0:T(8,128)S(1)}, u32[]{:S(2)}, u32[]{:S(2)}) %all-to-all-start.3) | async-done | bytes 524320 | tf_op jit(solution)/shard_map/all_to_all | solution.py:380
  259.8 1.4 broadcast_divide_fusion
  (84 shorter events, 2.7 us)
Async XLA Ops:
  0.6 2.2 copy-start
  2.8 0.7 copy-start.17
  6.3 2.0 copy-start.8
  8.3 8.8 %copy-start.18 = (s32[8,32]{1,0:T(8,128)S(1)}, s32[8,32]{1,0:T(8,128)}, u32[]{:S(2)}) copy-start(s32[8,32]{1,0:T(8,128)} %places_ref.5) | copy-start | bytes 3076
  8.3 59.0 %all-to-all-start = ((f32[32,4,64,128]{3,2,1,0:T(8,128)}), f32[32,4,64,128]{3,2,1,0:T(8,128)}, u32[]{:S(2)}, u32[]{:S(2)}) async-start(f32[32,4,64,128]{3,2,1,0:T(8,128)} %copy-done.8), calls=%async_computation | async-start | bytes 8388608 | tf_op jit(solution)/shard_map/all_to_all | solution.py:366
  17.1 2.2 copy-start.1
  67.3 63.4 %all-to-all-start.1 = ((f32[32,3,64,128]{3,2,1,0:T(8,128)}), f32[32,3,64,128]{3,2,1,0:T(8,128)}, u32[]{:S(2)}, u32[]{:S(2)}) async-start(f32[32,3,64,128]{3,2,1,0:T(8,128)} %pack_rows.4), calls=%async_computation.1 | async-start | bytes 6291456 | tf_op jit(solution)/shard_map/all_to_all | solution.py:366
  79.6 2.2 copy-start.2
  81.8 2.1 copy-start.22
  81.8 2.4 copy-start.19
  81.8 6.4 %copy-start.21 = (f32[8,1,8,4096]{3,2,1,0:T(8,128)S(1)}, f32[8,1,8,4096]{3,2,1,0:T(8,128)}, u32[]{:S(2)}) copy-start(f32[8,1,8,4096]{3,2,1,0:T(8,128)} %param.12) | copy-start | bytes 3145732
  84.2 81.1 %copy-start.11 = (s32[8,1,4224]{2,1,0:T(1,128)}, s32[8,1,4224]{2,1,0:T(1,128)S(1)}, u32[]{:S(2)}) copy-start(s32[8,1,4224]{2,1,0:T(1,128)S(1)} %pad.9.shift_ref) | copy-start | bytes 405508
  86.4 2.1 copy-start.25
  88.2 1.6 copy-start.20
  88.5 6.3 %copy-start.5 = (f32[8,8,4224]{2,1,0:T(8,128)}, f32[8,8,4224]{2,1,0:T(8,128)S(1)}, u32[]{:S(2)}) copy-start(f32[8,8,4224]{2,1,0:T(8,128)S(1)} %pad.8.taps_ref) | copy-start | bytes 3244036
  121.6 1.4 copy-start.13
  123.0 15.5 %collective-permute-start = (f32[4,5,2,4224]{3,2,1,0:T(2,128)}, f32[4,5,2,4224]{3,2,1,0:T(2,128)S(1)}, u32[]{:S(2)}, u32[]{:S(2)}) collective-permute-start(f32[4,5,2,4224]{3,2,1,0:T(2,128)} %get-tuple-element.22), channel_id=1, source_target_pairs={{0,4},{4,8},{8,12},{12,16},{16,20},{20,24},{24,28},{28,32},{32,36}... | collective-permute-start | bytes 2027528 | tf_op jit(solution)/shard_map/ppermute | solution.py:374
  125.0 17.7 %collective-permute-start.1 = (f32[4,5,2,4224]{3,2,1,0:T(2,128)}, f32[4,5,2,4224]{3,2,1,0:T(2,128)S(1)}, u32[]{:S(2)}, u32[]{:S(2)}) collective-permute-start(f32[4,5,2,4224]{3,2,1,0:T(2,128)} %get-tuple-element.23), channel_id=1, source_target_pairs={{4,0},{8,4},{12,8},{16,12},{20,16},{24,20},{28,24},{32,28},{36,32}... | collective-permute-start | bytes 2027528 | tf_op jit(solution)/shard_map/ppermute | solution.py:375
  130.7 87.7 %all-to-all-start.2 = ((f32[32,1,64,128]{3,2,1,0:T(8,128)}), f32[32,1,64,128]{3,2,1,0:T(8,128)}, u32[]{:S(2)}, u32[]{:S(2)}) async-start(f32[32,1,64,128]{3,2,1,0:T(8,128)} %pack_rows.5), calls=%async_computation.2 | async-start | bytes 2097152 | tf_op jit(solution)/shard_map/all_to_all | solution.py:366
  136.2 1.3 copy-start.23
  136.2 1.3 copy-start.24
  137.4 5.3 %copy-start.9 = (f32[32,4096]{1,0:T(8,128)S(1)}, f32[32,4096]{1,0:T(8,128)}, u32[]{:S(2)}) copy-start(f32[32,4096]{1,0:T(8,128)} %template_ref.3) | copy-start | bytes 1572868
  138.4 26.9 %copy-start.3 = (f32[8,9,4096]{2,1,0:T(8,128)}, f32[8,9,4096]{2,1,0:T(8,128)S(1)}, u32[]{:S(2)}) copy-start(f32[8,9,4096]{2,1,0:T(8,128)S(1)} %convolution_bitcast_fusion.refs_6_.coef_ref) | copy-start | bytes 3538948
  142.7 22.6 %copy-start.6 = (f32[8,8,4224]{2,1,0:T(8,128)S(1)}, f32[8,8,4224]{2,1,0:T(8,128)}, u32[]{:S(2)}) copy-start(f32[8,8,4224]{2,1,0:T(8,128)} %copy-done.5) | copy-start | bytes 3244036
  185.1 13.7 %collective-permute-start.2 = (f32[3,5,2,4224]{3,2,1,0:T(2,128)S(1)}, f32[3,5,2,4224]{3,2,1,0:T(2,128)S(1)}, u32[]{:S(2)}, u32[]{:S(2)}) collective-permute-start(f32[3,5,2,4224]{3,2,1,0:T(2,128)S(1)} %get-tuple-element.27), channel_id=1, source_target_pairs={{0,4},{4,8},{8,12},{12,16},{16,20},{20,24},{24,28},{28,32},{32,36}... | collective-permute-start | bytes 1520648 | tf_op jit(solution)/shard_map/ppermute | solution.py:374
  187.0 13.5 %collective-permute-start.3 = (f32[3,5,2,4224]{3,2,1,0:T(2,128)S(1)}, f32[3,5,2,4224]{3,2,1,0:T(2,128)S(1)}, u32[]{:S(2)}, u32[]{:S(2)}) collective-permute-start(f32[3,5,2,4224]{3,2,1,0:T(2,128)S(1)} %get-tuple-element.28), channel_id=1, source_target_pairs={{4,0},{8,4},{12,8},{16,12},{20,16},{24,20},{28,24},{32,28},{36,32}... | collective-permute-start | bytes 1520648 | tf_op jit(solution)/shard_map/ppermute | solution.py:375
  217.6 0.8 copy-start.14
  218.4 20.2 %copy-start.4 = (f32[8,9,4096]{2,1,0:T(8,128)S(1)}, f32[8,9,4096]{2,1,0:T(8,128)}, u32[]{:S(2)}) copy-start(f32[8,9,4096]{2,1,0:T(8,128)} %copy-done.3) | copy-start | bytes 3538948
  218.4 1.4 copy-start.7
  219.8 0.9 copy-start.12
  227.9 9.0 %collective-permute-start.4 = (f32[1,5,2,4224]{3,2,1,0:T(2,128)S(1)}, f32[1,5,2,4224]{3,2,1,0:T(2,128)S(1)}, u32[]{:S(2)}, u32[]{:S(2)}) collective-permute-start(f32[1,5,2,4224]{3,2,1,0:T(2,128)S(1)} %get-tuple-element.34), channel_id=1, source_target_pairs={{0,4},{4,8},{8,12},{12,16},{16,20},{20,24},{24,28},{28,32},{32,36}... | collective-permute-start | bytes 506888 | tf_op jit(solution)/shard_map/ppermute | solution.py:374
  229.8 8.8 %collective-permute-start.5 = (f32[1,5,2,4224]{3,2,1,0:T(2,128)S(1)}, f32[1,5,2,4224]{3,2,1,0:T(2,128)S(1)}, u32[]{:S(2)}, u32[]{:S(2)}) collective-permute-start(f32[1,5,2,4224]{3,2,1,0:T(2,128)S(1)} %get-tuple-element.35), channel_id=1, source_target_pairs={{4,0},{8,4},{12,8},{16,12},{20,16},{24,20},{28,24},{32,28},{36,32}... | collective-permute-start | bytes 506888 | tf_op jit(solution)/shard_map/ppermute | solution.py:375
  238.6 1.0 copy-start.10
  239.6 1.0 copy-start.15
  246.6 0.8 copy-start.16
  247.4 12.4 %all-to-all-start.3 = ((f32[4,8,4096]{2,1,0:T(8,128)}), f32[4,8,4096]{2,1,0:T(8,128)S(1)}, u32[]{:S(2)}, u32[]{:S(2)}) async-start(f32[4,8,4096]{2,1,0:T(8,128)} %bitcast.85), calls=%async_computation.3 | async-start | bytes 1048576 | tf_op jit(solution)/shard_map/all_to_all | solution.py:380

commit v3 on v2

v3 whole, which is shorter than its diff:
```python
import functools

import jax
import jax.numpy as jnp
from jax import lax
from jax.experimental import pallas as pl
from jax.experimental.pallas import tpu as pltpu
from jax.sharding import PartitionSpec as P

lane = 128
half_lane = 64
step = 108
parts = 2
room = 58 << 20
chunks = (4, 3, 1)
bf16 = jnp.bfloat16


def pack_kernel(first, places_ref, rows_ref, sent_ref):
    tiles = sent_ref.shape[2] // 2
    patch_rows = places_ref.shape[1]
    visit = first + pl.program_id(0)

    def step(row, carry):
        place = places_ref[visit, row]
        start = (row // 8) * (8 * tiles) + row % 8
        cells = rows_ref[0, pl.ds(start, tiles, stride=8), :]
        at = pl.multiple_of((place % 2) * tiles, tiles)
        sent_ref[place // patch_rows, pl.program_id(0), pl.ds(at, tiles), :] = cells
        return carry

    lax.fori_loop(0, patch_rows, step, 0, unroll=4)


def pack_rows(first, count, tract_row, tiled_rows, patches):
    visits, cells, _ = tiled_rows.shape
    tiles = cells // tract_row.shape[1]
    shape = (patches, count, 2 * tiles, lane)
    return pl.pallas_call(
        functools.partial(pack_kernel, first),
        out_shape=jax.ShapeDtypeStruct(shape, jnp.float32),
        grid=(count,),
        in_specs=[
            pl.BlockSpec(memory_space=pltpu.SMEM),
            pl.BlockSpec((1, cells, lane), lambda q: (q + first, 0, 0)),
        ],
        out_specs=pl.BlockSpec(shape, lambda q: (0, 0, 0, 0)),
        compiler_params=pltpu.CompilerParams(vmem_limit_bytes=room),
        cost_estimate=pl.CostEstimate(flops=0, bytes_accessed=3 * count << 20, transcendentals=0),
        name="pack_rows",
    )(tract_row, tiled_rows)


def split(values):
    high = values.astype(bf16)
    low = (values - high.astype(jnp.float32)).astype(bf16)
    return high, low


def warp_kernel(
    first, turn_ref, got_ref, taps_ref, shift_ref, upper_ref, lower_ref, rows, image, sems
):
    patches, count, depth = got_ref.shape[:3]
    tiles = depth // 2
    half_rows = upper_ref.shape[1]
    patch_rows = 2 * half_rows
    groups = patch_rows // 8
    visit = pl.program_id(0)

    @pl.when(visit == 0)
    def _():
        def fetch(item, carry):
            local = item // (patch_rows // 2)
            pair = item % (patch_rows // 2)
            source = (turn_ref[0] + first + local - pair + 2 * patches) % patches
            pltpu.make_async_copy(
                got_ref.at[source, local],
                rows.at[local, pl.ds(pl.multiple_of(pair * depth, depth), depth), :],
                sems.at[local],
            ).start()
            return carry

        lax.fori_loop(0, count * patch_rows // 2, fetch, 0)
        blank = jnp.zeros((2 * patch_rows, lane), bf16)
        image[:, :lane] = blank
        image[:, (tiles + 1) * lane :] = blank

    pltpu.make_async_copy(rows.at[visit], rows.at[visit], sems.at[visit]).wait()

    def split_step(tile, carry):
        values = jnp.concatenate(
            [
                rows[visit, pl.ds(8 * g * tiles + tile, 8, stride=tiles), :]
                for g in range(groups)
            ],
            axis=0,
        )
        window = pl.ds(pl.multiple_of((tile + 1) * lane, lane), lane)
        image[:, window] = jnp.concatenate(split(values), axis=0)
        return carry

    lax.fori_loop(0, tiles, split_step, 0, unroll=4)
    columns = lax.broadcasted_iota(jnp.int32, (8, lane), 1) + half_lane
    sublanes = lax.broadcasted_iota(jnp.int32, (8, lane), 0)

    def tile_step(u, carry):
        window = pl.ds(pl.multiple_of(u * lane, lane), lane)
        spot = columns + jnp.broadcast_to(shift_ref[0, :, window], (8, lane))
        taps = taps_ref[0, :, window]
        turned = jnp.take_along_axis(
            taps, (sublanes - spot) & 7, axis=0, mode="promise_in_bounds"
        )
        block = (spot >> 3) + jnp.where(sublanes < (spot & 7), 1, 0)
        high = turned.astype(bf16).astype(jnp.float32)
        low = turned - high
        here = [block == i for i in range(2 * lane // 8)]
        matrix = jnp.concatenate(
            [
                jnp.concatenate([jnp.where(m, high, 0.0) for m in here], axis=0).astype(bf16),
                jnp.concatenate([jnp.where(m, low, 0.0) for m in here], axis=0).astype(bf16),
            ],
            axis=1,
        )
        both = pl.ds(pl.multiple_of(u * lane, lane), 2 * lane)
        out = jnp.dot(image[:, both], matrix, preferred_element_type=jnp.float32)
        cells = out[:patch_rows, :lane] + out[:patch_rows, lane:] + out[patch_rows:, :lane]
        upper_ref[0, :, window] = cells[:half_rows]
        lower_ref[0, :, window] = cells[half_rows:]
        return carry

    lax.fori_loop(0, tiles + 1, tile_step, 0, unroll=3)


def warp_rows(first, turn, got, taps, shift, patch_rows):
    patches, count, depth = got.shape[:3]
    width = (depth // 2 + 1) * lane
    half_rows = patch_rows // 2
    shape = jax.ShapeDtypeStruct((count, half_rows, width), jnp.float32)
    return pl.pallas_call(
        functools.partial(warp_kernel, first),
        out_shape=(shape, shape),
        grid=(count,),
        in_specs=[
            pl.BlockSpec(memory_space=pltpu.SMEM),
            pl.BlockSpec(memory_space=pl.ANY),
            pl.BlockSpec((1,) + taps.shape[1:], lambda q: (q + first, 0, 0)),
            pl.BlockSpec((1,) + shift.shape[1:], lambda q: (q + first, 0, 0)),
        ],
        out_specs=[pl.BlockSpec((1, half_rows, width), lambda q: (q, 0, 0))] * 2,
        scratch_shapes=[
            pltpu.VMEM((count, patch_rows // 2 * depth, lane), jnp.float32),
            pltpu.VMEM((2 * patch_rows, width + lane), bf16),
            pltpu.SemaphoreType.DMA((count,)),
        ],
        compiler_params=pltpu.CompilerParams(vmem_limit_bytes=room),
        cost_estimate=pl.CostEstimate(flops=0, bytes_accessed=12 * count << 20, transcendentals=0),
        name="warp_rows",
    )(turn, got, taps, shift)


def match_kernel(
    first,
    fresh,
    weight_ref,
    upper_ref,
    lower_ref,
    above_ref,
    below_ref,
    down_ref,
    across_ref,
    coef_ref,
    template_ref,
    before_ref,
    _,
    difference_ref,
    total_ref,
    pieces,
    high_ref,
    low_ref,
    found,
):
    patch_rows, row_width = template_ref.shape
    bases = across_ref.shape[0]
    windows = pieces.shape[1] // lane
    part = high_ref.shape[1] // lane
    blocks = (upper_ref, lower_ref, above_ref, below_ref)
    half_rows = upper_ref.shape[1]
    inside = lax.broadcasted_iota(jnp.int32, (half_rows, lane), 1)

    @pl.when(pl.program_id(0) == 0)
    def _():
        total_ref[...] = jnp.zeros_like(total_ref) if fresh else before_ref[...]

    for w in range(windows):
        start = step * w + half_lane - (lane - step) // 2
        tile, turn = start // lane, start % lane
        here = slice(w * lane, (w + 1) * lane)
        for i, ref in enumerate(blocks):
            values = ref[0, :, tile * lane : (tile + 1) * lane]
            if turn:
                after = ref[0, :, (tile + 1) * lane : (tile + 2) * lane]
                values = jnp.where(
                    inside < lane - turn,
                    pltpu.roll(values, lane - turn, 1),
                    pltpu.roll(after, lane - turn, 1),
                )
            high, low = split(values)
            for j, value in enumerate((high, low, high)):
                at = (j * len(blocks) + i) * half_rows
                pieces[at : at + half_rows, here] = value

    def part_step(p, carry):
        wide = pl.ds(pl.multiple_of(p * part * lane, lane), part * lane)
        vertical = jnp.dot(down_ref[...], pieces[:, wide], preferred_element_type=jnp.float32)
        high_ref[...], low_ref[...] = split(vertical)

        def gathered(ref, b):
            rows = slice(b * patch_rows, (b + 1) * patch_rows)
            return jnp.concatenate(
                [ref[rows, lane * i : lane * (i + 1)] for i in range(part)], axis=0
            )

        matched = jnp.zeros((part * patch_rows, lane), jnp.float32)
        for b in range(bases):
            operand = jnp.concatenate([gathered(high_ref, b), gathered(low_ref, b)], axis=1)
            both = jnp.dot(operand, across_ref[b], preferred_element_type=jnp.float32)
            scales = coef_ref[0, b : b + 1, wide]
            scale = jnp.concatenate(
                [
                    jnp.broadcast_to(scales[:, lane * i : lane * (i + 1)], (patch_rows, lane))
                    for i in range(part)
                ],
                axis=0,
            )
            matched = matched + scale * (both[:, :lane] + both[:, lane:])
        found[pl.ds(pl.multiple_of(p * part * patch_rows, 8), part * patch_rows), :] = matched
        return carry

    lax.fori_loop(0, windows // part, part_step, 0)
    weight = weight_ref[first + pl.program_id(0)]
    inside = lax.broadcasted_iota(jnp.int32, (patch_rows, lane), 1)
    for tile in range(row_width // lane):
        piece = None
        for w in range(tile * lane // step, ((tile + 1) * lane - 1) // step + 1):
            start = step * w - tile * lane
            values = found[w * patch_rows : (w + 1) * patch_rows, :]
            if start % lane:
                values = pltpu.roll(values, start % lane, 1)
            piece = values if piece is None else jnp.where(inside < start, piece, values)
        here = slice(lane * tile, lane * (tile + 1))
        difference_ref[0, :, here] = piece - template_ref[:, here]
        total_ref[:, here] = total_ref[:, here] + weight * piece


def match_rows(
    first, weights, upper, lower, above, below, down, across, coefs, template, before, difference
):
    count, half_rows, width = upper.shape
    visits, bases, span = coefs.shape
    patch_rows, row_width = template.shape
    part = span // lane // parts
    fresh = before is None
    if fresh:
        before = template
    extra, aliases = [], {}
    if difference is not None:
        extra, aliases = [difference], {10: 0}
    kernel = functools.partial(match_kernel, first, fresh)
    if difference is None:

        def body(*refs):
            kernel(*refs[:10], None, *refs[10:])

    else:
        body = kernel
    rows_spec = pl.BlockSpec(template.shape, lambda q: (0, 0))
    return pl.pallas_call(
        body,
        out_shape=(
            jax.ShapeDtypeStruct((visits, patch_rows, row_width), jnp.float32),
            jax.ShapeDtypeStruct(template.shape, jnp.float32),
        ),
        grid=(count,),
        in_specs=[
            pl.BlockSpec(memory_space=pltpu.SMEM),
            *[pl.BlockSpec((1, half_rows, width), lambda q: (q, 0, 0))] * 4,
            pl.BlockSpec(down.shape, lambda q: (0, 0)),
            pl.BlockSpec(across.shape, lambda q: (0, 0, 0)),
            pl.BlockSpec((1, bases, span), lambda q: (q + first, 0, 0)),
            rows_spec,
            rows_spec,
        ]
        + [pl.BlockSpec(memory_space=pl.ANY)] * len(extra),
        out_specs=[
            pl.BlockSpec((1, patch_rows, row_width), lambda q: (q + first, 0, 0)),
            rows_spec,
        ],
        scratch_shapes=[
            pltpu.VMEM((down.shape[1], span), bf16),
            pltpu.VMEM((down.shape[0], part * lane), bf16),
            pltpu.VMEM((down.shape[0], part * lane), bf16),
            pltpu.VMEM((span // lane * patch_rows, lane), jnp.float32),
        ],
        input_output_aliases=aliases,
        compiler_params=pltpu.CompilerParams(vmem_limit_bytes=room),
        cost_estimate=pl.CostEstimate(flops=0, bytes_accessed=20 * count << 20, transcendentals=0),
        name="match_rows",
    )(weights, upper, lower, above, below, down, across, coefs, template, before, *extra)


def sum_kernel(total_ref, scale_ref, out_ref, slots, send_sems, recv_sems):
    me = lax.axis_index("visit")
    slabs = lax.axis_size("visit")
    rows = out_ref.shape[0]
    mesh_ids = pl.DeviceIdType.MESH
    barrier = pltpu.get_barrier_semaphore()
    for i in range(1, slabs):
        to = lax.rem(me + i, slabs)
        pl.semaphore_signal(barrier, inc=1, device_id={"visit": to}, device_id_type=mesh_ids)
    pl.semaphore_wait(barrier, slabs - 1)
    copies = []
    for i in range(1, slabs):
        to = lax.rem(me + i, slabs)
        copy = pltpu.make_async_remote_copy(
            src_ref=total_ref.at[pl.ds(pl.multiple_of(rows * to, rows), rows), :],
            dst_ref=slots.at[i - 1],
            send_sem=send_sems.at[i - 1],
            recv_sem=recv_sems.at[i - 1],
            device_id={"visit": to},
            device_id_type=mesh_ids,
        )
        copy.start()
        copies.append(copy)
    for copy in copies:
        copy.wait()
    result = total_ref[pl.ds(pl.multiple_of(rows * me, rows), rows), :]
    for i in range(slabs - 1):
        result = result + slots[i]
    out_ref[...] = result / scale_ref[0]


def sum_visits(total, scale):
    slabs = lax.axis_size("visit")
    shape = (total.shape[0] // slabs, total.shape[1])
    return pl.pallas_call(
        sum_kernel,
        out_shape=jax.ShapeDtypeStruct(shape, jnp.float32),
        in_specs=[
            pl.BlockSpec(memory_space=pltpu.VMEM),
            pl.BlockSpec(memory_space=pltpu.SMEM),
        ],
        out_specs=pl.BlockSpec(memory_space=pltpu.VMEM),
        scratch_shapes=[
            pltpu.VMEM((slabs - 1,) + shape, jnp.float32),
            pltpu.SemaphoreType.DMA((slabs - 1,)),
            pltpu.SemaphoreType.DMA((slabs - 1,)),
        ],
        compiler_params=pltpu.CompilerParams(collective_id=0, has_side_effects=True),
        name="sum_visits",
    )(total, scale)


def split_table(values):
    high = lax.reduce_precision(values, 8, 7)
    return high.astype(bf16), (values - high).astype(bf16)


def taken(values, index):
    table = jnp.zeros((values.shape[0],) + index.shape, jnp.float32)
    for lag in range(values.shape[1]):
        table = jnp.where((index == lag)[None], values[:, lag].reshape(-1, 1, 1), table)
    return table


def on_device(
    ccd_rows,
    tract_row,
    warp_taps,
    warp_shift,
    basis_rows,
    basis_cols,
    coef_table,
    grid_index,
    template,
    visit_weight,
):
    visits, patch_rows, row_width = ccd_rows.shape
    patches = lax.axis_size("patch")
    here = lax.axis_index("patch")
    half = basis_rows.shape[1] // 2
    tiles = row_width // lane

    tiled_rows = ccd_rows.reshape(visits, patch_rows // 8, 8, tiles, lane).transpose(0, 1, 3, 2, 4)
    tiled_rows = tiled_rows.reshape(visits, patch_rows * tiles, lane)
    place = tract_row[0, 0]
    offset = place // patch_rows - here - (place % patch_rows) // 2
    turn = ((here - offset) % patches).astype(jnp.int32).reshape(1)
    taps = jnp.pad(warp_taps[:, 0], ((0, 0), (0, 0), (half_lane, half_lane)))
    shift = jnp.pad(warp_shift, ((0, 0), (0, 0), (half_lane, half_lane)))

    windows = -(-row_width // step)
    cells = jnp.pad(grid_index[0], (0, windows * step - row_width)).reshape(windows, step)
    cells = jnp.pad(cells, ((0, 0), (0, lane - step))).reshape(-1)
    one_hot = (cells[None, :] == jnp.arange(coef_table.shape[3])[:, None]).astype(jnp.float32)
    coefs = jnp.einsum(
        "qbg,gx->qbx", coef_table[:, 0], one_hot, precision=lax.Precision.HIGHEST
    )

    rows = jnp.arange(patch_rows)
    inner = jnp.concatenate(
        [rows, jnp.arange(patch_rows // 2) - patch_rows // 2, jnp.arange(patch_rows // 2) + patch_rows]
    )
    down = taken(basis_rows, inner[None, :] - rows[:, None] + half).reshape(-1, inner.shape[0])
    down_high, down_low = split_table(down)
    down = jnp.concatenate([down_high, down_high, down_low], axis=1)
    out = jnp.arange(lane)[None, :]
    across = taken(
        basis_cols, jnp.where(out < step, jnp.arange(lane)[:, None] - out, basis_cols.shape[1])
    )
    high, low = split_table(across)
    across = jnp.concatenate(
        [
            jnp.concatenate([high, low], axis=2),
            jnp.concatenate([high, jnp.zeros_like(low)], axis=2),
        ],
        axis=1,
    )
    weights = lax.dynamic_slice_in_dim(
        visit_weight, lax.axis_index("visit") * visits, visits
    )

    starts = [sum(chunks[:i]) for i in range(len(chunks))]
    sent = [
        pack_rows(first, count, tract_row, tiled_rows, patches)
        for first, count in zip(starts, chunks)
    ]
    sent[1:], down, across, coefs, taps, shift, weights, turn = lax.optimization_barrier(
        (sent[1:], down, across, coefs, taps, shift, weights, turn)
    )
    got = [lax.all_to_all(block, "patch", split_axis=0, concat_axis=0, tiled=True) for block in sent]
    total, difference = None, None
    down_pairs = [(i, i + 1) for i in range(patches - 1)]
    up_pairs = [(i + 1, i) for i in range(patches - 1)]
    for first, block in zip(starts, got):
        if total is not None:
            turn, total = lax.optimization_barrier((turn, total))
        upper, lower = warp_rows(first, turn, block, taps, shift, patch_rows)
        above = lax.ppermute(lower, "patch", down_pairs)
        below = lax.ppermute(upper, "patch", up_pairs)
        difference, total = match_rows(
            first, weights, upper, lower, above, below, down, across, coefs, template, total, difference
        )
    coadd = sum_visits(total, jnp.sum(visit_weight).reshape(1))
    return difference, coadd


def solution(mesh):
    placed = (
        P("visit", "patch", None),
        P("visit", "patch"),
        P("visit", "patch", None, None),
        P("visit", "patch", None),
        P(),
        P(),
        P("visit", "patch", None, None),
        P("patch", None),
        P("patch", None),
        P(),
    )
    return jax.shard_map(
        on_device,
        mesh=mesh,
        in_specs=placed,
        out_specs=(P("visit", "patch", None), P(("patch", "visit"), None)),
        check_vma=False,
    )
```

time: 263 us -> 231 us (0.88)
  Pallas kernels: 108 us -> 93.9 us
  local copies, waits for them, and re-layouts: 22.5 us -> 12.1 us
  waiting for transfers between devices: 64.9 us -> 60 us
  other arithmetic: 8.89 us -> 5.44 us
    unnamed x52 -> x25, local copies, waits for them, and re-layouts: 16.6 us -> 3.25 us
    pallas_call x3 -> x4, Pallas kernels: 53.7 us -> 41.7 us  [the longest x3 30.7 us: warp_rows(): pl.pallas_call(functools.partial(warp_kernel, first), out_shape=(shape, s...]
    all_to_all x1 -> x0, waiting for transfers between devices: 7.4 us -> none  [on_device(): lax.all_to_all(total.reshape(parts, patch_rows // parts, row_width), 'vis...]
    ppermute x6, waiting for transfers between devices: 13.4 us -> 20.6 us  [the longest x3 16 us: on_device(): above = lax.ppermute(lower, 'patch', down_pairs)]
    pallas_call x3, Pallas kernels: 45.6 us -> 38.8 us  [match_rows(): pl.pallas_call(body, out_shape=(jax.ShapeDtypeStruct((visits, patch_rows,...]
    all_to_all x3, waiting for transfers between devices: 44.1 us -> 39.4 us  [on_device(): lax.all_to_all(block, 'patch', split_axis=0, concat_axis=0, tiled=True)]
    pallas_call x3, Pallas kernels: 8.82 us -> 13.3 us  [pack_rows(): pl.pallas_call(functools.partial(pack_kernel, first), out_shape=jax.Shape...]
    all_to_all x1 -> x0, starting transfers between devices: 4.28 us -> none  [on_device(): lax.all_to_all(total.reshape(parts, patch_rows // parts, row_width), 'vis...]
  transfers between devices with their start and end apart: 10 -> 9, of which waited for: 7 -> 8; matrix products, arithmetic and copies ran while one was open for 6% -> 7% of each run, Pallas kernels for 35% -> 29%
where the time goes in v3:
time: 231 us; the launch traced here: 227 us
  Pallas kernels  93.9 us (41%)
  waiting for transfers between devices  60 us (26%)
  starting transfers between devices  49.6 us (21%)
  local copies, waits for them, and re-layouts  12.1 us (5%)
  other arithmetic  5.44 us (2%)
  between operations  3.57 us (2%)
  matrix products  2.56 us (1%)
    all_to_all x3, waiting for transfers between devices, on_device(): lax.all_to_all(block, 'patch', split_axis=0, concat_axis=0, tiled=True)  39.4 us
    pallas_call x3, Pallas kernels, match_rows(): pl.pallas_call(body, out_shape=(jax.ShapeDtypeStruct((visits, patch_rows,...  38.8 us
    pallas_call x3, Pallas kernels, warp_rows(): pl.pallas_call(functools.partial(warp_kernel, first), out_shape=(shape, s...  30.7 us
    all_to_all x3, starting transfers between devices, on_device(): lax.all_to_all(block, 'patch', split_axis=0, concat_axis=0, tiled=True)  25.1 us
    ppermute x3, waiting for transfers between devices, on_device(): above = lax.ppermute(lower, 'patch', down_pairs)  16 us
    ppermute x3, starting transfers between devices, on_device(): below = lax.ppermute(upper, 'patch', up_pairs)  15.5 us
    pallas_call x3, Pallas kernels, pack_rows(): pl.pallas_call(functools.partial(pack_kernel, first), out_shape=jax.Shape...  13.3 us
    pallas_call x1, Pallas kernels, sum_visits(): pl.pallas_call(sum_kernel, out_shape=jax.ShapeDtypeStruct(shape, jnp.floa...  11 us
  transfers between devices with their start and end apart: 9, of which 8 were waited for; matrix products, arithmetic and copies ran while one was open for 7% of the time, Pallas kernels for 29%

profile of v3, /device:TPU:8, one launch (start us, length us, event | category | flops | bytes accessed | tf_op | source)
XLA Modules:
  0.0 227.1 jit_solution(11556700457514214043)
XLA Ops:
  0.6 5.8 %pack_rows.5 = f32[32,4,64,128]{3,2,1,0:T(8,128)} custom-call(s32[8,32]{1,0:T(8,128)} %places_ref.5, f32[8,1024,128]{2,1,0:T(8,128)} %bitcast.84), custom_call_target="tpu_custom_call" | custom-call | bytes 12582912 | tf_op jit(solution)/shard_map/pack_rows/pallas_call | solution.py:39
  6.4 8.6 %all-to-all-start = ((f32[32,4,64,128]{3,2,1,0:T(8,128)}), f32[32,4,64,128]{3,2,1,0:T(8,128)}, u32[]{:S(2)}, u32[]{:S(2)}) async-start(f32[32,4,64,128]{3,2,1,0:T(8,128)} %pack_rows.5), calls=%async_computation | async-start | bytes 8388608 | tf_op jit(solution)/shard_map/all_to_all | solution.py:440
  15.0 1.2 slice.171
  18.9 4.9 %pack_rows.3 = f32[32,3,64,128]{3,2,1,0:T(8,128)} custom-call(s32[8,32]{1,0:T(8,128)} %places_ref.5, f32[8,1024,128]{2,1,0:T(8,128)} %bitcast.85), custom_call_target="tpu_custom_call" | custom-call | bytes 9437184 | tf_op jit(solution)/shard_map/pack_rows/pallas_call | solution.py:39
  23.8 2.6 %pack_rows.4 = f32[32,1,64,128]{3,2,1,0:T(8,128)} custom-call(s32[8,32]{1,0:T(8,128)} %places_ref.5, f32[8,1024,128]{2,1,0:T(8,128)} %bitcast.86), custom_call_target="tpu_custom_call" | custom-call | bytes 3145728 | tf_op jit(solution)/shard_map/pack_rows/pallas_call | solution.py:39
  26.5 0.5 slice_reduce_fusion.41
  27.1 0.1 broadcast_in_dim.752
  27.2 0.1 broadcast_in_dim.758
  27.4 0.1 broadcast_in_dim.764
  27.5 0.1 broadcast_in_dim.770
  27.7 0.1 broadcast_in_dim.776
  27.8 0.1 broadcast_in_dim.782
  28.0 0.1 broadcast_in_dim.788
  28.1 0.1 broadcast_in_dim.794
  28.3 0.1 broadcast_in_dim.800
  28.4 0.1 broadcast_in_dim.806
  28.6 0.1 broadcast_in_dim.812
  28.7 0.1 broadcast_in_dim.818
  28.9 0.1 broadcast_in_dim.824
  29.0 0.1 broadcast_in_dim.830
  29.2 0.1 broadcast_in_dim.836
  29.3 0.1 broadcast_in_dim.842
  29.6 0.1 broadcast_in_dim.854
  29.9 0.2 slice_reduce_fusion.22
  30.2 0.1 broadcast_in_dim.866
  30.4 0.1 reshape.1003
  30.5 1.0 pad.20.shift_ref
  31.5 0.6 dynamic_slice.3.refs_0_.weight_ref
  32.1 1.4 pad.19.taps_ref
  33.6 0.9 reduce-precision_convert_fusion.1
  34.6 0.2 slice_reduce_fusion.1
  34.8 0.5 slice_reduce_fusion.20
  35.3 0.8 pad_maximum_fusion.refs_5_.down_ref
  36.1 0.2 fusion.29
  36.4 1.5 fusion.4
  37.9 1.2 fusion.1.refs_6_.across_ref
  39.1 2.6 %convolution_bitcast_fusion.refs_7_.coef_ref = f32[8,9,4864]{2,1,0:T(8,128)} fusion(s32[4864]{0:T(1024)S(1)} %pad_bitcast_fusion, f32[8,1,9,32]{3,1,2,0:T(1,128)S(1)} %copy-done.9), kind=kOutput, calls=%fused_computation | convolution fusion | flops 134635520 | bytes 1429504 | tf_op jit(solution)/shard_map/qbg,gx->qbx/dot_general | solution.py:405
  41.7 23.6 %all-to-all-done.got_ref = f32[32,4,64,128]{3,2,1,0:T(8,128)} async-done(((f32[32,4,64,128]{3,2,1,0:T(8,128)}), f32[32,4,64,128]{3,2,1,0:T(8,128)}, u32[]{:S(2)}, u32[]{:S(2)}) %all-to-all-start) | async-done | bytes 4194336 | tf_op jit(solution)/shard_map/all_to_all | solution.py:440
  65.3 9.1 %all-to-all-start.1 = ((f32[32,3,64,128]{3,2,1,0:T(8,128)}), f32[32,3,64,128]{3,2,1,0:T(8,128)S(1)}, u32[]{:S(2)}, u32[]{:S(2)}) async-start(f32[32,3,64,128]{3,2,1,0:T(8,128)} %pack_rows.3), calls=%async_computation.1 | async-start | bytes 6291456 | tf_op jit(solution)/shard_map/all_to_all | solution.py:440
  74.4 14.0 %warp_rows.3 = (f32[4,16,4224]{2,1,0:T(8,128)}, f32[4,16,4224]{2,1,0:T(8,128)}) custom-call(s32[1]{0:T(128)} %bitcast.34.turn_ref, f32[32,4,64,128]{3,2,1,0:T(8,128)} %all-to-all-done.got_ref, f32[8,8,4224]{2,1,0:T(8,128)} %pad.19.taps_ref, s32[8,1,4224]{2,1,0:T(1,128)} %pad.20.shift_ref), custom_call_target="tpu_custom_call" | custom-call | bytes 50331648 | tf_op jit(solution)/shard_map/warp_rows/pallas_call | solution.py:139
  88.4 2.1 collective-permute-start
  90.4 5.6 %collective-permute-start.1 = (f32[4,16,4224]{2,1,0:T(8,128)}, f32[4,16,4224]{2,1,0:T(8,128)}, u32[]{:S(2)}, u32[]{:S(2)}) collective-permute-start(f32[4,16,4224]{2,1,0:T(8,128)} %get-tuple-element.31.refs_1_), channel_id=1, source_target_pairs={{4,0},{8,4},{12,8},{16,12},{20,16},{24,20},{28,24},{32,28},{36,32}... | collective-permute-start | bytes 3244040 | tf_op jit(solution)/shard_map/ppermute | solution.py:449
  96.0 15.8 %all-to-all-done.1.got_ref = f32[32,3,64,128]{3,2,1,0:T(8,128)S(1)} async-done(((f32[32,3,64,128]{3,2,1,0:T(8,128)}), f32[32,3,64,128]{3,2,1,0:T(8,128)S(1)}, u32[]{:S(2)}, u32[]{:S(2)}) %all-to-all-start.1) | async-done | bytes 3145760 | tf_op jit(solution)/shard_map/all_to_all | solution.py:440
  111.8 7.5 %all-to-all-start.2 = ((f32[32,1,64,128]{3,2,1,0:T(8,128)}), f32[32,1,64,128]{3,2,1,0:T(8,128)}, u32[]{:S(2)}, u32[]{:S(2)}) async-start(f32[32,1,64,128]{3,2,1,0:T(8,128)} %pack_rows.4), calls=%async_computation.2 | async-start | bytes 2097152 | tf_op jit(solution)/shard_map/all_to_all | solution.py:440
  119.3 6.2 %collective-permute-done.refs_3_ = f32[4,16,4224]{2,1,0:T(8,128)} collective-permute-done((f32[4,16,4224]{2,1,0:T(8,128)}, f32[4,16,4224]{2,1,0:T(8,128)}, u32[]{:S(2)}, u32[]{:S(2)}) %collective-permute-start) | collective-permute-done | bytes 1081376 | tf_op jit(solution)/shard_map/ppermute | solution.py:448
  125.5 0.8 collective-permute-done.1.refs_4_
  126.3 18.0 %match_rows.3 = (f32[8,32,4096]{2,1,0:T(8,128)}, f32[32,4096]{1,0:T(8,128)}) custom-call(f32[8]{0:T(128)} %dynamic_slice.3.refs_0_.weight_ref, f32[4,16,4224]{2,1,0:T(8,128)} %get-tuple-element.31.refs_1_, f32[4,16,4224]{2,1,0:T(8,128)} %get-tuple-element.32.refs_2_, f32[4,16,4224]{2,1,0:T(8,128)} %collective-permute-done.refs_3_, ...), custom_call_target="tpu_custom_call" | custom-call | bytes 83886080 | tf_op jit(solution)/shard_map/match_rows/pallas_call | solution.py:277
  144.4 11.2 %warp_rows.4 = (f32[3,16,4224]{2,1,0:T(8,128)}, f32[3,16,4224]{2,1,0:T(8,128)}) custom-call(s32[1]{0:T(128)} %bitcast.34.turn_ref, f32[32,3,64,128]{3,2,1,0:T(8,128)} %copy-done, f32[8,8,4224]{2,1,0:T(8,128)} %pad.19.taps_ref, s32[8,1,4224]{2,1,0:T(1,128)} %pad.20.shift_ref), custom_call_target="tpu_custom_call" | custom-call | bytes 37748736 | tf_op jit(solution)/shard_map/warp_rows/pallas_call | solution.py:139
  155.6 4.9 %collective-permute-start.2 = (f32[3,16,4224]{2,1,0:T(8,128)}, f32[3,16,4224]{2,1,0:T(8,128)S(1)}, u32[]{:S(2)}, u32[]{:S(2)}) collective-permute-start(f32[3,16,4224]{2,1,0:T(8,128)} %get-tuple-element.40.lower_ref), channel_id=1, source_target_pairs={{0,4},{4,8},{8,12},{12,16},{16,20},{20,24},{24,28},{28,32},{32,36}... | collective-permute-start | bytes 2433032 | tf_op jit(solution)/shard_map/ppermute | solution.py:448
  160.5 4.1 %collective-permute-start.3 = (f32[3,16,4224]{2,1,0:T(8,128)}, f32[3,16,4224]{2,1,0:T(8,128)S(1)}, u32[]{:S(2)}, u32[]{:S(2)}) collective-permute-start(f32[3,16,4224]{2,1,0:T(8,128)} %get-tuple-element.39.upper_ref), channel_id=1, source_target_pairs={{4,0},{8,4},{12,8},{16,12},{20,16},{24,20},{28,24},{32,28},{36,32}... | collective-permute-start | bytes 2433032 | tf_op jit(solution)/shard_map/ppermute | solution.py:449
  164.6 8.0 %collective-permute-done.2.above_ref = f32[3,16,4224]{2,1,0:T(8,128)S(1)} collective-permute-done((f32[3,16,4224]{2,1,0:T(8,128)}, f32[3,16,4224]{2,1,0:T(8,128)S(1)}, u32[]{:S(2)}, u32[]{:S(2)}) %collective-permute-start.2) | collective-permute-done | bytes 811040 | tf_op jit(solution)/shard_map/ppermute | solution.py:448
  172.6 1.9 collective-permute-done.3.below_ref
  174.5 0.9 copy-done.5
  175.4 14.2 %match_rows.4 = (f32[8,32,4096]{2,1,0:T(8,128)}, f32[32,4096]{1,0:T(8,128)}) custom-call(f32[8]{0:T(128)} %dynamic_slice.3.refs_0_.weight_ref, f32[3,16,4224]{2,1,0:T(8,128)} %get-tuple-element.39.upper_ref, f32[3,16,4224]{2,1,0:T(8,128)} %get-tuple-element.40.lower_ref, f32[3,16,4224]{2,1,0:T(8,128)} %copy-done.4, ...), custom_call_target="tpu_custom_call", output_to_operand_aliasing={{0}: (10, {})} | custom-call | bytes 62914560 | tf_op jit(solution)/shard_map/match_rows/pallas_call | solution.py:277
  189.6 5.5 %warp_rows.5 = (f32[1,16,4224]{2,1,0:T(8,128)}, f32[1,16,4224]{2,1,0:T(8,128)}) custom-call(s32[1]{0:T(128)} %bitcast.34.turn_ref, f32[32,1,64,128]{3,2,1,0:T(8,128)} %all-to-all-done.2.got_ref, f32[8,8,4224]{2,1,0:T(8,128)} %pad.19.taps_ref, s32[8,1,4224]{2,1,0:T(1,128)} %pad.20.shift_ref), custom_call_target="tpu_custom_call" | custom-call | bytes 12582912 | tf_op jit(solution)/shard_map/warp_rows/pallas_call | solution.py:139
  195.1 1.9 collective-permute-start.4
  197.1 5.8 %collective-permute-start.5 = (f32[1,16,4224]{2,1,0:T(8,128)}, f32[1,16,4224]{2,1,0:T(8,128)S(1)}, u32[]{:S(2)}, u32[]{:S(2)}) collective-permute-start(f32[1,16,4224]{2,1,0:T(8,128)} %get-tuple-element.46.upper_ref), channel_id=1, source_target_pairs={{4,0},{8,4},{12,8},{16,12},{20,16},{24,20},{28,24},{32,28},{36,32}... | collective-permute-start | bytes 811016 | tf_op jit(solution)/shard_map/ppermute | solution.py:449
  202.9 0.6 reduce_sum.9
  203.5 1.8 collective-permute-done.4.above_ref
  205.3 1.9 collective-permute-done.5.below_ref
  207.2 0.7 copy-done.7
  207.9 6.6 %match_rows.5 = (f32[8,32,4096]{2,1,0:T(8,128)}, f32[32,4096]{1,0:T(8,128)}) custom-call(f32[8]{0:T(128)} %dynamic_slice.3.refs_0_.weight_ref, f32[1,16,4224]{2,1,0:T(8,128)} %get-tuple-element.46.upper_ref, f32[1,16,4224]{2,1,0:T(8,128)} %get-tuple-element.47.lower_ref, f32[1,16,4224]{2,1,0:T(8,128)} %copy-done.6, ...), custom_call_target="tpu_custom_call", output_to_operand_aliasing={{0}: (10, {})} | custom-call | bytes 20971520 | tf_op jit(solution)/shard_map/match_rows/pallas_call | solution.py:277
  214.5 11.0 %sum_visits.1 = f32[8,4096]{1,0:T(8,128)} custom-call(f32[32,4096]{1,0:T(8,128)} %get-tuple-element.51.total_ref, f32[1]{0:T(128)} %bitcast.35.scale_ref), custom_call_target="tpu_custom_call" | custom-call | tf_op jit(solution)/shard_map/sum_visits/pallas_call | solution.py:345
  225.5 1.6 copy.24
  (56 shorter events, 2.0 us)
Async XLA Ops:
  6.4 58.9 %all-to-all-start = ((f32[32,4,64,128]{3,2,1,0:T(8,128)}), f32[32,4,64,128]{3,2,1,0:T(8,128)}, u32[]{:S(2)}, u32[]{:S(2)}) async-start(f32[32,4,64,128]{3,2,1,0:T(8,128)} %pack_rows.5), calls=%async_computation | async-start | bytes 8388608 | tf_op jit(solution)/shard_map/all_to_all | solution.py:440
  23.8 2.7 %copy-start.1 = (f32[9,21]{1,0:T(8,128)S(1)}, f32[9,21]{1,0:T(8,128)}, u32[]{:S(2)}) copy-start(f32[9,21]{1,0:T(8,128)} %param.14) | copy-start | bytes 2272
  23.8 6.6 %copy-start.10 = (s32[1,4096]{1,0:T(1,128)S(1)}, s32[1,4096]{1,0:T(1,128)}, u32[]{:S(2)}) copy-start(s32[1,4096]{1,0:T(1,128)} %param.17) | copy-start | bytes 49156
  23.8 6.7 %copy-start.8 = (s32[8,1,4096]{2,1,0:T(1,128)S(1)}, s32[8,1,4096]{2,1,0:T(1,128)}, u32[]{:S(2)}) copy-start(s32[8,1,4096]{2,1,0:T(1,128)} %param.13) | copy-start | bytes 393220
  23.8 7.7 %copy-start.11 = (f32[32]{0:T(128)S(1)}, f32[32]{0:T(128)}, u32[]{:S(2)}) copy-start(f32[32]{0:T(128)} %param.19) | copy-start | bytes 388
  23.8 8.3 %copy-start.3 = (f32[8,1,8,4096]{3,2,1,0:T(8,128)S(1)}, f32[8,1,8,4096]{3,2,1,0:T(8,128)}, u32[]{:S(2)}) copy-start(f32[8,1,8,4096]{3,2,1,0:T(8,128)} %param.12) | copy-start | bytes 3145732
  26.5 8.1 %copy-start.2 = (f32[9,21]{1,0:T(8,128)S(1)}, f32[9,21]{1,0:T(8,128)}, u32[]{:S(2)}) copy-start(f32[9,21]{1,0:T(8,128)} %param.15) | copy-start | bytes 2272
  35.3 3.8 %copy-start.9 = (f32[8,1,9,32]{3,1,2,0:T(1,128)S(1)}, f32[8,1,9,32]{3,1,2,0:T(1,128)}, u32[]{:S(2)}) copy-start(f32[8,1,9,32]{3,1,2,0:T(1,128)} %param.16) | copy-start | bytes 27652
  65.3 46.5 %all-to-all-start.1 = ((f32[32,3,64,128]{3,2,1,0:T(8,128)}), f32[32,3,64,128]{3,2,1,0:T(8,128)S(1)}, u32[]{:S(2)}, u32[]{:S(2)}) async-start(f32[32,3,64,128]{3,2,1,0:T(8,128)} %pack_rows.3), calls=%async_computation.1 | async-start | bytes 6291456 | tf_op jit(solution)/shard_map/all_to_all | solution.py:440
  88.4 37.1 %collective-permute-start = (f32[4,16,4224]{2,1,0:T(8,128)}, f32[4,16,4224]{2,1,0:T(8,128)}, u32[]{:S(2)}, u32[]{:S(2)}) collective-permute-start(f32[4,16,4224]{2,1,0:T(8,128)} %get-tuple-element.32.refs_2_), channel_id=1, source_target_pairs={{0,4},{4,8},{8,12},{12,16},{16,20},{20,24},{24,28},{28,32},{32,36}... | collective-permute-start | bytes 3244040 | tf_op jit(solution)/shard_map/ppermute | solution.py:448
  90.4 35.9 %collective-permute-start.1 = (f32[4,16,4224]{2,1,0:T(8,128)}, f32[4,16,4224]{2,1,0:T(8,128)}, u32[]{:S(2)}, u32[]{:S(2)}) collective-permute-start(f32[4,16,4224]{2,1,0:T(8,128)} %get-tuple-element.31.refs_1_), channel_id=1, source_target_pairs={{4,0},{8,4},{12,8},{16,12},{20,16},{24,20},{28,24},{32,28},{36,32}... | collective-permute-start | bytes 3244040 | tf_op jit(solution)/shard_map/ppermute | solution.py:449
  111.8 32.6 %copy-start = (f32[32,3,64,128]{3,2,1,0:T(8,128)}, f32[32,3,64,128]{3,2,1,0:T(8,128)S(1)}, u32[]{:S(2)}) copy-start(f32[32,3,64,128]{3,2,1,0:T(8,128)S(1)} %all-to-all-done.1.got_ref) | copy-start | bytes 9437188
  111.8 77.8 %all-to-all-start.2 = ((f32[32,1,64,128]{3,2,1,0:T(8,128)}), f32[32,1,64,128]{3,2,1,0:T(8,128)}, u32[]{:S(2)}, u32[]{:S(2)}) async-start(f32[32,1,64,128]{3,2,1,0:T(8,128)} %pack_rows.4), calls=%async_computation.2 | async-start | bytes 2097152 | tf_op jit(solution)/shard_map/all_to_all | solution.py:440
  155.6 17.0 %collective-permute-start.2 = (f32[3,16,4224]{2,1,0:T(8,128)}, f32[3,16,4224]{2,1,0:T(8,128)S(1)}, u32[]{:S(2)}, u32[]{:S(2)}) collective-permute-start(f32[3,16,4224]{2,1,0:T(8,128)} %get-tuple-element.40.lower_ref), channel_id=1, source_target_pairs={{0,4},{4,8},{8,12},{12,16},{16,20},{20,24},{24,28},{28,32},{32,36}... | collective-permute-start | bytes 2433032 | tf_op jit(solution)/shard_map/ppermute | solution.py:448
  160.5 14.0 %collective-permute-start.3 = (f32[3,16,4224]{2,1,0:T(8,128)}, f32[3,16,4224]{2,1,0:T(8,128)S(1)}, u32[]{:S(2)}, u32[]{:S(2)}) collective-permute-start(f32[3,16,4224]{2,1,0:T(8,128)} %get-tuple-element.39.upper_ref), channel_id=1, source_target_pairs={{4,0},{8,4},{12,8},{16,12},{20,16},{24,20},{28,24},{32,28},{36,32}... | collective-permute-start | bytes 2433032 | tf_op jit(solution)/shard_map/ppermute | solution.py:449
  172.6 1.9 copy-start.4
  174.5 0.9 copy-start.5
  195.1 10.2 %collective-permute-start.4 = (f32[1,16,4224]{2,1,0:T(8,128)}, f32[1,16,4224]{2,1,0:T(8,128)S(1)}, u32[]{:S(2)}, u32[]{:S(2)}) collective-permute-start(f32[1,16,4224]{2,1,0:T(8,128)} %get-tuple-element.47.lower_ref), channel_id=1, source_target_pairs={{0,4},{4,8},{8,12},{12,16},{16,20},{20,24},{24,28},{28,32},{32,36}... | collective-permute-start | bytes 811016 | tf_op jit(solution)/shard_map/ppermute | solution.py:448
  197.1 10.1 %collective-permute-start.5 = (f32[1,16,4224]{2,1,0:T(8,128)}, f32[1,16,4224]{2,1,0:T(8,128)S(1)}, u32[]{:S(2)}, u32[]{:S(2)}) collective-permute-start(f32[1,16,4224]{2,1,0:T(8,128)} %get-tuple-element.46.upper_ref), channel_id=1, source_target_pairs={{4,0},{8,4},{12,8},{16,12},{20,16},{24,20},{28,24},{32,28},{36,32}... | collective-permute-start | bytes 811016 | tf_op jit(solution)/shard_map/ppermute | solution.py:449
  205.3 1.9 copy-start.6
  207.2 0.7 copy-start.7

commit v4 on v3

--- a/solution.py
+++ b/solution.py
@@ -11,8 +11,8 @@
 half_lane = 64
 step = 108
 parts = 2
-room = 58 << 20
-chunks = (4, 3, 1)
+room = 24 << 20
+chunks = (5, 3)
 bf16 = jnp.bfloat16
 
 
@@ -26,7 +26,7 @@
         start = (row // 8) * (8 * tiles) + row % 8
         cells = rows_ref[0, pl.ds(start, tiles, stride=8), :]
         at = pl.multiple_of((place % 2) * tiles, tiles)
-        sent_ref[place // patch_rows, pl.program_id(0), pl.ds(at, tiles), :] = cells
+        sent_ref[place // patch_rows, 0, pl.ds(at, tiles), :] = cells
         return carry
 
     lax.fori_loop(0, patch_rows, step, 0, unroll=4)
@@ -44,8 +44,8 @@
             pl.BlockSpec(memory_space=pltpu.SMEM),
             pl.BlockSpec((1, cells, lane), lambda q: (q + first, 0, 0)),
         ],
-        out_specs=pl.BlockSpec(shape, lambda q: (0, 0, 0, 0)),
-        compiler_params=pltpu.CompilerParams(vmem_limit_bytes=room),
+        out_specs=pl.BlockSpec((patches, 1, 2 * tiles, lane), lambda q: (0, q, 0, 0)),
+        compiler_params=pltpu.CompilerParams(vmem_limit_bytes=58 << 20),
         cost_estimate=pl.CostEstimate(flops=0, bytes_accessed=3 * count << 20, transcendentals=0),
         name="pack_rows",
     )(tract_row, tiled_rows)
@@ -128,7 +128,7 @@
         lower_ref[0, :, window] = cells[half_rows:]
         return carry
 
-    lax.fori_loop(0, tiles + 1, tile_step, 0, unroll=3)
+    lax.fori_loop(0, tiles + 1, tile_step, 0, unroll=33)
 
 
 def warp_rows(first, turn, got, taps, shift, patch_rows):
@@ -175,14 +175,14 @@
     difference_ref,
     total_ref,
     pieces,
-    high_ref,
-    low_ref,
+    high_refs,
+    low_refs,
     found,
 ):
     patch_rows, row_width = template_ref.shape
     bases = across_ref.shape[0]
     windows = pieces.shape[1] // lane
-    part = high_ref.shape[1] // lane
+    part = high_refs.shape[2] // lane
     blocks = (upper_ref, lower_ref, above_ref, below_ref)
     half_rows = upper_ref.shape[1]
     inside = lax.broadcasted_iota(jnp.int32, (half_rows, lane), 1)
@@ -191,7 +191,7 @@
     def _():
         total_ref[...] = jnp.zeros_like(total_ref) if fresh else before_ref[...]
 
-    for w in range(windows):
+    def cut_window(w):
         start = step * w + half_lane - (lane - step) // 2
         tile, turn = start // lane, start % lane
         here = slice(w * lane, (w + 1) * lane)
@@ -209,8 +209,12 @@
                 at = (j * len(blocks) + i) * half_rows
                 pieces[at : at + half_rows, here] = value
 
-    def part_step(p, carry):
-        wide = pl.ds(pl.multiple_of(p * part * lane, lane), part * lane)
+    def part_step(p):
+        for w in range(p * part, (p + 1) * part):
+            cut_window(w)
+        wide = slice(p * part * lane, (p + 1) * part * lane)
+        high_ref = high_refs.at[p]
+        low_ref = low_refs.at[p]
         vertical = jnp.dot(down_ref[...], pieces[:, wide], preferred_element_type=jnp.float32)
         high_ref[...], low_ref[...] = split(vertical)
 
@@ -233,10 +237,10 @@
                 axis=0,
             )
             matched = matched + scale * (both[:, :lane] + both[:, lane:])
-        found[pl.ds(pl.multiple_of(p * part * patch_rows, 8), part * patch_rows), :] = matched
-        return carry
-
-    lax.fori_loop(0, windows // part, part_step, 0)
+        found[p * part * patch_rows : (p + 1) * part * patch_rows, :] = matched
+
+    for p in range(windows // part):
+        part_step(p)
     weight = weight_ref[first + pl.program_id(0)]
     inside = lax.broadcasted_iota(jnp.int32, (patch_rows, lane), 1)
     for tile in range(row_width // lane):
@@ -297,8 +301,8 @@
         ],
         scratch_shapes=[
             pltpu.VMEM((down.shape[1], span), bf16),
-            pltpu.VMEM((down.shape[0], part * lane), bf16),
-            pltpu.VMEM((down.shape[0], part * lane), bf16),
+            pltpu.VMEM((parts, down.shape[0], part * lane), bf16),
+            pltpu.VMEM((parts, down.shape[0], part * lane), bf16),
             pltpu.VMEM((span // lane * patch_rows, lane), jnp.float32),
         ],
         input_output_aliases=aliases,
@@ -308,11 +312,15 @@
     )(weights, upper, lower, above, below, down, across, coefs, template, before, *extra)
 
 
-def sum_kernel(total_ref, scale_ref, out_ref, slots, send_sems, recv_sems):
+def sum_kernel(total_ref, scale_ref, out_ref, own, slots, own_sem, send_sems, recv_sems):
     me = lax.axis_index("visit")
     slabs = lax.axis_size("visit")
     rows = out_ref.shape[0]
     mesh_ids = pl.DeviceIdType.MESH
+    mine = pltpu.make_async_copy(
+        total_ref.at[pl.ds(pl.multiple_of(rows * me, rows), rows), :], own, own_sem
+    )
+    mine.start()
     barrier = pltpu.get_barrier_semaphore()
     for i in range(1, slabs):
         to = lax.rem(me + i, slabs)
@@ -333,7 +341,8 @@
         copies.append(copy)
     for copy in copies:
         copy.wait()
-    result = total_ref[pl.ds(pl.multiple_of(rows * me, rows), rows), :]
+    mine.wait()
+    result = own[...]
     for i in range(slabs - 1):
         result = result + slots[i]
     out_ref[...] = result / scale_ref[0]
@@ -346,12 +355,14 @@
         sum_kernel,
         out_shape=jax.ShapeDtypeStruct(shape, jnp.float32),
         in_specs=[
-            pl.BlockSpec(memory_space=pltpu.VMEM),
+            pl.BlockSpec(memory_space=pl.ANY),
             pl.BlockSpec(memory_space=pltpu.SMEM),
         ],
         out_specs=pl.BlockSpec(memory_space=pltpu.VMEM),
         scratch_shapes=[
+            pltpu.VMEM(shape, jnp.float32),
             pltpu.VMEM((slabs - 1,) + shape, jnp.float32),
+            pltpu.SemaphoreType.DMA,
             pltpu.SemaphoreType.DMA((slabs - 1,)),
             pltpu.SemaphoreType.DMA((slabs - 1,)),
         ],

time: 231 us -> 211 us (0.913); the launches traced: 227 us -> 210 us
  Pallas kernels: 93.9 us -> 61 us
  waiting for transfers between devices: 60 us -> 88.4 us
  starting transfers between devices: 49.6 us -> 35.2 us
  local copies, waits for them, and re-layouts: 12.1 us -> 15.6 us
    ppermute x3 -> x2, waiting for transfers between devices: 16 us -> 43.8 us  [on_device(): above = lax.ppermute(lower, 'patch', down_pairs)]
    pallas_call x3 -> x2, Pallas kernels: 30.7 us -> 13.4 us  [warp_rows(): pl.pallas_call(functools.partial(warp_kernel, first), out_shape=(shape, s...]
    pallas_call x3 -> x2, Pallas kernels: 38.8 us -> 26.2 us  [match_rows(): pl.pallas_call(body, out_shape=(jax.ShapeDtypeStruct((visits, patch_rows,...]
    all_to_all x3 -> x2, starting transfers between devices: 25.1 us -> 19.7 us  [on_device(): lax.all_to_all(block, 'patch', split_axis=0, concat_axis=0, tiled=True)]
    ppermute x3 -> x2, starting transfers between devices: 8.89 us -> 3.98 us  [on_device(): above = lax.ppermute(lower, 'patch', down_pairs)]
    unnamed x25 -> x31, local copies, waits for them, and re-layouts: 3.25 us -> 7.97 us
    ppermute x3 -> x2, starting transfers between devices: 15.5 us -> 11.5 us  [on_device(): below = lax.ppermute(upper, 'patch', up_pairs)]
    all_to_all x3 -> x2, waiting for transfers between devices: 39.4 us -> 42.8 us  [on_device(): lax.all_to_all(block, 'patch', split_axis=0, concat_axis=0, tiled=True)]
  transfers between devices with their start and end apart: 9 -> 6, of which waited for: 8 -> 4; matrix products, arithmetic and copies ran while one was open for 7% -> 6% of each run, Pallas kernels for 29% -> 13%
where the time goes in v4:
time: 211 us; the launch traced here: 210 us
  waiting for transfers between devices  88.4 us (42%)
  Pallas kernels  61 us (29%)
  starting transfers between devices  35.2 us (17%)
  local copies, waits for them, and re-layouts  15.6 us (7%)
  other arithmetic  4.78 us (2%)
  between operations  3.58 us (2%)
    ppermute x2, waiting for transfers between devices, on_device(): above = lax.ppermute(lower, 'patch', down_pairs)  43.8 us
    all_to_all x2, waiting for transfers between devices, on_device(): lax.all_to_all(block, 'patch', split_axis=0, concat_axis=0, tiled=True)  42.8 us
    pallas_call x2, Pallas kernels, match_rows(): pl.pallas_call(body, out_shape=(jax.ShapeDtypeStruct((visits, patch_rows,...  26.2 us
    all_to_all x2, starting transfers between devices, on_device(): lax.all_to_all(block, 'patch', split_axis=0, concat_axis=0, tiled=True)  19.7 us
    pallas_call x2, Pallas kernels, warp_rows(): pl.pallas_call(functools.partial(warp_kernel, first), out_shape=(shape, s...  13.4 us
    ppermute x2, starting transfers between devices, on_device(): below = lax.ppermute(upper, 'patch', up_pairs)  11.5 us
    pallas_call x2, Pallas kernels, pack_rows(): pl.pallas_call(functools.partial(pack_kernel, first), out_shape=jax.Shape...  11.1 us
    pallas_call x1, Pallas kernels, sum_visits(): pl.pallas_call(sum_kernel, out_shape=jax.ShapeDtypeStruct(shape, jnp.floa...  10.3 us
  transfers between devices with their start and end apart: 6, of which 4 were waited for; matrix products, arithmetic and copies ran while one was open for 6% of the time, Pallas kernels for 13%

profile of v4, /device:TPU:8, one launch (start us, length us, event | category | flops | bytes accessed | tf_op | source)
XLA Modules:
  0.0 209.7 jit_solution(5532097546885123206)
XLA Ops:
  0.6 6.5 %pack_rows.3 = f32[32,5,64,128]{3,2,1,0:T(8,128)} custom-call(s32[8,32]{1,0:T(8,128)} %places_ref.3, f32[8,1024,128]{2,1,0:T(8,128)} %bitcast.84), custom_call_target="tpu_custom_call" | custom-call | bytes 15728640 | tf_op jit(solution)/shard_map/pack_rows/pallas_call | solution.py:39
  7.1 8.6 %all-to-all-start = ((f32[32,5,64,128]{3,2,1,0:T(8,128)}), f32[32,5,64,128]{3,2,1,0:T(8,128)}, u32[]{:S(2)}, u32[]{:S(2)}) async-start(f32[32,5,64,128]{3,2,1,0:T(8,128)} %pack_rows.3), calls=%async_computation | async-start | bytes 10485760 | tf_op jit(solution)/shard_map/all_to_all | solution.py:451
  15.7 1.2 slice.171
  19.6 4.6 %pack_rows.2 = f32[32,3,64,128]{3,2,1,0:T(8,128)} custom-call(s32[8,32]{1,0:T(8,128)} %places_ref.3, f32[8,1024,128]{2,1,0:T(8,128)} %bitcast.85), custom_call_target="tpu_custom_call" | custom-call | bytes 9437184 | tf_op jit(solution)/shard_map/pack_rows/pallas_call | solution.py:39
  24.2 0.5 slice_reduce_fusion.41
  24.8 0.1 broadcast_in_dim.752
  24.9 0.1 broadcast_in_dim.757
  25.0 0.1 broadcast_in_dim.758
  25.1 0.1 broadcast_in_dim.764
  25.3 0.1 broadcast_in_dim.770
  25.4 0.1 broadcast_in_dim.776
  25.6 0.1 broadcast_in_dim.782
  25.7 0.1 broadcast_in_dim.788
  25.9 0.1 broadcast_in_dim.794
  26.0 0.1 broadcast_in_dim.800
  26.2 0.1 broadcast_in_dim.806
  26.3 0.1 broadcast_in_dim.812
  26.5 0.1 broadcast_in_dim.818
  26.6 0.1 broadcast_in_dim.824
  26.8 0.1 broadcast_in_dim.830
  26.9 0.1 broadcast_in_dim.836
  27.1 0.1 broadcast_in_dim.842
  27.2 0.1 broadcast_in_dim.848
  27.4 0.1 broadcast_in_dim.854
  27.5 0.1 broadcast_in_dim.860
  27.6 0.2 slice_reduce_fusion.22
  27.8 0.1 broadcast_in_dim.865
  27.9 0.1 broadcast_in_dim.866
  28.1 0.1 broadcast_in_dim.872
  28.2 0.1 reshape.1003
  28.3 0.3 pad.20.shift_ref
  28.7 0.1 dynamic_slice.3.refs_0_.weight_ref
  28.7 1.3 pad.19.taps_ref
  30.1 0.1 pad_add_fusion
  30.2 0.9 reduce-precision_convert_fusion.1
  31.2 0.2 slice_reduce_fusion.1
  31.4 0.5 slice_reduce_fusion.20
  31.9 0.1 pad_maximum_fusion.refs_5_.down_ref
  32.1 0.3 fusion.29
  32.3 1.5 fusion.4
  33.9 1.2 fusion.1.refs_6_.across_ref
  35.1 1.1 convolution_bitcast_fusion.refs_7_.coef_ref
  36.2 42.8 %all-to-all-done.got_ref = f32[32,5,64,128]{3,2,1,0:T(8,128)} async-done(((f32[32,5,64,128]{3,2,1,0:T(8,128)}), f32[32,5,64,128]{3,2,1,0:T(8,128)}, u32[]{:S(2)}, u32[]{:S(2)}) %all-to-all-start) | async-done | bytes 5242912 | tf_op jit(solution)/shard_map/all_to_all | solution.py:451
  79.0 11.1 %all-to-all-start.1 = ((f32[32,3,64,128]{3,2,1,0:T(8,128)}), f32[32,3,64,128]{3,2,1,0:T(8,128)}, u32[]{:S(2)}, u32[]{:S(2)}) async-start(f32[32,3,64,128]{3,2,1,0:T(8,128)} %pack_rows.2), calls=%async_computation.1 | async-start | bytes 6291456 | tf_op jit(solution)/shard_map/all_to_all | solution.py:451
  90.2 1.2 copy-done.2
  91.4 7.7 %warp_rows.2 = (f32[5,16,4224]{2,1,0:T(8,128)S(1)}, f32[5,16,4224]{2,1,0:T(8,128)S(1)}) custom-call(s32[1]{0:T(128)} %bitcast.32.turn_ref, f32[32,5,64,128]{3,2,1,0:T(8,128)} %all-to-all-done.got_ref, f32[8,8,4224]{2,1,0:T(8,128)S(1)} %copy-done.2, s32[8,1,4224]{2,1,0:T(1,128)S(1)} %pad.20.shift_ref), custom_call_target="tpu_custom_call" | custom-call | bytes 62914560 | tf_op jit(solution)/shard_map/warp_rows/pallas_call | solution.py:139
  99.1 2.1 collective-permute-start
  101.1 5.8 %collective-permute-start.1 = (f32[5,16,4224]{2,1,0:T(8,128)S(1)}, f32[5,16,4224]{2,1,0:T(8,128)S(1)}, u32[]{:S(2)}, u32[]{:S(2)}) collective-permute-start(f32[5,16,4224]{2,1,0:T(8,128)S(1)} %get-tuple-element.24.refs_1_), channel_id=1, source_target_pairs={{4,0},{8,4},{12,8},{16,12},{20,16},{24,20},{28,24},{32,28},{36,32}... | collective-permute-start | bytes 4055048 | tf_op jit(solution)/shard_map/ppermute | solution.py:460
  106.9 36.1 %collective-permute-done.refs_3_ = f32[5,16,4224]{2,1,0:T(8,128)S(1)} collective-permute-done((f32[5,16,4224]{2,1,0:T(8,128)S(1)}, f32[5,16,4224]{2,1,0:T(8,128)S(1)}, u32[]{:S(2)}, u32[]{:S(2)}) %collective-permute-start) | collective-permute-done | bytes 1351712 | tf_op jit(solution)/shard_map/ppermute | solution.py:459
  143.0 15.7 %match_rows.2 = (f32[8,32,4096]{2,1,0:T(8,128)}, f32[32,4096]{1,0:T(8,128)S(1)}) custom-call(f32[8]{0:T(128)S(1)} %dynamic_slice.3.refs_0_.weight_ref, f32[5,16,4224]{2,1,0:T(8,128)S(1)} %get-tuple-element.24.refs_1_, f32[5,16,4224]{2,1,0:T(8,128)S(1)} %get-tuple-element.25.refs_2_, f32[5,16,4224]{2,1,0:T(8,128)S(1)} %collective-permute-done.refs_3_, ...), custom_call_target="tpu_custom_call" | custom-call | bytes 104857600 | tf_op jit(solution)/shard_map/match_rows/pallas_call | solution.py:281
  158.7 0.8 copy-done.5
  159.5 1.2 copy-done.3
  160.7 5.8 %warp_rows.3 = (f32[3,16,4224]{2,1,0:T(8,128)}, f32[3,16,4224]{2,1,0:T(8,128)}) custom-call(s32[1]{0:T(128)} %bitcast.32.turn_ref, f32[32,3,64,128]{3,2,1,0:T(8,128)} %all-to-all-done.1.got_ref, f32[8,8,4224]{2,1,0:T(8,128)S(1)} %copy-done.3, s32[8,1,4224]{2,1,0:T(1,128)S(1)} %pad.20.shift_ref), custom_call_target="tpu_custom_call" | custom-call | bytes 37748736 | tf_op jit(solution)/shard_map/warp_rows/pallas_call | solution.py:139
  166.5 1.9 collective-permute-start.2
  168.4 5.8 %collective-permute-start.3 = (f32[3,16,4224]{2,1,0:T(8,128)}, f32[3,16,4224]{2,1,0:T(8,128)}, u32[]{:S(2)}, u32[]{:S(2)}) collective-permute-start(f32[3,16,4224]{2,1,0:T(8,128)} %get-tuple-element.32.upper_ref), channel_id=1, source_target_pairs={{4,0},{8,4},{12,8},{16,12},{20,16},{24,20},{28,24},{32,28},{36,32}... | collective-permute-start | bytes 2433032 | tf_op jit(solution)/shard_map/ppermute | solution.py:460
  174.2 0.6 reduce_sum.9
  174.8 7.7 %collective-permute-done.2.above_ref = f32[3,16,4224]{2,1,0:T(8,128)} collective-permute-done((f32[3,16,4224]{2,1,0:T(8,128)}, f32[3,16,4224]{2,1,0:T(8,128)}, u32[]{:S(2)}, u32[]{:S(2)}) %collective-permute-start.2) | collective-permute-done | bytes 811040 | tf_op jit(solution)/shard_map/ppermute | solution.py:459
  182.5 1.8 collective-permute-done.3.below_ref
  184.2 1.3 copy-done.1
  185.5 1.0 copy-done.6
  186.5 10.5 %match_rows.3 = (f32[8,32,4096]{2,1,0:T(8,128)}, f32[32,4096]{1,0:T(8,128)S(1)}) custom-call(f32[8]{0:T(128)S(1)} %dynamic_slice.3.refs_0_.weight_ref, f32[3,16,4224]{2,1,0:T(8,128)} %get-tuple-element.32.upper_ref, f32[3,16,4224]{2,1,0:T(8,128)} %get-tuple-element.33.lower_ref, ...), custom_call_target="tpu_custom_call", output_to_operand_aliasing={{0}: (10, {})} | custom-call | bytes 62914560 | tf_op jit(solution)/shard_map/match_rows/pallas_call | solution.py:281
  197.1 0.8 copy-done.7
  197.9 10.3 %sum_visits.1 = f32[8,4096]{1,0:T(8,128)} custom-call(f32[32,4096]{1,0:T(8,128)} %copy-done.7, f32[1]{0:T(128)} %bitcast.35.scale_ref), custom_call_target="tpu_custom_call" | custom-call | tf_op jit(solution)/shard_map/sum_visits/pallas_call | solution.py:354
  208.1 1.6 copy.22
  (53 shorter events, 1.5 us)
Async XLA Ops:
  7.1 71.9 %all-to-all-start = ((f32[32,5,64,128]{3,2,1,0:T(8,128)}), f32[32,5,64,128]{3,2,1,0:T(8,128)}, u32[]{:S(2)}, u32[]{:S(2)}) async-start(f32[32,5,64,128]{3,2,1,0:T(8,128)} %pack_rows.3), calls=%async_computation | async-start | bytes 10485760 | tf_op jit(solution)/shard_map/all_to_all | solution.py:451
  19.6 4.7 %copy-start.8 = (f32[9,21]{1,0:T(8,128)S(1)}, f32[9,21]{1,0:T(8,128)}, u32[]{:S(2)}) copy-start(f32[9,21]{1,0:T(8,128)} %param.14) | copy-start | bytes 2272
  19.6 8.6 %copy-start.13 = (s32[1,4096]{1,0:T(1,128)S(1)}, s32[1,4096]{1,0:T(1,128)}, u32[]{:S(2)}) copy-start(s32[1,4096]{1,0:T(1,128)} %param.17) | copy-start | bytes 49156
  19.6 8.7 %copy-start.11 = (s32[8,1,4096]{2,1,0:T(1,128)S(1)}, s32[8,1,4096]{2,1,0:T(1,128)}, u32[]{:S(2)}) copy-start(s32[8,1,4096]{2,1,0:T(1,128)} %param.13) | copy-start | bytes 393220
  19.6 9.0 %copy-start.14 = (f32[32]{0:T(128)S(1)}, f32[32]{0:T(128)}, u32[]{:S(2)}) copy-start(f32[32]{0:T(128)} %param.19) | copy-start | bytes 388
  19.6 9.1 %copy-start.10 = (f32[8,1,8,4096]{3,2,1,0:T(8,128)S(1)}, f32[8,1,8,4096]{3,2,1,0:T(8,128)}, u32[]{:S(2)}) copy-start(f32[8,1,8,4096]{3,2,1,0:T(8,128)} %param.12) | copy-start | bytes 3145732
  24.2 6.9 %copy-start.9 = (f32[9,21]{1,0:T(8,128)S(1)}, f32[9,21]{1,0:T(8,128)}, u32[]{:S(2)}) copy-start(f32[9,21]{1,0:T(8,128)} %param.15) | copy-start | bytes 2272
  31.9 3.1 %copy-start.12 = (f32[8,1,9,32]{3,1,2,0:T(1,128)S(1)}, f32[8,1,9,32]{3,1,2,0:T(1,128)}, u32[]{:S(2)}) copy-start(f32[8,1,9,32]{3,1,2,0:T(1,128)} %param.16) | copy-start | bytes 27652
  79.0 80.4 %all-to-all-start.1 = ((f32[32,3,64,128]{3,2,1,0:T(8,128)}), f32[32,3,64,128]{3,2,1,0:T(8,128)}, u32[]{:S(2)}, u32[]{:S(2)}) async-start(f32[32,3,64,128]{3,2,1,0:T(8,128)} %pack_rows.2), calls=%async_computation.1 | async-start | bytes 6291456 | tf_op jit(solution)/shard_map/all_to_all | solution.py:451
  90.1 1.2 copy-start.2
  91.4 51.6 %copy-start = (bf16[9,256,256]{2,1,0:T(8,128)(2,1)S(1)}, bf16[9,256,256]{2,1,0:T(8,128)(2,1)}, u32[]{:S(2)}) copy-start(bf16[9,256,256]{2,1,0:T(8,128)(2,1)} %fusion.1.refs_6_.across_ref) | copy-start | bytes 3538948
  91.4 51.6 %copy-start.4 = (f32[32,4096]{1,0:T(8,128)S(1)}, f32[32,4096]{1,0:T(8,128)}, u32[]{:S(2)}) copy-start(f32[32,4096]{1,0:T(8,128)} %template_ref.1) | copy-start | bytes 1572868
  99.1 43.9 %collective-permute-start = (f32[5,16,4224]{2,1,0:T(8,128)S(1)}, f32[5,16,4224]{2,1,0:T(8,128)S(1)}, u32[]{:S(2)}, u32[]{:S(2)}) collective-permute-start(f32[5,16,4224]{2,1,0:T(8,128)S(1)} %get-tuple-element.25.refs_2_), channel_id=1, source_target_pairs={{0,4},{4,8},{8,12},{12,16},{16,20},{20,24},{24,28},{28,32},{32,36}... | collective-permute-start | bytes 4055048 | tf_op jit(solution)/shard_map/ppermute | solution.py:459
  101.1 41.9 %collective-permute-start.1 = (f32[5,16,4224]{2,1,0:T(8,128)S(1)}, f32[5,16,4224]{2,1,0:T(8,128)S(1)}, u32[]{:S(2)}, u32[]{:S(2)}) collective-permute-start(f32[5,16,4224]{2,1,0:T(8,128)S(1)} %get-tuple-element.24.refs_1_), channel_id=1, source_target_pairs={{4,0},{8,4},{12,8},{16,12},{20,16},{24,20},{28,24},{32,28},{36,32}... | collective-permute-start | bytes 4055048 | tf_op jit(solution)/shard_map/ppermute | solution.py:460
  158.7 0.8 copy-start.5
  159.5 1.2 copy-start.3
  166.5 16.0 %collective-permute-start.2 = (f32[3,16,4224]{2,1,0:T(8,128)}, f32[3,16,4224]{2,1,0:T(8,128)}, u32[]{:S(2)}, u32[]{:S(2)}) collective-permute-start(f32[3,16,4224]{2,1,0:T(8,128)} %get-tuple-element.33.lower_ref), channel_id=1, source_target_pairs={{0,4},{4,8},{8,12},{12,16},{16,20},{20,24},{24,28},{28,32},{32,36}... | collective-permute-start | bytes 2433032 | tf_op jit(solution)/shard_map/ppermute | solution.py:459
  168.4 15.8 %collective-permute-start.3 = (f32[3,16,4224]{2,1,0:T(8,128)}, f32[3,16,4224]{2,1,0:T(8,128)}, u32[]{:S(2)}, u32[]{:S(2)}) collective-permute-start(f32[3,16,4224]{2,1,0:T(8,128)} %get-tuple-element.32.upper_ref), channel_id=1, source_target_pairs={{4,0},{8,4},{12,8},{16,12},{20,16},{24,20},{28,24},{32,28},{36,32}... | collective-permute-start | bytes 2433032 | tf_op jit(solution)/shard_map/ppermute | solution.py:460
  184.2 1.3 copy-start.1
  185.5 1.0 copy-start.6
  197.1 0.8 copy-start.7

commit v5 on v4

--- a/solution.py
+++ b/solution.py
@@ -12,7 +12,7 @@
 step = 108
 parts = 2
 room = 24 << 20
-chunks = (5, 3)
+chunks = (4, 4)
 bf16 = jnp.bfloat16
 
 
@@ -29,7 +29,7 @@
         sent_ref[place // patch_rows, 0, pl.ds(at, tiles), :] = cells
         return carry
 
-    lax.fori_loop(0, patch_rows, step, 0, unroll=4)
+    lax.fori_loop(0, patch_rows, step, 0, unroll=True)
 
 
 def pack_rows(first, count, tract_row, tiled_rows, patches):
@@ -51,6 +51,10 @@
     )(tract_row, tiled_rows)
 
 
+def folded(tiles):
+    return -(-tiles // 4)
+
+
 def split(values):
     high = values.astype(bf16)
     low = (values - high.astype(jnp.float32)).astype(bf16)
@@ -58,29 +62,27 @@
 
 
 def warp_kernel(
-    first, turn_ref, got_ref, taps_ref, shift_ref, upper_ref, lower_ref, rows, image, sems
+    first, turn_ref, got_ref, taps_ref, shift_ref, warped_ref, head_ref, tail_ref, rows, image, sems
 ):
-    patches, count, depth = got_ref.shape[:3]
+    patches, _, depth = got_ref.shape[:3]
     tiles = depth // 2
-    half_rows = upper_ref.shape[1]
-    patch_rows = 2 * half_rows
+    patch_rows = warped_ref.shape[1]
     groups = patch_rows // 8
     visit = pl.program_id(0)
 
     @pl.when(visit == 0)
     def _():
-        def fetch(item, carry):
-            local = item // (patch_rows // 2)
-            pair = item % (patch_rows // 2)
-            source = (turn_ref[0] + first + local - pair + 2 * patches) % patches
-            pltpu.make_async_copy(
-                got_ref.at[source, local],
-                rows.at[local, pl.ds(pl.multiple_of(pair * depth, depth), depth), :],
-                sems.at[local],
-            ).start()
+        def fetch(local, carry):
+            for pair in range(patch_rows // 2):
+                source = (turn_ref[0] + first + local - pair + 2 * patches) % patches
+                pltpu.make_async_copy(
+                    got_ref.at[source, first + local],
+                    rows.at[local, pl.ds(pair * depth, depth), :],
+                    sems.at[local],
+                ).start()
             return carry
 
-        lax.fori_loop(0, count * patch_rows // 2, fetch, 0)
+        lax.fori_loop(0, pl.num_programs(0), fetch, 0)
         blank = jnp.zeros((2 * patch_rows, lane), bf16)
         image[:, :lane] = blank
         image[:, (tiles + 1) * lane :] = blank
@@ -103,8 +105,11 @@
     columns = lax.broadcasted_iota(jnp.int32, (8, lane), 1) + half_lane
     sublanes = lax.broadcasted_iota(jnp.int32, (8, lane), 0)
 
-    def tile_step(u, carry):
-        window = pl.ds(pl.multiple_of(u * lane, lane), lane)
+    fold = folded(tiles + 1)
+    for ref in (head_ref, tail_ref):
+        ref[0, :, (tiles + 1) * lane :] = jnp.zeros((8, fold * lane), jnp.float32)
+    for u in range(tiles + 1):
+        window = slice(u * lane, (u + 1) * lane)
         spot = columns + jnp.broadcast_to(shift_ref[0, :, window], (8, lane))
         taps = taps_ref[0, :, window]
         turned = jnp.take_along_axis(
@@ -121,24 +126,26 @@
             ],
             axis=1,
         )
-        both = pl.ds(pl.multiple_of(u * lane, lane), 2 * lane)
+        both = slice(u * lane, (u + 2) * lane)
         out = jnp.dot(image[:, both], matrix, preferred_element_type=jnp.float32)
         cells = out[:patch_rows, :lane] + out[:patch_rows, lane:] + out[patch_rows:, :lane]
-        upper_ref[0, :, window] = cells[:half_rows]
-        lower_ref[0, :, window] = cells[half_rows:]
-        return carry
-
-    lax.fori_loop(0, tiles + 1, tile_step, 0, unroll=33)
-
-
-def warp_rows(first, turn, got, taps, shift, patch_rows):
-    patches, count, depth = got.shape[:3]
+        warped_ref[0, :, window] = cells
+        at = 2 * (u // fold)
+        spare = slice((tiles + 1 + u % fold) * lane, (tiles + 2 + u % fold) * lane)
+        head_ref[0, :, window] = cells[:8]
+        head_ref[0, at : at + 2, spare] = cells[8:10]
+        tail_ref[0, :, window] = cells[patch_rows - 8 :]
+        tail_ref[0, at : at + 2, spare] = cells[patch_rows - 10 : patch_rows - 8]
+
+
+def warp_rows(first, count, turn, got, taps, shift, patch_rows):
+    depth = got.shape[2]
     width = (depth // 2 + 1) * lane
-    half_rows = patch_rows // 2
-    shape = jax.ShapeDtypeStruct((count, half_rows, width), jnp.float32)
+    span = width + folded(width // lane) * lane
+    edge = jax.ShapeDtypeStruct((count, 8, span), jnp.float32)
     return pl.pallas_call(
         functools.partial(warp_kernel, first),
-        out_shape=(shape, shape),
+        out_shape=(jax.ShapeDtypeStruct((count, patch_rows, width), jnp.float32), edge, edge),
         grid=(count,),
         in_specs=[
             pl.BlockSpec(memory_space=pltpu.SMEM),
@@ -146,7 +153,10 @@
             pl.BlockSpec((1,) + taps.shape[1:], lambda q: (q + first, 0, 0)),
             pl.BlockSpec((1,) + shift.shape[1:], lambda q: (q + first, 0, 0)),
         ],
-        out_specs=[pl.BlockSpec((1, half_rows, width), lambda q: (q, 0, 0))] * 2,
+        out_specs=[
+            pl.BlockSpec((1, patch_rows, width), lambda q: (q, 0, 0)),
+            *[pl.BlockSpec((1, 8, span), lambda q: (q, 0, 0))] * 2,
+        ],
         scratch_shapes=[
             pltpu.VMEM((count, patch_rows // 2 * depth, lane), jnp.float32),
             pltpu.VMEM((2 * patch_rows, width + lane), bf16),
@@ -162,8 +172,7 @@
     first,
     fresh,
     weight_ref,
-    upper_ref,
-    lower_ref,
+    warped_ref,
     above_ref,
     below_ref,
     down_ref,
@@ -183,9 +192,20 @@
     bases = across_ref.shape[0]
     windows = pieces.shape[1] // lane
     part = high_refs.shape[2] // lane
-    blocks = (upper_ref, lower_ref, above_ref, below_ref)
-    half_rows = upper_ref.shape[1]
-    inside = lax.broadcasted_iota(jnp.int32, (half_rows, lane), 1)
+    tiles = warped_ref.shape[2] // lane
+    fold = folded(tiles)
+    inside = lax.broadcasted_iota(jnp.int32, (16, lane), 1)
+    quarter = lax.broadcasted_iota(jnp.int32, (16, lane), 0) % 8 // 2
+
+    def columns(tile):
+        own = warped_ref[0, :, tile * lane : (tile + 1) * lane]
+        edges = []
+        for at in (tile, tiles + tile % fold):
+            here = slice(at * lane, (at + 1) * lane)
+            edges.append(jnp.concatenate([above_ref[0, :, here], below_ref[0, :, here]], axis=0))
+        edges[1] = jnp.where(quarter == tile // fold, edges[1], 0.0)
+        return [own[:16], own[16:], *edges]
+
 
     @pl.when(pl.program_id(0) == 0)
     def _():
@@ -195,19 +215,21 @@
         start = step * w + half_lane - (lane - step) // 2
         tile, turn = start // lane, start % lane
         here = slice(w * lane, (w + 1) * lane)
-        for i, ref in enumerate(blocks):
-            values = ref[0, :, tile * lane : (tile + 1) * lane]
-            if turn:
-                after = ref[0, :, (tile + 1) * lane : (tile + 2) * lane]
-                values = jnp.where(
+        blocks = columns(tile)
+        if turn:
+            blocks = [
+                jnp.where(
                     inside < lane - turn,
-                    pltpu.roll(values, lane - turn, 1),
+                    pltpu.roll(before, lane - turn, 1),
                     pltpu.roll(after, lane - turn, 1),
                 )
+                for before, after in zip(blocks, columns(tile + 1))
+            ]
+        for i, values in enumerate(blocks):
             high, low = split(values)
             for j, value in enumerate((high, low, high)):
-                at = (j * len(blocks) + i) * half_rows
-                pieces[at : at + half_rows, here] = value
+                at = (j * len(blocks) + i) * 16
+                pieces[at : at + 16, here] = value
 
     def part_step(p):
         for w in range(p * part, (p + 1) * part):
@@ -257,9 +279,10 @@
 
 
 def match_rows(
-    first, weights, upper, lower, above, below, down, across, coefs, template, before, difference
+    first, weights, warped, above, below, down, across, coefs, template, before, difference
 ):
-    count, half_rows, width = upper.shape
+    count, _, width = warped.shape
+    edge = above.shape[2]
     visits, bases, span = coefs.shape
     patch_rows, row_width = template.shape
     part = span // lane // parts
@@ -268,12 +291,12 @@
         before = template
     extra, aliases = [], {}
     if difference is not None:
-        extra, aliases = [difference], {10: 0}
+        extra, aliases = [difference], {9: 0}
     kernel = functools.partial(match_kernel, first, fresh)
     if difference is None:
 
         def body(*refs):
-            kernel(*refs[:10], None, *refs[10:])
+            kernel(*refs[:9], None, *refs[9:])
 
     else:
         body = kernel
@@ -287,7 +310,8 @@
         grid=(count,),
         in_specs=[
             pl.BlockSpec(memory_space=pltpu.SMEM),
-            *[pl.BlockSpec((1, half_rows, width), lambda q: (q, 0, 0))] * 4,
+            pl.BlockSpec((1, patch_rows, width), lambda q: (q, 0, 0)),
+            *[pl.BlockSpec((1, 8, edge), lambda q: (q, 0, 0))] * 2,
             pl.BlockSpec(down.shape, lambda q: (0, 0)),
             pl.BlockSpec(across.shape, lambda q: (0, 0, 0)),
             pl.BlockSpec((1, bases, span), lambda q: (q + first, 0, 0)),
@@ -309,7 +333,7 @@
         compiler_params=pltpu.CompilerParams(vmem_limit_bytes=room),
         cost_estimate=pl.CostEstimate(flops=0, bytes_accessed=20 * count << 20, transcendentals=0),
         name="match_rows",
-    )(weights, upper, lower, above, below, down, across, coefs, template, before, *extra)
+    )(weights, warped, above, below, down, across, coefs, template, before, *extra)
 
 
 def sum_kernel(total_ref, scale_ref, out_ref, own, slots, own_sem, send_sems, recv_sems):
@@ -418,8 +442,9 @@
     )
 
     rows = jnp.arange(patch_rows)
+    pair = jnp.arange(8)
     inner = jnp.concatenate(
-        [rows, jnp.arange(patch_rows // 2) - patch_rows // 2, jnp.arange(patch_rows // 2) + patch_rows]
+        [rows, pair - 8, pair + patch_rows, pair % 2 - half, pair % 2 + patch_rows + half - 2]
     )
     down = taken(basis_rows, inner[None, :] - rows[:, None] + half).reshape(-1, inner.shape[0])
     down_high, down_low = split_table(down)
@@ -441,25 +466,22 @@
     )
 
     starts = [sum(chunks[:i]) for i in range(len(chunks))]
-    sent = [
-        pack_rows(first, count, tract_row, tiled_rows, patches)
-        for first, count in zip(starts, chunks)
-    ]
-    sent[1:], down, across, coefs, taps, shift, weights, turn = lax.optimization_barrier(
-        (sent[1:], down, across, coefs, taps, shift, weights, turn)
-    )
-    got = [lax.all_to_all(block, "patch", split_axis=0, concat_axis=0, tiled=True) for block in sent]
-    total, difference = None, None
+    sent = pack_rows(0, visits, tract_row, tiled_rows, patches)
+    got = lax.all_to_all(sent, "patch", split_axis=0, concat_axis=0, tiled=True)
     down_pairs = [(i, i + 1) for i in range(patches - 1)]
     up_pairs = [(i + 1, i) for i in range(patches - 1)]
-    for first, block in zip(starts, got):
-        if total is not None:
-            turn, total = lax.optimization_barrier((turn, total))
-        upper, lower = warp_rows(first, turn, block, taps, shift, patch_rows)
-        above = lax.ppermute(lower, "patch", down_pairs)
-        below = lax.ppermute(upper, "patch", up_pairs)
+    fields = []
+    for first, count in zip(starts, chunks):
+        warped, head, tail = warp_rows(first, count, turn, got, taps, shift, patch_rows)
+        if fields:
+            head, tail, fields[-1] = lax.optimization_barrier((head, tail, fields[-1]))
+        above = lax.ppermute(tail, "patch", down_pairs)
+        below = lax.ppermute(head, "patch", up_pairs)
+        fields.append((warped, above, below))
+    total, difference = None, None
+    for first, field in zip(starts, fields):
         difference, total = match_rows(
-            first, weights, upper, lower, above, below, down, across, coefs, template, total, difference
+            first, weights, *field, down, across, coefs, template, total, difference
         )
     coadd = sum_visits(total, jnp.sum(visit_weight).reshape(1))
     return difference, coadd

time: 211 us -> 218 us (1.033)
  the two profiles are of different devices: /device:TPU:8 before, /device:TPU:1 now
where the time goes in v5:
time: 218 us; the launch traced here: 217 us
  waiting for transfers between devices  98.7 us (45%)
  Pallas kernels  59.7 us (27%)
  starting transfers between devices  36.2 us (17%)
  local copies, waits for them, and re-layouts  10.5 us (5%)
  other arithmetic  6.94 us (3%)
  between operations  3.61 us (2%)
    all_to_all x1, waiting for transfers between devices, on_device(): got = lax.all_to_all(sent, 'patch', split_axis=0, concat_axis=0, tiled=True)  98.2 us
    pallas_call x2, Pallas kernels, match_rows(): pl.pallas_call(body, out_shape=(jax.ShapeDtypeStruct((visits, patch_rows,...  26.6 us
    ppermute x2, starting transfers between devices, on_device(): above = lax.ppermute(tail, 'patch', down_pairs)  22.4 us
    pallas_call x2, Pallas kernels, warp_rows(): pl.pallas_call(functools.partial(warp_kernel, first), out_shape=(jax.Shap...  14 us
    pallas_call x1, Pallas kernels, sum_visits(): pl.pallas_call(sum_kernel, out_shape=jax.ShapeDtypeStruct(shape, jnp.floa...  11.1 us
    all_to_all x1, starting transfers between devices, on_device(): got = lax.all_to_all(sent, 'patch', split_axis=0, concat_axis=0, tiled=True)  9.8 us
    pallas_call x1, Pallas kernels, pack_rows(): pl.pallas_call(functools.partial(pack_kernel, first), out_shape=jax.Shape...  8.02 us
    convert_element_type x4, other arithmetic, split_table(): return (high.astype(bf16), (values - high).astype(bf16))  4.64 us
  transfers between devices with their start and end apart: 5, of which 2 were waited for; matrix products, arithmetic and copies ran while one was open for 7% of the time, Pallas kernels for 9%

profile of v5, /device:TPU:1, one launch (start us, length us, event | category | flops | bytes accessed | tf_op | source)
XLA Modules:
  0.0 216.8 jit_solution(12539488692251840864)
XLA Ops:
  0.6 8.0 %pack_rows.1 = f32[32,8,64,128]{3,2,1,0:T(8,128)} custom-call(s32[8,32]{1,0:T(8,128)} %places_ref.1, f32[8,1024,128]{2,1,0:T(8,128)} %bitcast.84), custom_call_target="tpu_custom_call" | custom-call | bytes 25165824 | tf_op jit(solution)/shard_map/pack_rows/pallas_call | solution.py:39
  8.7 9.8 %all-to-all-start = ((f32[32,8,64,128]{3,2,1,0:T(8,128)}), f32[32,8,64,128]{3,2,1,0:T(8,128)}, u32[]{:S(2)}, u32[]{:S(2)}) async-start(f32[32,8,64,128]{3,2,1,0:T(8,128)} %pack_rows.1), calls=%async_computation | async-start | bytes 16777216 | tf_op jit(solution)/shard_map/all_to_all | solution.py:470
  18.5 1.2 slice.129
  22.3 0.3 pad.18.shift_ref
  22.7 0.5 slice_reduce_fusion.41
  23.2 0.1 broadcast_in_dim.751
  23.3 0.1 broadcast_in_dim.752
  23.4 0.1 broadcast_in_dim.758
  23.5 0.1 broadcast_in_dim.763
  23.6 0.1 broadcast_in_dim.764
  23.7 0.1 broadcast_in_dim.769
  23.7 0.1 broadcast_in_dim.770
  23.9 0.1 broadcast_in_dim.776
  24.0 0.1 broadcast_in_dim.781
  24.0 0.1 broadcast_in_dim.782
  24.2 0.1 broadcast_in_dim.788
  24.3 0.1 broadcast_in_dim.793
  24.3 0.1 broadcast_in_dim.794
  24.4 0.1 broadcast_in_dim.799
  24.5 0.1 broadcast_in_dim.800
  24.6 0.1 broadcast_in_dim.806
  24.7 0.1 broadcast_in_dim.811
  24.8 0.1 broadcast_in_dim.812
  24.9 0.1 broadcast_in_dim.817
  24.9 0.1 broadcast_in_dim.818
  25.1 0.1 broadcast_in_dim.824
  25.3 0.1 broadcast_in_dim.830
  25.4 0.1 broadcast_in_dim.836
  25.6 0.1 broadcast_in_dim.842
  25.7 0.1 broadcast_in_dim.848
  25.9 0.1 broadcast_in_dim.854
  26.0 0.1 broadcast_in_dim.860
  26.1 0.2 slice_reduce_fusion.22
  26.3 0.1 broadcast_in_dim.865
  26.4 0.1 broadcast_in_dim.866
  26.5 0.1 broadcast_in_dim.872
  26.6 0.4 pad.17.taps_ref
  27.0 0.1 concatenate.15
  27.1 0.9 reduce-precision_convert_fusion.1
  28.1 0.2 slice_reduce_fusion.1
  28.3 0.5 slice_reduce_fusion.20
  28.8 98.2 %all-to-all-done.got_ref = f32[32,8,64,128]{3,2,1,0:T(8,128)} async-done(((f32[32,8,64,128]{3,2,1,0:T(8,128)}), f32[32,8,64,128]{3,2,1,0:T(8,128)}, u32[]{:S(2)}, u32[]{:S(2)}) %all-to-all-start) | async-done | bytes 8388640 | tf_op jit(solution)/shard_map/all_to_all | solution.py:470
  127.0 7.0 %warp_rows.3 = (f32[4,32,4224]{2,1,0:T(8,128)S(1)}, f32[4,8,5376]{2,1,0:T(8,128)}, f32[4,8,5376]{2,1,0:T(8,128)}) custom-call(s32[1]{0:T(128)} %bitcast.1.turn_ref, f32[32,8,64,128]{3,2,1,0:T(8,128)} %all-to-all-done.got_ref, f32[8,8,4224]{2,1,0:T(8,128)S(1)} %pad.17.taps_ref, s32[8,1,4224]{2,1,0:T(1,128)S(1)} %pad.18.shift_ref), custom_call_target="tpu_custom_call" | custom-call | bytes 50331648 | tf_op jit(solution)/shard_map/warp_rows/pallas_call | solution.py:146
  134.0 1.3 copy-done.1
  135.4 19.2 %collective-permute-start = (f32[4,8,5376]{2,1,0:T(8,128)}, f32[4,8,5376]{2,1,0:T(8,128)}, u32[]{:S(2)}, u32[]{:S(2)}) collective-permute-start(f32[4,8,5376]{2,1,0:T(8,128)} %get-tuple-element.21), channel_id=1, source_target_pairs={{0,4},{4,8},{8,12},{12,16},{16,20},{20,24},{24,28},{28,32},{32,36}... | collective-permute-start | bytes 2064392 | tf_op jit(solution)/shard_map/ppermute | solution.py:478
  154.6 1.9 collective-permute-start.1
  156.6 0.1 reshape.1004
  156.7 0.1 pad_maximum_fusion.refs_4_.down_ref
  156.8 0.3 fusion.29
  157.1 2.6 %fusion.4 = (bf16[9,128,128]{2,1,0:T(8,128)(2,1)}, f32[9,128,128]{2,1,0:T(8,128)}) fusion(f32[9]{0:T(128)S(1)} %get-tuple-element.52, pred[128,128]{1,0:T(8,128)(4,1)S(1)} %get-tuple-element.79, f32[9]{0:T(128)S(1)} %get-tuple-element.51, pred[128,128]{1,0:T(8,128)(4,1)S(1)} %get-tuple-element.80, f32[9]{0:T(128)S(1)} %get-tuple-element.33, ...), kind=kLoop, calls=%fused_computation.8 | loop fusion | flops 3538944 | bytes 1229556 | tf_op jit(solution)/shard_map/convert_element_type | solution.py:400
  159.6 7.0 %warp_rows.2 = (f32[4,32,4224]{2,1,0:T(8,128)S(1)}, f32[4,8,5376]{2,1,0:T(8,128)}, f32[4,8,5376]{2,1,0:T(8,128)}) custom-call(s32[1]{0:T(128)} %bitcast.1.turn_ref, f32[32,8,64,128]{3,2,1,0:T(8,128)} %all-to-all-done.got_ref, f32[8,8,4224]{2,1,0:T(8,128)S(1)} %pad.17.taps_ref, s32[8,1,4224]{2,1,0:T(1,128)S(1)} %pad.18.shift_ref), custom_call_target="tpu_custom_call" | custom-call | bytes 50331648 | tf_op jit(solution)/shard_map/warp_rows/pallas_call | solution.py:146
  166.7 0.5 collective-permute-done.1.refs_3_
  167.2 3.1 %collective-permute-start.2 = (f32[4,8,5376]{2,1,0:T(8,128)}, f32[4,8,5376]{2,1,0:T(8,128)S(1)}, u32[]{:S(2)}, u32[]{:S(2)}) collective-permute-start(f32[4,8,5376]{2,1,0:T(8,128)} %get-tuple-element.23), channel_id=1, source_target_pairs={{0,4},{4,8},{8,12},{12,16},{16,20},{20,24},{24,28},{28,32},{32,36}... | collective-permute-start | bytes 2064392 | tf_op jit(solution)/shard_map/ppermute | solution.py:478
  170.3 2.1 collective-permute-start.3
  172.5 0.6 reduce_sum.9
  173.1 0.1 dynamic_slice.3.refs_0_.weight_ref
  173.2 1.1 reduce-precision_convert_fusion
  174.3 1.3 fusion.1.refs_5_.across_ref
  175.6 1.1 convolution_bitcast_fusion.refs_6_.coef_ref
  176.7 13.3 %match_rows.2 = (f32[8,32,4096]{2,1,0:T(8,128)}, f32[32,4096]{1,0:T(8,128)S(1)}) custom-call(f32[8]{0:T(128)S(1)} %dynamic_slice.3.refs_0_.weight_ref, f32[4,32,4224]{2,1,0:T(8,128)S(1)} %copy-done.2, f32[4,8,5376]{2,1,0:T(8,128)} %collective-permute-done.refs_2_, f32[4,8,5376]{2,1,0:T(8,128)} %collective-permute-done.1.refs_3_, ...), custom_call_target="tpu_custom_call" | custom-call | bytes 83886080 | tf_op jit(solution)/shard_map/match_rows/pallas_call | solution.py:304
  190.0 13.3 %match_rows.3 = (f32[8,32,4096]{2,1,0:T(8,128)}, f32[32,4096]{1,0:T(8,128)S(1)}) custom-call(f32[8]{0:T(128)S(1)} %dynamic_slice.3.refs_0_.weight_ref, f32[4,32,4224]{2,1,0:T(8,128)S(1)} %get-tuple-element.17.warped_ref, f32[4,8,5376]{2,1,0:T(8,128)S(1)} %collective-permute-done.2.above_ref, ...), custom_call_target="tpu_custom_call", output_to_operand_aliasing={{0}: (9, {})} | custom-call | bytes 83886080 | tf_op jit(solution)/shard_map/match_rows/pallas_call | solution.py:304
  203.3 0.8 copy-done.3
  204.1 11.1 %sum_visits.1 = f32[8,4096]{1,0:T(8,128)} custom-call(f32[32,4096]{1,0:T(8,128)} %copy-done.3, f32[1]{0:T(128)} %bitcast.33.scale_ref), custom_call_target="tpu_custom_call" | custom-call | tf_op jit(solution)/shard_map/sum_visits/pallas_call | solution.py:378
  215.2 1.6 copy.22
  (43 shorter events, 1.0 us)
Async XLA Ops:
  8.6 13.7 %copy-start.7 = (s32[8,1,4096]{2,1,0:T(1,128)S(1)}, s32[8,1,4096]{2,1,0:T(1,128)}, u32[]{:S(2)}) copy-start(s32[8,1,4096]{2,1,0:T(1,128)} %param.13) | copy-start | bytes 393220
  8.6 14.0 %copy-start.4 = (f32[9,21]{1,0:T(8,128)S(1)}, f32[9,21]{1,0:T(8,128)}, u32[]{:S(2)}) copy-start(f32[9,21]{1,0:T(8,128)} %param.14) | copy-start | bytes 2272
  8.6 18.0 %copy-start.6 = (f32[8,1,8,4096]{3,2,1,0:T(8,128)S(1)}, f32[8,1,8,4096]{3,2,1,0:T(8,128)}, u32[]{:S(2)}) copy-start(f32[8,1,8,4096]{3,2,1,0:T(8,128)} %param.12) | copy-start | bytes 3145732
  8.7 118.3 %all-to-all-start = ((f32[32,8,64,128]{3,2,1,0:T(8,128)}), f32[32,8,64,128]{3,2,1,0:T(8,128)}, u32[]{:S(2)}, u32[]{:S(2)}) async-start(f32[32,8,64,128]{3,2,1,0:T(8,128)} %pack_rows.1), calls=%async_computation | async-start | bytes 16777216 | tf_op jit(solution)/shard_map/all_to_all | solution.py:470
  18.5 9.6 %copy-start.5 = (f32[9,21]{1,0:T(8,128)S(1)}, f32[9,21]{1,0:T(8,128)}, u32[]{:S(2)}) copy-start(f32[9,21]{1,0:T(8,128)} %param.15) | copy-start | bytes 2272
  127.0 29.6 %copy-start.9 = (s32[1,4096]{1,0:T(1,128)S(1)}, s32[1,4096]{1,0:T(1,128)}, u32[]{:S(2)}) copy-start(s32[1,4096]{1,0:T(1,128)} %param.17) | copy-start | bytes 49156
  134.0 1.3 copy-start.1
  135.4 31.3 %collective-permute-start = (f32[4,8,5376]{2,1,0:T(8,128)}, f32[4,8,5376]{2,1,0:T(8,128)}, u32[]{:S(2)}, u32[]{:S(2)}) collective-permute-start(f32[4,8,5376]{2,1,0:T(8,128)} %get-tuple-element.21), channel_id=1, source_target_pairs={{0,4},{4,8},{8,12},{12,16},{16,20},{20,24},{24,28},{28,32},{32,36}... | collective-permute-start | bytes 2064392 | tf_op jit(solution)/shard_map/ppermute | solution.py:478
  154.6 12.6 %collective-permute-start.1 = (f32[4,8,5376]{2,1,0:T(8,128)}, f32[4,8,5376]{2,1,0:T(8,128)}, u32[]{:S(2)}, u32[]{:S(2)}) collective-permute-start(f32[4,8,5376]{2,1,0:T(8,128)} %get-tuple-element.22), channel_id=1, source_target_pairs={{4,0},{8,4},{12,8},{16,12},{20,16},{24,20},{28,24},{32,28},{36,32}... | collective-permute-start | bytes 2064392 | tf_op jit(solution)/shard_map/ppermute | solution.py:479
  159.6 12.8 %copy-start.10 = (f32[32]{0:T(128)S(1)}, f32[32]{0:T(128)}, u32[]{:S(2)}) copy-start(f32[32]{0:T(128)} %param.19) | copy-start | bytes 388
  166.7 8.9 %copy-start.8 = (f32[8,1,9,32]{3,1,2,0:T(1,128)S(1)}, f32[8,1,9,32]{3,1,2,0:T(1,128)}, u32[]{:S(2)}) copy-start(f32[8,1,9,32]{3,1,2,0:T(1,128)} %param.16) | copy-start | bytes 27652
  167.2 22.8 %collective-permute-start.2 = (f32[4,8,5376]{2,1,0:T(8,128)}, f32[4,8,5376]{2,1,0:T(8,128)S(1)}, u32[]{:S(2)}, u32[]{:S(2)}) collective-permute-start(f32[4,8,5376]{2,1,0:T(8,128)} %get-tuple-element.23), channel_id=1, source_target_pairs={{0,4},{4,8},{8,12},{12,16},{16,20},{20,24},{24,28},{28,32},{32,36}... | collective-permute-start | bytes 2064392 | tf_op jit(solution)/shard_map/ppermute | solution.py:478
  170.3 19.7 %collective-permute-start.3 = (f32[4,8,5376]{2,1,0:T(8,128)}, f32[4,8,5376]{2,1,0:T(8,128)}, u32[]{:S(2)}, u32[]{:S(2)}) collective-permute-start(f32[4,8,5376]{2,1,0:T(8,128)} %get-tuple-element.24), channel_id=1, source_target_pairs={{4,0},{8,4},{12,8},{16,12},{20,16},{24,20},{28,24},{32,28},{36,32}... | collective-permute-start | bytes 2064392 | tf_op jit(solution)/shard_map/ppermute | solution.py:479
  174.3 2.4 %copy-start = (f32[32,4096]{1,0:T(8,128)S(1)}, f32[32,4096]{1,0:T(8,128)}, u32[]{:S(2)}) copy-start(f32[32,4096]{1,0:T(8,128)} %template_ref.1) | copy-start | bytes 1572868
  174.3 2.4 %copy-start.2 = (f32[4,32,4224]{2,1,0:T(8,128)S(1)}, f32[4,32,4224]{2,1,0:T(8,128)}, u32[]{:S(2)}) copy-start(f32[4,32,4224]{2,1,0:T(8,128)} %copy-done.1) | copy-start | bytes 6488068
  203.3 0.8 copy-start.3

commit v6 on v5

--- a/solution.py
+++ b/solution.py
@@ -12,7 +12,7 @@
 step = 108
 parts = 2
 room = 24 << 20
-chunks = (4, 4)
+chunks = (5, 3)
 bf16 = jnp.bfloat16
 
 
@@ -76,7 +76,7 @@
             for pair in range(patch_rows // 2):
                 source = (turn_ref[0] + first + local - pair + 2 * patches) % patches
                 pltpu.make_async_copy(
-                    got_ref.at[source, first + local],
+                    got_ref.at[source, local],
                     rows.at[local, pl.ds(pair * depth, depth), :],
                     sems.at[local],
                 ).start()
@@ -278,6 +278,198 @@
         total_ref[:, here] = total_ref[:, here] + weight * piece
 
 
+def spread_kernel(
+    weight_ref,
+    warped_ref,
+    down_ref,
+    across_ref,
+    coef_ref,
+    coef_up_ref,
+    coef_dn_ref,
+    template_ref,
+    difference_ref,
+    total_ref,
+    up_ref,
+    dn_ref,
+    pieces,
+    high_refs,
+    low_refs,
+    found,
+):
+    patch_rows, row_width = template_ref.shape
+    rows_out = patch_rows + 32
+    bases = across_ref.shape[0]
+    windows = pieces.shape[1] // lane
+    part = high_refs.shape[2] // lane
+    inside = lax.broadcasted_iota(jnp.int32, (patch_rows, lane), 1)
+
+    @pl.when(pl.program_id(0) == 0)
+    def _():
+        total_ref[...] = jnp.zeros_like(total_ref)
+
+    for p in range(windows // part):
+        for w in range(p * part, (p + 1) * part):
+            start = step * w + half_lane - (lane - step) // 2
+            tile, turn = start // lane, start % lane
+            values = warped_ref[0, :, tile * lane : (tile + 1) * lane]
+            if turn:
+                after = warped_ref[0, :, (tile + 1) * lane : (tile + 2) * lane]
+                values = jnp.where(
+                    inside < lane - turn,
+                    pltpu.roll(values, lane - turn, 1),
+                    pltpu.roll(after, lane - turn, 1),
+                )
+            high, low = split(values)
+            here = slice(w * lane, (w + 1) * lane)
+            for j, value in enumerate((high, low, high)):
+                pieces[j * patch_rows : (j + 1) * patch_rows, here] = value
+        wide = slice(p * part * lane, (p + 1) * part * lane)
+        vertical = jnp.dot(down_ref[...], pieces[:, wide], preferred_element_type=jnp.float32)
+        high_refs[p], low_refs[p] = split(vertical)
+
+        def gathered(refs, b):
+            rows = slice(b * rows_out, (b + 1) * rows_out)
+            return jnp.concatenate(
+                [refs[p, rows, lane * i : lane * (i + 1)] for i in range(part)], axis=0
+            )
+
+        matched = jnp.zeros((part * rows_out, lane), jnp.float32)
+        for b in range(bases):
+            operand = jnp.concatenate([gathered(high_refs, b), gathered(low_refs, b)], axis=1)
+            both = jnp.dot(operand, across_ref[b], preferred_element_type=jnp.float32)
+            scales = []
+            for w in range(p * part, (p + 1) * part):
+                here = slice(w * lane, (w + 1) * lane)
+                for ref, count in ((coef_ref, patch_rows), (coef_up_ref, 16), (coef_dn_ref, 16)):
+                    scales.append(jnp.broadcast_to(ref[0, b : b + 1, here], (count, lane)))
+            matched = matched + jnp.concatenate(scales, axis=0) * (both[:, :lane] + both[:, lane:])
+        found[p * part * rows_out : (p + 1) * part * rows_out, :] = matched
+    weight = weight_ref[pl.program_id(0)]
+    inside = lax.broadcasted_iota(jnp.int32, (rows_out, lane), 1)
+    tiles = row_width // lane
+    fold = folded(tiles)
+    for tile in range(tiles):
+        piece = None
+        for w in range(tile * lane // step, ((tile + 1) * lane - 1) // step + 1):
+            start = step * w - tile * lane
+            values = found[w * rows_out : (w + 1) * rows_out, :]
+            if start % lane:
+                values = pltpu.roll(values, start % lane, 1)
+            piece = values if piece is None else jnp.where(inside < start, piece, values)
+        here = slice(lane * tile, lane * (tile + 1))
+        own, above, below = piece[:patch_rows], piece[patch_rows : patch_rows + 16], piece[-16:]
+        difference_ref[0, :, here] = own - template_ref[:, here]
+        total_ref[:, here] = total_ref[:, here] + weight * own
+        at = 2 * (tile // fold)
+        spare = slice((tiles + tile % fold) * lane, (tiles + tile % fold + 1) * lane)
+        up_ref[0, :, here] = above[8:]
+        up_ref[0, at : at + 2, spare] = above[6:8]
+        dn_ref[0, :, here] = below[:8]
+        dn_ref[0, at : at + 2, spare] = below[8:10]
+
+
+def spread_rows(weights, warped, down, across, coefs, coefs_up, coefs_dn, template):
+    count, patch_rows, width = warped.shape
+    visits, bases, span = coefs.shape
+    row_width = template.shape[1]
+    part = span // lane // parts
+    edge = row_width + folded(row_width // lane) * lane
+    coef_spec = pl.BlockSpec((1, bases, span), lambda q: (q, 0, 0))
+    edge_spec = pl.BlockSpec((1, 8, edge), lambda q: (q, 0, 0))
+    return pl.pallas_call(
+        spread_kernel,
+        out_shape=(
+            jax.ShapeDtypeStruct((visits, patch_rows, row_width), jnp.float32),
+            jax.ShapeDtypeStruct(template.shape, jnp.float32),
+            jax.ShapeDtypeStruct((count, 8, edge), jnp.float32),
+            jax.ShapeDtypeStruct((count, 8, edge), jnp.float32),
+        ),
+        grid=(count,),
+        in_specs=[
+            pl.BlockSpec(memory_space=pltpu.SMEM),
+            pl.BlockSpec((1, patch_rows, width), lambda q: (q, 0, 0)),
+            pl.BlockSpec(down.shape, lambda q: (0, 0)),
+            pl.BlockSpec(across.shape, lambda q: (0, 0, 0)),
+            coef_spec,
+            coef_spec,
+            coef_spec,
+            pl.BlockSpec(template.shape, lambda q: (0, 0)),
+        ],
+        out_specs=[
+            pl.BlockSpec((1, patch_rows, row_width), lambda q: (q, 0, 0)),
+            pl.BlockSpec(template.shape, lambda q: (0, 0)),
+            edge_spec,
+            edge_spec,
+        ],
+        scratch_shapes=[
+            pltpu.VMEM((down.shape[1], span), bf16),
+            pltpu.VMEM((parts, down.shape[0], part * lane), bf16),
+            pltpu.VMEM((parts, down.shape[0], part * lane), bf16),
+            pltpu.VMEM((span // lane * (patch_rows + 32), lane), jnp.float32),
+        ],
+        compiler_params=pltpu.CompilerParams(vmem_limit_bytes=40 << 20),
+        cost_estimate=pl.CostEstimate(flops=0, bytes_accessed=24 * count << 20, transcendentals=0),
+        name="spread_rows",
+    )(weights, warped, down, across, coefs, coefs_up, coefs_dn, template)
+
+
+def add_kernel(
+    weight_ref, above_ref, below_ref, before_ref, sums_ref, difference_ref, total_ref
+):
+    _, patch_rows, row_width = before_ref.shape
+    tiles = row_width // lane
+    fold = folded(tiles)
+    weight = weight_ref[pl.program_id(0)]
+
+    @pl.when(pl.program_id(0) == 0)
+    def _():
+        total_ref[...] = sums_ref[...]
+
+    difference_ref[0, 10 : patch_rows - 10, :] = before_ref[0, 10 : patch_rows - 10, :]
+    for tile in range(tiles):
+        here = slice(lane * tile, lane * (tile + 1))
+        at = 2 * (tile // fold)
+        spare = slice((tiles + tile % fold) * lane, (tiles + tile % fold + 1) * lane)
+        for first, ref, rows, columns in (
+            (0, above_ref, slice(0, 8), here),
+            (8, above_ref, slice(at, at + 2), spare),
+            (patch_rows - 10, below_ref, slice(at, at + 2), spare),
+            (patch_rows - 8, below_ref, slice(0, 8), here),
+        ):
+            values = ref[0, rows, columns]
+            to = slice(first, first + rows.stop - rows.start)
+            difference_ref[0, to, here] = before_ref[0, to, here] + values
+            total_ref[to, here] = total_ref[to, here] + weight * values
+
+
+def add_edges(weights, above, below, difference, total):
+    count, _, edge = above.shape
+    _, patch_rows, row_width = difference.shape
+    row_spec = pl.BlockSpec((1, patch_rows, row_width), lambda q: (q, 0, 0))
+    edge_spec = pl.BlockSpec((1, 8, edge), lambda q: (q, 0, 0))
+    total_spec = pl.BlockSpec(total.shape, lambda q: (0, 0))
+    return pl.pallas_call(
+        add_kernel,
+        out_shape=(
+            jax.ShapeDtypeStruct(difference.shape, jnp.float32),
+            jax.ShapeDtypeStruct(total.shape, jnp.float32),
+        ),
+        grid=(count,),
+        in_specs=[
+            pl.BlockSpec(memory_space=pltpu.SMEM),
+            edge_spec,
+            edge_spec,
+            row_spec,
+            total_spec,
+        ],
+        out_specs=[row_spec, total_spec],
+        input_output_aliases={3: 0},
+        compiler_params=pltpu.CompilerParams(vmem_limit_bytes=room),
+        cost_estimate=pl.CostEstimate(flops=0, bytes_accessed=3 * count << 20, transcendentals=0),
+        name="add_edges",
+    )(weights, above, below, difference, total)
+
+
 def match_rows(
     first, weights, warped, above, below, down, across, coefs, template, before, difference
 ):
@@ -433,13 +625,17 @@
     taps = jnp.pad(warp_taps[:, 0], ((0, 0), (0, 0), (half_lane, half_lane)))
     shift = jnp.pad(warp_shift, ((0, 0), (0, 0), (half_lane, half_lane)))
 
-    windows = -(-row_width // step)
-    cells = jnp.pad(grid_index[0], (0, windows * step - row_width)).reshape(windows, step)
-    cells = jnp.pad(cells, ((0, 0), (0, lane - step))).reshape(-1)
-    one_hot = (cells[None, :] == jnp.arange(coef_table.shape[3])[:, None]).astype(jnp.float32)
-    coefs = jnp.einsum(
-        "qbg,gx->qbx", coef_table[:, 0], one_hot, precision=lax.Precision.HIGHEST
-    )
+    def windowed_coefs(table, grid):
+        windows = -(-row_width // step)
+        cells = jnp.pad(grid, (0, windows * step - row_width)).reshape(windows, step)
+        cells = jnp.pad(cells, ((0, 0), (0, lane - step))).reshape(-1)
+        one_hot = (cells[None, :] == jnp.arange(table.shape[2])[:, None]).astype(jnp.float32)
+        return jnp.einsum("qbg,gx->qbx", table, one_hot, precision=lax.Precision.HIGHEST)
+
+    down_pairs = [(i, i + 1) for i in range(patches - 1)]
+    up_pairs = [(i + 1, i) for i in range(patches - 1)]
+    table = coef_table[:, 0]
+    coefs = windowed_coefs(table, grid_index[0])
 
     rows = jnp.arange(patch_rows)
     pair = jnp.arange(8)
@@ -449,6 +645,10 @@
     down = taken(basis_rows, inner[None, :] - rows[:, None] + half).reshape(-1, inner.shape[0])
     down_high, down_low = split_table(down)
     down = jnp.concatenate([down_high, down_high, down_low], axis=1)
+    outer = jnp.concatenate([rows, jnp.arange(16) - 16, jnp.arange(16) + patch_rows])
+    wide = taken(basis_rows, rows[None, :] - outer[:, None] + half).reshape(-1, patch_rows)
+    wide_high, wide_low = split_table(wide)
+    wide = jnp.concatenate([wide_high, wide_high, wide_low], axis=1)
     out = jnp.arange(lane)[None, :]
     across = taken(
         basis_cols, jnp.where(out < step, jnp.arange(lane)[:, None] - out, basis_cols.shape[1])
@@ -465,24 +665,45 @@
         visit_weight, lax.axis_index("visit") * visits, visits
     )
 
-    starts = [sum(chunks[:i]) for i in range(len(chunks))]
-    sent = pack_rows(0, visits, tract_row, tiled_rows, patches)
-    got = lax.all_to_all(sent, "patch", split_axis=0, concat_axis=0, tiled=True)
-    down_pairs = [(i, i + 1) for i in range(patches - 1)]
-    up_pairs = [(i + 1, i) for i in range(patches - 1)]
-    fields = []
-    for first, count in zip(starts, chunks):
-        warped, head, tail = warp_rows(first, count, turn, got, taps, shift, patch_rows)
-        if fields:
-            head, tail, fields[-1] = lax.optimization_barrier((head, tail, fields[-1]))
-        above = lax.ppermute(tail, "patch", down_pairs)
-        below = lax.ppermute(head, "patch", up_pairs)
-        fields.append((warped, above, below))
-    total, difference = None, None
-    for first, field in zip(starts, fields):
-        difference, total = match_rows(
-            first, weights, *field, down, across, coefs, template, total, difference
+    early, late = chunks
+    sent = [
+        pack_rows(first, count, tract_row, tiled_rows, patches)
+        for first, count in ((0, early), (early, late))
+    ]
+    packed = jnp.concatenate([table.reshape(-1), grid_index[0].astype(jnp.float32)])
+    nearby = [lax.ppermute(packed, "patch", pairs) for pairs in (down_pairs, up_pairs)]
+    sent[1], down, wide, across, coefs, taps, shift, weights, turn, nearby = (
+        lax.optimization_barrier(
+            (sent[1], down, wide, across, coefs, taps, shift, weights, turn, nearby)
         )
+    )
+    got = [lax.all_to_all(block, "patch", split_axis=0, concat_axis=0, tiled=True) for block in sent]
+
+    def neighbour_coefs(values):
+        cells = values[table.size :].astype(jnp.int32)
+        return windowed_coefs(values[: table.size].reshape(table.shape), cells)
+
+    warped, _, _ = warp_rows(0, early, turn, got[0], taps, shift, patch_rows)
+    difference, total, up, dn = spread_rows(
+        weights,
+        warped,
+        wide,
+        across,
+        coefs,
+        *map(neighbour_coefs, nearby),
+        template,
+    )
+    from_above = lax.ppermute(dn, "patch", down_pairs)
+    from_below = lax.ppermute(up, "patch", up_pairs)
+    turn, total = lax.optimization_barrier((turn, total))
+    warped, head, tail = warp_rows(early, late, turn, got[1], taps, shift, patch_rows)
+    above = lax.ppermute(tail, "patch", down_pairs)
+    below = lax.ppermute(head, "patch", up_pairs)
+    from_above, from_below, warped = lax.optimization_barrier((from_above, from_below, warped))
+    difference, total = add_edges(weights, from_above, from_below, difference, total)
+    difference, total = match_rows(
+        early, weights, warped, above, below, down, across, coefs, template, total, difference
+    )
     coadd = sum_visits(total, jnp.sum(visit_weight).reshape(1))
     return difference, coadd
 

time: 218 us -> 182 us (0.83)
  the two profiles are of different devices: /device:TPU:1 before, /device:TPU:8 now
where the time goes in v6:
time: 182 us; the launch traced here: 181 us
  Pallas kernels  75.6 us (42%)
  starting transfers between devices  42.3 us (23%)
  waiting for transfers between devices  29.8 us (16%)
  local copies, waits for them, and re-layouts  19.1 us (10%)
  other arithmetic  7.15 us (4%)
  between operations  3.84 us (2%)
  matrix products  3.32 us (2%)
    ppermute x2, waiting for transfers between devices, on_device(): lax.ppermute(packed, 'patch', pairs)  29.8 us
    pallas_call x1, Pallas kernels, spread_rows(): pl.pallas_call(spread_kernel, out_shape=(jax.ShapeDtypeStruct((visits, pa...  25.5 us
    all_to_all x2, starting transfers between devices, on_device(): lax.all_to_all(block, 'patch', split_axis=0, concat_axis=0, tiled=True)  19 us
    pallas_call x2, Pallas kernels, warp_rows(): pl.pallas_call(functools.partial(warp_kernel, first), out_shape=(jax.Shap...  14.2 us
    pallas_call x1, Pallas kernels, sum_visits(): pl.pallas_call(sum_kernel, out_shape=jax.ShapeDtypeStruct(shape, jnp.floa...  10.3 us
    pallas_call x1, Pallas kernels, match_rows(): pl.pallas_call(body, out_shape=(jax.ShapeDtypeStruct((visits, patch_rows,...  10.3 us
    pallas_call x2, Pallas kernels, pack_rows(): pl.pallas_call(functools.partial(pack_kernel, first), out_shape=jax.Shape...  9.82 us
    ppermute x2, starting transfers between devices, on_device(): lax.ppermute(packed, 'patch', pairs)  7.67 us
  transfers between devices with their start and end apart: 8, of which 1 were waited for; matrix products, arithmetic and copies ran while one was open for 13% of the time, Pallas kernels for 27%

profile of v6, /device:TPU:8, one launch (start us, length us, event | category | flops | bytes accessed | tf_op | source)
XLA Modules:
  0.0 181.0 jit_solution(1865773502549101300)
XLA Ops:
  0.6 5.8 %pack_rows.3 = f32[32,5,64,128]{3,2,1,0:T(8,128)} custom-call(s32[8,32]{1,0:T(8,128)} %places_ref.3, f32[8,1024,128]{2,1,0:T(8,128)} %bitcast.159), custom_call_target="tpu_custom_call" | custom-call | bytes 15728640 | tf_op jit(solution)/shard_map/pack_rows/pallas_call | solution.py:39
  6.4 8.7 %all-to-all-start = ((f32[32,5,64,128]{3,2,1,0:T(8,128)}), f32[32,5,64,128]{3,2,1,0:T(8,128)}, u32[]{:S(2)}, u32[]{:S(2)}) async-start(f32[32,5,64,128]{3,2,1,0:T(8,128)} %pack_rows.3), calls=%async_computation | async-start | bytes 10485760 | tf_op jit(solution)/shard_map/all_to_all | solution.py:680
  15.2 0.1 reduce.42
  15.4 2.1 %collective-permute-start = (f32[6400]{0:T(1024)S(1)}, f32[6400]{0:T(1024)S(1)}, u32[]{:S(2)}, u32[]{:S(2)}) collective-permute-start(f32[6400]{0:T(1024)S(1)} %pad_maximum_fusion.2), channel_id=1, source_target_pairs={{0,4},{4,8},{8,12},{12,16},{16,20},{20,24},{24,28},{28,32},{32,36}... | collective-permute-start | bytes 76808 | tf_op jit(solution)/shard_map/ppermute | solution.py:674
  17.5 5.6 %collective-permute-start.1 = (f32[6400]{0:T(1024)S(1)}, f32[6400]{0:T(1024)S(1)}, u32[]{:S(2)}, u32[]{:S(2)}) collective-permute-start(f32[6400]{0:T(1024)S(1)} %pad_maximum_fusion.2), channel_id=1, source_target_pairs={{4,0},{8,4},{12,8},{16,12},{20,16},{24,20},{28,24},{32,28},{36,32}... | collective-permute-start | bytes 76808 | tf_op jit(solution)/shard_map/ppermute | solution.py:674
  23.1 0.2 slice_reduce_fusion.22
  23.3 0.1 broadcast_in_dim.1242
  23.5 0.1 broadcast_in_dim.1236
  23.6 0.5 slice_reduce_fusion.41
  24.2 0.1 broadcast_in_dim.1230
  24.3 0.1 broadcast_in_dim.1224
  24.5 0.1 broadcast_in_dim.1218
  24.6 0.1 broadcast_in_dim.1212
  24.8 0.1 broadcast_in_dim.1206
  24.9 0.1 broadcast_in_dim.1200
  25.1 0.1 broadcast_in_dim.1194
  25.2 0.1 broadcast_in_dim.1188
  25.4 0.1 broadcast_in_dim.1182
  25.5 0.1 broadcast_in_dim.1176
  25.7 0.1 broadcast_in_dim.1170
  25.8 0.1 broadcast_in_dim.1164
  26.0 0.1 broadcast_in_dim.1158
  26.1 0.1 broadcast_in_dim.1152
  26.3 0.1 broadcast_in_dim.1146
  26.6 0.1 broadcast_in_dim.1134
  30.0 0.2 reshape.1380
  30.3 0.9 reduce-precision_convert_fusion.2
  31.4 0.2 fusion.59
  31.6 1.9 %reduce-precision_convert_fusion.1 = (bf16[576,32]{1,0:T(8,128)(2,1)S(1)}, f32[576,32]{1,0:T(8,128)S(1)}) fusion(f32[576]{0:T(1024)S(1)} %broadcast_in_dim.1348, pred[64,32]{1,0:T(8,128)(4,1)S(1)} %get-tuple-element.128, f32[576]{0:T(1024)S(1)} %broadcast_in_dim.1343, pred[64,32]{1,0:T(8,128)(4,1)S(1)} %get-tuple-element.129, ...), kind=kLoop, calls=%fused_computation.17 | loop fusion | flops 423936 | bytes 201984 | tf_op jit(solution)/shard_map/convert_element_type | solution.py:592
  33.5 0.2 slice_reduce_fusion.1
  33.7 0.5 slice_reduce_fusion.20
  34.2 0.1 pad_maximum_fusion.down_ref
  34.4 0.2 fusion.38
  34.6 1.5 fusion.10
  36.2 1.2 fusion.1.across_ref
  37.4 1.1 convolution_bitcast_fusion.coef_ref
  38.5 0.2 pad_maximum_fusion.1.down_ref
  38.7 4.1 %pack_rows.2 = f32[32,3,64,128]{3,2,1,0:T(8,128)} custom-call(s32[8,32]{1,0:T(8,128)} %places_ref.3, f32[8,1024,128]{2,1,0:T(8,128)} %bitcast.160), custom_call_target="tpu_custom_call" | custom-call | bytes 9437184 | tf_op jit(solution)/shard_map/pack_rows/pallas_call | solution.py:39
  42.7 1.2 slice.204
  46.6 0.3 pad.32.shift_ref
  46.9 2.6 %pad.31.taps_ref = f32[8,8,4224]{2,1,0:T(8,128)} pad(f32[8,8,4096]{2,1,0:T(8,128)} %bitcast.161, f32[]{:T(128)} %constant.74.clone.1), padding=0_0x0_0x64_64 | pad | bytes 2129924 | tf_op jit(solution)/shard_map/jit(_pad)/pad | solution.py:625
  49.6 29.8 %collective-permute-done = f32[6400]{0:T(1024)S(1)} collective-permute-done((f32[6400]{0:T(1024)S(1)}, f32[6400]{0:T(1024)S(1)}, u32[]{:S(2)}, u32[]{:S(2)}) %collective-permute-start) | collective-permute-done | bytes 25632 | tf_op jit(solution)/shard_map/ppermute | solution.py:674
  79.3 10.3 %all-to-all-start.1 = ((f32[32,3,64,128]{3,2,1,0:T(8,128)}), f32[32,3,64,128]{3,2,1,0:T(8,128)}, u32[]{:S(2)}, u32[]{:S(2)}) async-start(f32[32,3,64,128]{3,2,1,0:T(8,128)} %pack_rows.2), calls=%async_computation.1 | async-start | bytes 6291456 | tf_op jit(solution)/shard_map/all_to_all | solution.py:680
  89.8 0.1 reshape.1383
  90.0 0.1 reshape.1385
  90.1 1.1 fusion.5.coef_up_ref
  91.2 1.1 fusion.8.coef_dn_ref
  92.4 8.5 %warp_rows.2 = (f32[5,32,4224]{2,1,0:T(8,128)S(1)}, f32[5,8,5376]{2,1,0:T(8,128)}, f32[5,8,5376]{2,1,0:T(8,128)}) custom-call(s32[1]{0:T(128)} %bitcast.53.turn_ref, f32[32,5,64,128]{3,2,1,0:T(8,128)} %all-to-all-done.got_ref, f32[8,8,4224]{2,1,0:T(8,128)S(1)} %copy-done.2, s32[8,1,4224]{2,1,0:T(1,128)S(1)} %pad.32.shift_ref), custom_call_target="tpu_custom_call" | custom-call | bytes 62914560 | tf_op jit(solution)/shard_map/warp_rows/pallas_call | solution.py:146
  100.9 25.5 %spread_rows.1 = (f32[8,32,4096]{2,1,0:T(8,128)}, f32[32,4096]{1,0:T(8,128)S(1)}, f32[5,8,5120]{2,1,0:T(8,128)}, f32[5,8,5120]{2,1,0:T(8,128)}) custom-call(f32[8]{0:T(128)S(1)} %dynamic_slice.3.weight_ref, f32[5,32,4224]{2,1,0:T(8,128)S(1)} %get-tuple-element.34.warped_ref, bf16[576,96]{1,0:T(8,128)(2,1)S(1)} %pad_maximum_fusion.1.down_ref, ...), custom_call_target="tpu_custom_call" | custom-call | bytes 125829120 | tf_op jit(solution)/shard_map/spread_rows/pallas_call | solution.py:379
  126.4 0.8 copy-done.7
  127.2 2.1 %collective-permute-start.2 = (f32[5,8,5120]{2,1,0:T(8,128)}, f32[5,8,5120]{2,1,0:T(8,128)}, u32[]{:S(2)}, u32[]{:S(2)}) collective-permute-start(f32[5,8,5120]{2,1,0:T(8,128)} %get-tuple-element.40), channel_id=1, source_target_pairs={{0,4},{4,8},{8,12},{12,16},{16,20},{20,24},{24,28},{28,32},{32,36}... | collective-permute-start | bytes 2457608 | tf_op jit(solution)/shard_map/ppermute | solution.py:696
  129.2 5.6 %collective-permute-start.3 = (f32[5,8,5120]{2,1,0:T(8,128)}, f32[5,8,5120]{2,1,0:T(8,128)}, u32[]{:S(2)}, u32[]{:S(2)}) collective-permute-start(f32[5,8,5120]{2,1,0:T(8,128)} %get-tuple-element.41), channel_id=1, source_target_pairs={{4,0},{8,4},{12,8},{16,12},{20,16},{24,20},{28,24},{32,28},{36,32}... | collective-permute-start | bytes 2457608 | tf_op jit(solution)/shard_map/ppermute | solution.py:697
  134.9 1.2 copy-done.3
  136.1 5.7 %warp_rows.3 = (f32[3,32,4224]{2,1,0:T(8,128)S(1)}, f32[3,8,5376]{2,1,0:T(8,128)}, f32[3,8,5376]{2,1,0:T(8,128)}) custom-call(s32[1]{0:T(128)} %bitcast.53.turn_ref, f32[32,3,64,128]{3,2,1,0:T(8,128)} %all-to-all-done.1.got_ref, f32[8,8,4224]{2,1,0:T(8,128)S(1)} %copy-done.3, s32[8,1,4224]{2,1,0:T(1,128)S(1)} %pad.32.shift_ref), custom_call_target="tpu_custom_call" | custom-call | bytes 37748736 | tf_op jit(solution)/shard_map/warp_rows/pallas_call | solution.py:146
  141.8 1.2 copy-done.5
  143.0 1.9 %collective-permute-start.4 = (f32[3,8,5376]{2,1,0:T(8,128)}, f32[3,8,5376]{2,1,0:T(8,128)}, u32[]{:S(2)}, u32[]{:S(2)}) collective-permute-start(f32[3,8,5376]{2,1,0:T(8,128)} %get-tuple-element.47), channel_id=1, source_target_pairs={{0,4},{4,8},{8,12},{12,16},{16,20},{20,24},{24,28},{28,32},{32,36}... | collective-permute-start | bytes 1548296 | tf_op jit(solution)/shard_map/ppermute | solution.py:700
  144.9 6.0 %collective-permute-start.5 = (f32[3,8,5376]{2,1,0:T(8,128)}, f32[3,8,5376]{2,1,0:T(8,128)}, u32[]{:S(2)}, u32[]{:S(2)}) collective-permute-start(f32[3,8,5376]{2,1,0:T(8,128)} %get-tuple-element.48), channel_id=1, source_target_pairs={{4,0},{8,4},{12,8},{16,12},{20,16},{24,20},{28,24},{32,28},{36,32}... | collective-permute-start | bytes 1548296 | tf_op jit(solution)/shard_map/ppermute | solution.py:701
  150.9 0.6 reduce_sum.9
  151.5 1.0 copy-done.8
  152.5 5.6 %add_edges.1 = (f32[8,32,4096]{2,1,0:T(8,128)}, f32[32,4096]{1,0:T(8,128)S(1)}) custom-call(f32[8]{0:T(128)S(1)} %dynamic_slice.3.weight_ref, f32[5,8,5120]{2,1,0:T(8,128)} %collective-permute-done.2.above_ref, f32[5,8,5120]{2,1,0:T(8,128)} %collective-permute-done.3.below_ref, ...), custom_call_target="tpu_custom_call", output_to_operand_aliasing={{0}: (3, {})} | custom-call | bytes 15728640 | tf_op jit(solution)/shard_map/add_edges/pallas_call | solution.py:451
  158.1 10.3 %match_rows.1 = (f32[8,32,4096]{2,1,0:T(8,128)}, f32[32,4096]{1,0:T(8,128)S(1)}) custom-call(f32[8]{0:T(128)S(1)} %dynamic_slice.3.weight_ref, f32[3,32,4224]{2,1,0:T(8,128)S(1)} %copy-done.6, f32[3,8,5376]{2,1,0:T(8,128)} %collective-permute-done.4.above_ref, f32[3,8,5376]{2,1,0:T(8,128)} %collective-permute-done.5.below_ref, ...), custom_call_target="tpu_custom_call", output_to_operand_aliasing={{0}: (9, {})} | custom-call | bytes 62914560 | tf_op jit(solution)/shard_map/match_rows/pallas_call | solution.py:496
  168.4 0.8 copy-done.9
  169.2 10.3 %sum_visits.1 = f32[8,4096]{1,0:T(8,128)} custom-call(f32[32,4096]{1,0:T(8,128)} %copy-done.9, f32[1]{0:T(128)} %bitcast.60.scale_ref), custom_call_target="tpu_custom_call" | custom-call | tf_op jit(solution)/shard_map/sum_visits/pallas_call | solution.py:570
  179.5 1.6 copy.26
  (128 shorter events, 5.5 us)
Async XLA Ops:
  6.4 8.8 %copy-start.14 = (s32[1,4096]{1,0:T(1,128)S(1)}, s32[1,4096]{1,0:T(1,128)}, u32[]{:S(2)}) copy-start(s32[1,4096]{1,0:T(1,128)} %param.17) | copy-start | bytes 49156
  6.4 8.8 %copy-start.12 = (f32[8,1,9,32]{3,1,2,0:T(1,128)S(1)}, f32[8,1,9,32]{3,1,2,0:T(1,128)}, u32[]{:S(2)}) copy-start(f32[8,1,9,32]{3,1,2,0:T(1,128)} %param.16) | copy-start | bytes 27652
  6.4 16.7 %copy-start.10 = (f32[9,21]{1,0:T(8,128)S(1)}, f32[9,21]{1,0:T(8,128)}, u32[]{:S(2)}) copy-start(f32[9,21]{1,0:T(8,128)} %param.14) | copy-start | bytes 2272
  6.4 72.9 %all-to-all-start = ((f32[32,5,64,128]{3,2,1,0:T(8,128)}), f32[32,5,64,128]{3,2,1,0:T(8,128)}, u32[]{:S(2)}, u32[]{:S(2)}) async-start(f32[32,5,64,128]{3,2,1,0:T(8,128)} %pack_rows.3), calls=%async_computation | async-start | bytes 10485760 | tf_op jit(solution)/shard_map/all_to_all | solution.py:680
  15.2 18.3 %copy-start.11 = (f32[9,21]{1,0:T(8,128)S(1)}, f32[9,21]{1,0:T(8,128)}, u32[]{:S(2)}) copy-start(f32[9,21]{1,0:T(8,128)} %param.15) | copy-start | bytes 2272
  15.4 63.9 %collective-permute-start = (f32[6400]{0:T(1024)S(1)}, f32[6400]{0:T(1024)S(1)}, u32[]{:S(2)}, u32[]{:S(2)}) collective-permute-start(f32[6400]{0:T(1024)S(1)} %pad_maximum_fusion.2), channel_id=1, source_target_pairs={{0,4},{4,8},{8,12},{12,16},{16,20},{20,24},{24,28},{28,32},{32,36}... | collective-permute-start | bytes 76808 | tf_op jit(solution)/shard_map/ppermute | solution.py:674
  17.5 61.9 %collective-permute-start.1 = (f32[6400]{0:T(1024)S(1)}, f32[6400]{0:T(1024)S(1)}, u32[]{:S(2)}, u32[]{:S(2)}) collective-permute-start(f32[6400]{0:T(1024)S(1)} %pad_maximum_fusion.2), channel_id=1, source_target_pairs={{4,0},{8,4},{12,8},{16,12},{20,16},{24,20},{28,24},{32,28},{36,32}... | collective-permute-start | bytes 76808 | tf_op jit(solution)/shard_map/ppermute | solution.py:674
  38.6 7.9 %copy-start.13 = (s32[8,1,4096]{2,1,0:T(1,128)S(1)}, s32[8,1,4096]{2,1,0:T(1,128)}, u32[]{:S(2)}) copy-start(s32[8,1,4096]{2,1,0:T(1,128)} %param.13) | copy-start | bytes 393220
  42.7 6.8 %copy-start.15 = (f32[32]{0:T(128)S(1)}, f32[32]{0:T(128)}, u32[]{:S(2)}) copy-start(f32[32]{0:T(128)} %param.19) | copy-start | bytes 388
  79.3 55.5 %all-to-all-start.1 = ((f32[32,3,64,128]{3,2,1,0:T(8,128)}), f32[32,3,64,128]{3,2,1,0:T(8,128)}, u32[]{:S(2)}, u32[]{:S(2)}) async-start(f32[32,3,64,128]{3,2,1,0:T(8,128)} %pack_rows.2), calls=%async_computation.1 | async-start | bytes 6291456 | tf_op jit(solution)/shard_map/all_to_all | solution.py:680
  90.1 2.2 %copy-start.2 = (f32[8,8,4224]{2,1,0:T(8,128)S(1)}, f32[8,8,4224]{2,1,0:T(8,128)}, u32[]{:S(2)}) copy-start(f32[8,8,4224]{2,1,0:T(8,128)} %pad.31.taps_ref) | copy-start | bytes 3244036
  92.4 8.5 %copy-start = (bf16[9,256,256]{2,1,0:T(8,128)(2,1)S(1)}, bf16[9,256,256]{2,1,0:T(8,128)(2,1)}, u32[]{:S(2)}) copy-start(bf16[9,256,256]{2,1,0:T(8,128)(2,1)} %fusion.1.across_ref) | copy-start | bytes 3538948
  92.4 8.5 %copy-start.4 = (f32[32,4096]{1,0:T(8,128)S(1)}, f32[32,4096]{1,0:T(8,128)}, u32[]{:S(2)}) copy-start(f32[32,4096]{1,0:T(8,128)} %template_ref.3) | copy-start | bytes 1572868
  126.4 0.8 copy-start.7
  127.2 24.3 %collective-permute-start.2 = (f32[5,8,5120]{2,1,0:T(8,128)}, f32[5,8,5120]{2,1,0:T(8,128)}, u32[]{:S(2)}, u32[]{:S(2)}) collective-permute-start(f32[5,8,5120]{2,1,0:T(8,128)} %get-tuple-element.40), channel_id=1, source_target_pairs={{0,4},{4,8},{8,12},{12,16},{16,20},{20,24},{24,28},{28,32},{32,36}... | collective-permute-start | bytes 2457608 | tf_op jit(solution)/shard_map/ppermute | solution.py:696
  129.2 22.3 %collective-permute-start.3 = (f32[5,8,5120]{2,1,0:T(8,128)}, f32[5,8,5120]{2,1,0:T(8,128)}, u32[]{:S(2)}, u32[]{:S(2)}) collective-permute-start(f32[5,8,5120]{2,1,0:T(8,128)} %get-tuple-element.41), channel_id=1, source_target_pairs={{4,0},{8,4},{12,8},{16,12},{20,16},{24,20},{28,24},{32,28},{36,32}... | collective-permute-start | bytes 2457608 | tf_op jit(solution)/shard_map/ppermute | solution.py:697
  134.9 1.2 copy-start.3
  141.8 1.2 copy-start.5
  143.0 15.1 %collective-permute-start.4 = (f32[3,8,5376]{2,1,0:T(8,128)}, f32[3,8,5376]{2,1,0:T(8,128)}, u32[]{:S(2)}, u32[]{:S(2)}) collective-permute-start(f32[3,8,5376]{2,1,0:T(8,128)} %get-tuple-element.47), channel_id=1, source_target_pairs={{0,4},{4,8},{8,12},{12,16},{16,20},{20,24},{24,28},{28,32},{32,36}... | collective-permute-start | bytes 1548296 | tf_op jit(solution)/shard_map/ppermute | solution.py:700
  144.9 13.2 %collective-permute-start.5 = (f32[3,8,5376]{2,1,0:T(8,128)}, f32[3,8,5376]{2,1,0:T(8,128)}, u32[]{:S(2)}, u32[]{:S(2)}) collective-permute-start(f32[3,8,5376]{2,1,0:T(8,128)} %get-tuple-element.48), channel_id=1, source_target_pairs={{4,0},{8,4},{12,8},{16,12},{20,16},{24,20},{28,24},{32,28},{36,32}... | collective-permute-start | bytes 1548296 | tf_op jit(solution)/shard_map/ppermute | solution.py:701
  151.5 1.0 copy-start.8
  152.5 5.6 %copy-start.1 = (bf16[9,256,256]{2,1,0:T(8,128)(2,1)S(1)}, bf16[9,256,256]{2,1,0:T(8,128)(2,1)}, u32[]{:S(2)}) copy-start(bf16[9,256,256]{2,1,0:T(8,128)(2,1)} %fusion.1.across_ref) | copy-start | bytes 3538948
  152.5 5.6 %copy-start.6 = (f32[3,32,4224]{2,1,0:T(8,128)S(1)}, f32[3,32,4224]{2,1,0:T(8,128)}, u32[]{:S(2)}) copy-start(f32[3,32,4224]{2,1,0:T(8,128)} %copy-done.5) | copy-start | bytes 4866052
  168.4 0.8 copy-start.9

commit v7 on v6

--- a/solution.py
+++ b/solution.py
@@ -11,7 +11,7 @@
 half_lane = 64
 step = 108
 parts = 2
-room = 24 << 20
+whole = 58 << 20
 chunks = (5, 3)
 bf16 = jnp.bfloat16
 
@@ -45,7 +45,7 @@
             pl.BlockSpec((1, cells, lane), lambda q: (q + first, 0, 0)),
         ],
         out_specs=pl.BlockSpec((patches, 1, 2 * tiles, lane), lambda q: (0, q, 0, 0)),
-        compiler_params=pltpu.CompilerParams(vmem_limit_bytes=58 << 20),
+        compiler_params=pltpu.CompilerParams(vmem_limit_bytes=whole),
         cost_estimate=pl.CostEstimate(flops=0, bytes_accessed=3 * count << 20, transcendentals=0),
         name="pack_rows",
     )(tract_row, tiled_rows)
@@ -162,7 +162,7 @@
             pltpu.VMEM((2 * patch_rows, width + lane), bf16),
             pltpu.SemaphoreType.DMA((count,)),
         ],
-        compiler_params=pltpu.CompilerParams(vmem_limit_bytes=room),
+        compiler_params=pltpu.CompilerParams(vmem_limit_bytes=52 << 20),
         cost_estimate=pl.CostEstimate(flops=0, bytes_accessed=12 * count << 20, transcendentals=0),
         name="warp_rows",
     )(turn, got, taps, shift)
@@ -407,7 +407,7 @@
             pltpu.VMEM((parts, down.shape[0], part * lane), bf16),
             pltpu.VMEM((span // lane * (patch_rows + 32), lane), jnp.float32),
         ],
-        compiler_params=pltpu.CompilerParams(vmem_limit_bytes=40 << 20),
+        compiler_params=pltpu.CompilerParams(vmem_limit_bytes=58 << 20),
         cost_estimate=pl.CostEstimate(flops=0, bytes_accessed=24 * count << 20, transcendentals=0),
         name="spread_rows",
     )(weights, warped, down, across, coefs, coefs_up, coefs_dn, template)
@@ -464,7 +464,7 @@
         ],
         out_specs=[row_spec, total_spec],
         input_output_aliases={3: 0},
-        compiler_params=pltpu.CompilerParams(vmem_limit_bytes=room),
+        compiler_params=pltpu.CompilerParams(vmem_limit_bytes=52 << 20),
         cost_estimate=pl.CostEstimate(flops=0, bytes_accessed=3 * count << 20, transcendentals=0),
         name="add_edges",
     )(weights, above, below, difference, total)
@@ -522,21 +522,17 @@
             pltpu.VMEM((span // lane * patch_rows, lane), jnp.float32),
         ],
         input_output_aliases=aliases,
-        compiler_params=pltpu.CompilerParams(vmem_limit_bytes=room),
+        compiler_params=pltpu.CompilerParams(vmem_limit_bytes=50 << 20),
         cost_estimate=pl.CostEstimate(flops=0, bytes_accessed=20 * count << 20, transcendentals=0),
         name="match_rows",
     )(weights, warped, above, below, down, across, coefs, template, before, *extra)
 
 
-def sum_kernel(total_ref, scale_ref, out_ref, own, slots, own_sem, send_sems, recv_sems):
+def sum_kernel(total_ref, scale_ref, out_ref, slots, send_sems, recv_sems):
     me = lax.axis_index("visit")
     slabs = lax.axis_size("visit")
     rows = out_ref.shape[0]
     mesh_ids = pl.DeviceIdType.MESH
-    mine = pltpu.make_async_copy(
-        total_ref.at[pl.ds(pl.multiple_of(rows * me, rows), rows), :], own, own_sem
-    )
-    mine.start()
     barrier = pltpu.get_barrier_semaphore()
     for i in range(1, slabs):
         to = lax.rem(me + i, slabs)
@@ -557,8 +553,7 @@
         copies.append(copy)
     for copy in copies:
         copy.wait()
-    mine.wait()
-    result = own[...]
+    result = total_ref[pl.ds(pl.multiple_of(rows * me, rows), rows), :]
     for i in range(slabs - 1):
         result = result + slots[i]
     out_ref[...] = result / scale_ref[0]
@@ -571,18 +566,18 @@
         sum_kernel,
         out_shape=jax.ShapeDtypeStruct(shape, jnp.float32),
         in_specs=[
-            pl.BlockSpec(memory_space=pl.ANY),
+            pl.BlockSpec(memory_space=pltpu.VMEM),
             pl.BlockSpec(memory_space=pltpu.SMEM),
         ],
         out_specs=pl.BlockSpec(memory_space=pltpu.VMEM),
         scratch_shapes=[
-            pltpu.VMEM(shape, jnp.float32),
             pltpu.VMEM((slabs - 1,) + shape, jnp.float32),
-            pltpu.SemaphoreType.DMA,
             pltpu.SemaphoreType.DMA((slabs - 1,)),
             pltpu.SemaphoreType.DMA((slabs - 1,)),
         ],
-        compiler_params=pltpu.CompilerParams(collective_id=0, has_side_effects=True),
+        compiler_params=pltpu.CompilerParams(
+            collective_id=0, has_side_effects=True, vmem_limit_bytes=16 << 20
+        ),
         name="sum_visits",
     )(total, scale)
 

time: 182 us -> 182 us (level)
  local copies, waits for them, and re-layouts: 19.1 us -> 12.5 us
  matrix products: 3.32 us -> 7.71 us
  Pallas kernels: 75.6 us -> 78.4 us
    unnamed x33 -> x23, local copies, waits for them, and re-layouts: 6.65 us -> 0.71 us
    dot_general x3, matrix products: 3.32 us -> 7.71 us  [windowed_coefs(): jnp.einsum('qbg,gx->qbx', table, one_hot, precision=lax.Precision.HIGHEST)]
    pallas_call x2, Pallas kernels: 14.2 us -> 16.2 us  [warp_rows(): pl.pallas_call(functools.partial(warp_kernel, first), out_shape=(jax.Shap...]
  transfers between devices with their start and end apart: 8 -> 8, of which waited for: 1 -> 2; matrix products, arithmetic and copies ran while one was open for 13% -> 15% of each run, Pallas kernels for 27% -> 29%
where the time goes in v7:
time: 182 us; the launch traced here: 181 us
  Pallas kernels  78.4 us (43%)
  starting transfers between devices  42.4 us (23%)
  waiting for transfers between devices  28.6 us (16%)
  local copies, waits for them, and re-layouts  12.5 us (7%)
  other arithmetic  7.85 us (4%)
  matrix products  7.71 us (4%)
  between operations  3.77 us (2%)
    ppermute x2, waiting for transfers between devices, on_device(): lax.ppermute(packed, 'patch', pairs)  28.3 us
    pallas_call x1, Pallas kernels, spread_rows(): pl.pallas_call(spread_kernel, out_shape=(jax.ShapeDtypeStruct((visits, pa...  27.1 us
    all_to_all x2, starting transfers between devices, on_device(): lax.all_to_all(block, 'patch', split_axis=0, concat_axis=0, tiled=True)  19 us
    pallas_call x2, Pallas kernels, warp_rows(): pl.pallas_call(functools.partial(warp_kernel, first), out_shape=(jax.Shap...  16.2 us
    pallas_call x1, Pallas kernels, match_rows(): pl.pallas_call(body, out_shape=(jax.ShapeDtypeStruct((visits, patch_rows,...  10.4 us
    pallas_call x2, Pallas kernels, pack_rows(): pl.pallas_call(functools.partial(pack_kernel, first), out_shape=jax.Shape...  9.87 us
    pallas_call x1, Pallas kernels, sum_visits(): pl.pallas_call(sum_kernel, out_shape=jax.ShapeDtypeStruct(shape, jnp.floa...  9.38 us
    dot_general x3, matrix products, windowed_coefs(): jnp.einsum('qbg,gx->qbx', table, one_hot, precision=lax.Precision.HIGHEST)  7.71 us
  transfers between devices with their start and end apart: 8, of which 2 were waited for; matrix products, arithmetic and copies ran while one was open for 15% of the time, Pallas kernels for 29%

profile of v7, /device:TPU:8, one launch (start us, length us, event | category | flops | bytes accessed | tf_op | source)
XLA Modules:
  0.0 181.2 jit_solution(10754909974102261166)
XLA Ops:
  0.6 5.8 %pack_rows.3 = f32[32,5,64,128]{3,2,1,0:T(8,128)} custom-call(s32[8,32]{1,0:T(8,128)} %places_ref.3, f32[8,1024,128]{2,1,0:T(8,128)} %bitcast.159), custom_call_target="tpu_custom_call" | custom-call | bytes 15728640 | tf_op jit(solution)/shard_map/pack_rows/pallas_call | solution.py:39
  6.4 8.7 %all-to-all-start = ((f32[32,5,64,128]{3,2,1,0:T(8,128)}), f32[32,5,64,128]{3,2,1,0:T(8,128)}, u32[]{:S(2)}, u32[]{:S(2)}) async-start(f32[32,5,64,128]{3,2,1,0:T(8,128)} %pack_rows.3), calls=%async_computation | async-start | bytes 10485760 | tf_op jit(solution)/shard_map/all_to_all | solution.py:675
  15.2 0.1 reduce.42
  15.4 2.1 %collective-permute-start = (f32[6400]{0:T(1024)S(1)}, f32[6400]{0:T(1024)S(1)}, u32[]{:S(2)}, u32[]{:S(2)}) collective-permute-start(f32[6400]{0:T(1024)S(1)} %pad_maximum_fusion.2), channel_id=1, source_target_pairs={{0,4},{4,8},{8,12},{12,16},{16,20},{20,24},{24,28},{28,32},{32,36}... | collective-permute-start | bytes 76808 | tf_op jit(solution)/shard_map/ppermute | solution.py:669
  17.5 5.6 %collective-permute-start.1 = (f32[6400]{0:T(1024)S(1)}, f32[6400]{0:T(1024)S(1)}, u32[]{:S(2)}, u32[]{:S(2)}) collective-permute-start(f32[6400]{0:T(1024)S(1)} %pad_maximum_fusion.2), channel_id=1, source_target_pairs={{4,0},{8,4},{12,8},{16,12},{20,16},{24,20},{28,24},{32,28},{36,32}... | collective-permute-start | bytes 76808 | tf_op jit(solution)/shard_map/ppermute | solution.py:669
  23.1 0.2 slice_reduce_fusion.22
  23.3 0.1 broadcast_in_dim.1242
  23.5 0.1 broadcast_in_dim.1236
  23.6 0.5 slice_reduce_fusion.41
  24.2 0.1 broadcast_in_dim.1230
  24.3 0.1 broadcast_in_dim.1224
  24.5 0.1 broadcast_in_dim.1218
  24.6 0.1 broadcast_in_dim.1212
  24.8 0.1 broadcast_in_dim.1206
  24.9 0.1 broadcast_in_dim.1200
  25.1 0.1 broadcast_in_dim.1194
  25.2 0.1 broadcast_in_dim.1188
  25.4 0.1 broadcast_in_dim.1182
  25.5 0.1 broadcast_in_dim.1176
  25.7 0.1 broadcast_in_dim.1170
  25.8 0.1 broadcast_in_dim.1164
  26.0 0.1 broadcast_in_dim.1158
  26.1 0.1 broadcast_in_dim.1152
  26.3 0.1 broadcast_in_dim.1146
  26.4 0.1 broadcast_in_dim.1140
  26.6 0.1 broadcast_in_dim.1134
  26.7 0.1 broadcast_in_dim.1128
  26.9 0.1 broadcast_in_dim.1122
  30.0 0.2 reshape.1380
  30.3 0.9 reduce-precision_convert_fusion.2
  31.4 0.2 fusion.59
  31.6 1.9 %reduce-precision_convert_fusion.1 = (bf16[576,32]{1,0:T(8,128)(2,1)S(1)}, f32[576,32]{1,0:T(8,128)S(1)}) fusion(f32[576]{0:T(1024)S(1)} %broadcast_in_dim.1348, pred[64,32]{1,0:T(8,128)(4,1)S(1)} %get-tuple-element.128, f32[576]{0:T(1024)S(1)} %broadcast_in_dim.1343, pred[64,32]{1,0:T(8,128)(4,1)S(1)} %get-tuple-element.129, ...), kind=kLoop, calls=%fused_computation.17 | loop fusion | flops 423936 | bytes 201984 | tf_op jit(solution)/shard_map/convert_element_type | solution.py:587
  33.5 0.2 slice_reduce_fusion.1
  33.7 0.5 slice_reduce_fusion.20
  34.2 0.1 pad_maximum_fusion.down_ref
  34.4 0.2 fusion.38
  34.6 1.5 fusion.10
  36.2 1.2 fusion.1.across_ref
  37.4 2.6 %convolution_bitcast_fusion.coef_ref = f32[8,9,4864]{2,1,0:T(8,128)} fusion(s32[4864]{0:T(1024)S(1)} %pad_bitcast_fusion.2, f32[8,1,9,32]{3,1,2,0:T(1,128)S(1)} %copy-done.7), kind=kOutput, calls=%fused_computation | convolution fusion | flops 134635520 | bytes 1429504 | tf_op jit(solution)/shard_map/qbg,gx->qbx/dot_general | solution.py:628
  39.9 0.8 pad_maximum_fusion.1.down_ref
  40.7 4.1 %pack_rows.2 = f32[32,3,64,128]{3,2,1,0:T(8,128)} custom-call(s32[8,32]{1,0:T(8,128)} %places_ref.3, f32[8,1024,128]{2,1,0:T(8,128)} %bitcast.160), custom_call_target="tpu_custom_call" | custom-call | bytes 9437184 | tf_op jit(solution)/shard_map/pack_rows/pallas_call | solution.py:39
  44.8 1.2 slice.204
  48.7 0.3 pad.32.shift_ref
  49.1 1.4 pad.31.taps_ref
  50.5 0.6 dynamic_slice.3.weight_ref
  51.1 28.3 %collective-permute-done = f32[6400]{0:T(1024)S(1)} collective-permute-done((f32[6400]{0:T(1024)S(1)}, f32[6400]{0:T(1024)S(1)}, u32[]{:S(2)}, u32[]{:S(2)}) %collective-permute-start) | collective-permute-done | bytes 25632 | tf_op jit(solution)/shard_map/ppermute | solution.py:669
  79.3 10.3 %all-to-all-start.1 = ((f32[32,3,64,128]{3,2,1,0:T(8,128)}), f32[32,3,64,128]{3,2,1,0:T(8,128)}, u32[]{:S(2)}, u32[]{:S(2)}) async-start(f32[32,3,64,128]{3,2,1,0:T(8,128)} %pack_rows.2), calls=%async_computation.1 | async-start | bytes 6291456 | tf_op jit(solution)/shard_map/all_to_all | solution.py:675
  89.8 0.1 reshape.1383
  90.0 0.1 reshape.1385
  90.1 2.5 %fusion.5.coef_up_ref = f32[8,9,4864]{2,1,0:T(8,128)} fusion(f32[8,9,32]{2,1,0:T(8,128)S(1)} %reshape.1382, s32[4864]{0:T(1024)S(1)} %pad_bitcast_fusion.1), kind=kOutput, calls=%fused_computation.11 | convolution fusion | flops 134635520 | bytes 1429504 | tf_op jit(solution)/shard_map/qbg,gx->qbx/dot_general | solution.py:628
  92.7 2.6 %fusion.8.coef_dn_ref = f32[8,9,4864]{2,1,0:T(8,128)} fusion(f32[8,9,32]{2,1,0:T(8,128)S(1)} %reshape.1384, s32[4864]{0:T(1024)S(1)} %pad_bitcast_fusion), kind=kOutput, calls=%fused_computation.13 | convolution fusion | flops 134635520 | bytes 1429504 | tf_op jit(solution)/shard_map/qbg,gx->qbx/dot_general | solution.py:628
  95.3 9.4 %warp_rows.2 = (f32[5,32,4224]{2,1,0:T(8,128)}, f32[5,8,5376]{2,1,0:T(8,128)}, f32[5,8,5376]{2,1,0:T(8,128)}) custom-call(s32[1]{0:T(128)} %bitcast.53.turn_ref, f32[32,5,64,128]{3,2,1,0:T(8,128)} %all-to-all-done.got_ref, f32[8,8,4224]{2,1,0:T(8,128)} %pad.31.taps_ref, s32[8,1,4224]{2,1,0:T(1,128)S(1)} %pad.32.shift_ref), custom_call_target="tpu_custom_call" | custom-call | bytes 62914560 | tf_op jit(solution)/shard_map/warp_rows/pallas_call | solution.py:146
  104.7 27.1 %spread_rows.1 = (f32[8,32,4096]{2,1,0:T(8,128)}, f32[32,4096]{1,0:T(8,128)}, f32[5,8,5120]{2,1,0:T(8,128)}, f32[5,8,5120]{2,1,0:T(8,128)}) custom-call(f32[8]{0:T(128)} %dynamic_slice.3.weight_ref, f32[5,32,4224]{2,1,0:T(8,128)} %get-tuple-element.34.warped_ref, bf16[576,96]{1,0:T(8,128)(2,1)} %pad_maximum_fusion.1.down_ref, ...), custom_call_target="tpu_custom_call" | custom-call | bytes 125829120 | tf_op jit(solution)/shard_map/spread_rows/pallas_call | solution.py:379
  131.9 2.2 %collective-permute-start.2 = (f32[5,8,5120]{2,1,0:T(8,128)}, f32[5,8,5120]{2,1,0:T(8,128)S(1)}, u32[]{:S(2)}, u32[]{:S(2)}) collective-permute-start(f32[5,8,5120]{2,1,0:T(8,128)} %get-tuple-element.40), channel_id=1, source_target_pairs={{0,4},{4,8},{8,12},{12,16},{16,20},{20,24},{24,28},{28,32},{32,36}... | collective-permute-start | bytes 2457608 | tf_op jit(solution)/shard_map/ppermute | solution.py:691
  134.1 5.6 %collective-permute-start.3 = (f32[5,8,5120]{2,1,0:T(8,128)}, f32[5,8,5120]{2,1,0:T(8,128)}, u32[]{:S(2)}, u32[]{:S(2)}) collective-permute-start(f32[5,8,5120]{2,1,0:T(8,128)} %get-tuple-element.41), channel_id=1, source_target_pairs={{4,0},{8,4},{12,8},{16,12},{20,16},{24,20},{28,24},{32,28},{36,32}... | collective-permute-start | bytes 2457608 | tf_op jit(solution)/shard_map/ppermute | solution.py:692
  139.7 6.8 %warp_rows.3 = (f32[3,32,4224]{2,1,0:T(8,128)}, f32[3,8,5376]{2,1,0:T(8,128)S(1)}, f32[3,8,5376]{2,1,0:T(8,128)}) custom-call(s32[1]{0:T(128)} %bitcast.53.turn_ref, f32[32,3,64,128]{3,2,1,0:T(8,128)} %all-to-all-done.1.got_ref, f32[8,8,4224]{2,1,0:T(8,128)} %pad.31.taps_ref, s32[8,1,4224]{2,1,0:T(1,128)S(1)} %pad.32.shift_ref), custom_call_target="tpu_custom_call" | custom-call | bytes 37748736 | tf_op jit(solution)/shard_map/warp_rows/pallas_call | solution.py:146
  146.5 1.9 %collective-permute-start.4 = (f32[3,8,5376]{2,1,0:T(8,128)}, f32[3,8,5376]{2,1,0:T(8,128)S(1)}, u32[]{:S(2)}, u32[]{:S(2)}) collective-permute-start(f32[3,8,5376]{2,1,0:T(8,128)} %get-tuple-element.47), channel_id=1, source_target_pairs={{0,4},{4,8},{8,12},{12,16},{16,20},{20,24},{24,28},{28,32},{32,36}... | collective-permute-start | bytes 1548296 | tf_op jit(solution)/shard_map/ppermute | solution.py:695
  148.4 6.0 %collective-permute-start.5 = (f32[3,8,5376]{2,1,0:T(8,128)S(1)}, f32[3,8,5376]{2,1,0:T(8,128)S(1)}, u32[]{:S(2)}, u32[]{:S(2)}) collective-permute-start(f32[3,8,5376]{2,1,0:T(8,128)S(1)} %get-tuple-element.48), channel_id=1, source_target_pairs={{4,0},{8,4},{12,8},{16,12},{20,16},{24,20},{28,24},{32,28},{36,32}... | collective-permute-start | bytes 1548296 | tf_op jit(solution)/shard_map/ppermute | solution.py:696
  154.4 0.7 reduce_sum.9
  155.1 5.4 %add_edges.1 = (f32[8,32,4096]{2,1,0:T(8,128)}, f32[32,4096]{1,0:T(8,128)S(1)}) custom-call(f32[8]{0:T(128)S(1)} %copy-done.3, f32[5,8,5120]{2,1,0:T(8,128)S(1)} %collective-permute-done.2.above_ref, f32[5,8,5120]{2,1,0:T(8,128)} %collective-permute-done.3.below_ref, f32[8,32,4096]{2,1,0:T(8,128)} %get-tuple-element.52.before_ref, ...), custom_call_target="tpu_custom_call", output_to_operand_aliasing={{0}: (3, {})} | custom-call | bytes 15728640 | tf_op jit(solution)/shard_map/add_edges/pallas_call | solution.py:451
  160.4 0.3 collective-permute-done.5.below_ref
  160.7 10.4 %match_rows.1 = (f32[8,32,4096]{2,1,0:T(8,128)}, f32[32,4096]{1,0:T(8,128)S(1)}) custom-call(f32[8]{0:T(128)S(1)} %copy-done.3, f32[3,32,4224]{2,1,0:T(8,128)} %get-tuple-element.46.warped_ref, f32[3,8,5376]{2,1,0:T(8,128)S(1)} %collective-permute-done.4.above_ref, ...), custom_call_target="tpu_custom_call", output_to_operand_aliasing={{0}: (9, {})} | custom-call | bytes 62914560 | tf_op jit(solution)/shard_map/match_rows/pallas_call | solution.py:496
  171.2 9.4 %sum_visits.1 = f32[8,4096]{1,0:T(8,128)S(1)} custom-call(f32[32,4096]{1,0:T(8,128)S(1)} %get-tuple-element.57.total_ref, f32[1]{0:T(128)} %bitcast.60.scale_ref), custom_call_target="tpu_custom_call" | custom-call | tf_op jit(solution)/shard_map/sum_visits/pallas_call | solution.py:565
  180.5 0.7 copy.26
  (118 shorter events, 5.1 us)
Async XLA Ops:
  6.4 8.8 %copy-start.9 = (s32[1,4096]{1,0:T(1,128)S(1)}, s32[1,4096]{1,0:T(1,128)}, u32[]{:S(2)}) copy-start(s32[1,4096]{1,0:T(1,128)} %param.17) | copy-start | bytes 49156
  6.4 8.8 %copy-start.7 = (f32[8,1,9,32]{3,1,2,0:T(1,128)S(1)}, f32[8,1,9,32]{3,1,2,0:T(1,128)}, u32[]{:S(2)}) copy-start(f32[8,1,9,32]{3,1,2,0:T(1,128)} %param.16) | copy-start | bytes 27652
  6.4 16.7 %copy-start.4 = (f32[9,21]{1,0:T(8,128)S(1)}, f32[9,21]{1,0:T(8,128)}, u32[]{:S(2)}) copy-start(f32[9,21]{1,0:T(8,128)} %param.14) | copy-start | bytes 2272
  6.4 72.9 %all-to-all-start = ((f32[32,5,64,128]{3,2,1,0:T(8,128)}), f32[32,5,64,128]{3,2,1,0:T(8,128)}, u32[]{:S(2)}, u32[]{:S(2)}) async-start(f32[32,5,64,128]{3,2,1,0:T(8,128)} %pack_rows.3), calls=%async_computation | async-start | bytes 10485760 | tf_op jit(solution)/shard_map/all_to_all | solution.py:675
  15.2 18.3 %copy-start.5 = (f32[9,21]{1,0:T(8,128)S(1)}, f32[9,21]{1,0:T(8,128)}, u32[]{:S(2)}) copy-start(f32[9,21]{1,0:T(8,128)} %param.15) | copy-start | bytes 2272
  15.4 63.9 %collective-permute-start = (f32[6400]{0:T(1024)S(1)}, f32[6400]{0:T(1024)S(1)}, u32[]{:S(2)}, u32[]{:S(2)}) collective-permute-start(f32[6400]{0:T(1024)S(1)} %pad_maximum_fusion.2), channel_id=1, source_target_pairs={{0,4},{4,8},{8,12},{12,16},{16,20},{20,24},{24,28},{28,32},{32,36}... | collective-permute-start | bytes 76808 | tf_op jit(solution)/shard_map/ppermute | solution.py:669
  17.5 61.9 %collective-permute-start.1 = (f32[6400]{0:T(1024)S(1)}, f32[6400]{0:T(1024)S(1)}, u32[]{:S(2)}, u32[]{:S(2)}) collective-permute-start(f32[6400]{0:T(1024)S(1)} %pad_maximum_fusion.2), channel_id=1, source_target_pairs={{4,0},{8,4},{12,8},{16,12},{20,16},{24,20},{28,24},{32,28},{36,32}... | collective-permute-start | bytes 76808 | tf_op jit(solution)/shard_map/ppermute | solution.py:669
  40.7 8.0 %copy-start.8 = (s32[8,1,4096]{2,1,0:T(1,128)S(1)}, s32[8,1,4096]{2,1,0:T(1,128)}, u32[]{:S(2)}) copy-start(s32[8,1,4096]{2,1,0:T(1,128)} %param.13) | copy-start | bytes 393220
  40.7 8.3 %copy-start.6 = (f32[8,1,8,4096]{3,2,1,0:T(8,128)S(1)}, f32[8,1,8,4096]{3,2,1,0:T(8,128)}, u32[]{:S(2)}) copy-start(f32[8,1,8,4096]{3,2,1,0:T(8,128)} %param.12) | copy-start | bytes 3145732
  44.8 5.6 %copy-start.10 = (f32[32]{0:T(128)S(1)}, f32[32]{0:T(128)}, u32[]{:S(2)}) copy-start(f32[32]{0:T(128)} %param.19) | copy-start | bytes 388
  79.3 60.3 %all-to-all-start.1 = ((f32[32,3,64,128]{3,2,1,0:T(8,128)}), f32[32,3,64,128]{3,2,1,0:T(8,128)}, u32[]{:S(2)}, u32[]{:S(2)}) async-start(f32[32,3,64,128]{3,2,1,0:T(8,128)} %pack_rows.2), calls=%async_computation.1 | async-start | bytes 6291456 | tf_op jit(solution)/shard_map/all_to_all | solution.py:675
  131.8 23.2 %copy-start.2 = (f32[32,4096]{1,0:T(8,128)S(1)}, f32[32,4096]{1,0:T(8,128)}, u32[]{:S(2)}) copy-start(f32[32,4096]{1,0:T(8,128)} %get-tuple-element.53.sums_ref) | copy-start | bytes 1572868
  131.8 23.2 %copy-start.3 = (f32[8]{0:T(128)S(1)}, f32[8]{0:T(128)}, u32[]{:S(2)}) copy-start(f32[8]{0:T(128)} %dynamic_slice.3.weight_ref) | copy-start | bytes 100
  131.9 23.2 %collective-permute-start.2 = (f32[5,8,5120]{2,1,0:T(8,128)}, f32[5,8,5120]{2,1,0:T(8,128)S(1)}, u32[]{:S(2)}, u32[]{:S(2)}) collective-permute-start(f32[5,8,5120]{2,1,0:T(8,128)} %get-tuple-element.40), channel_id=1, source_target_pairs={{0,4},{4,8},{8,12},{12,16},{16,20},{20,24},{24,28},{28,32},{32,36}... | collective-permute-start | bytes 2457608 | tf_op jit(solution)/shard_map/ppermute | solution.py:691
  134.1 21.0 %collective-permute-start.3 = (f32[5,8,5120]{2,1,0:T(8,128)}, f32[5,8,5120]{2,1,0:T(8,128)}, u32[]{:S(2)}, u32[]{:S(2)}) collective-permute-start(f32[5,8,5120]{2,1,0:T(8,128)} %get-tuple-element.41), channel_id=1, source_target_pairs={{4,0},{8,4},{12,8},{16,12},{20,16},{24,20},{28,24},{32,28},{36,32}... | collective-permute-start | bytes 2457608 | tf_op jit(solution)/shard_map/ppermute | solution.py:692
  146.5 14.0 %collective-permute-start.4 = (f32[3,8,5376]{2,1,0:T(8,128)}, f32[3,8,5376]{2,1,0:T(8,128)S(1)}, u32[]{:S(2)}, u32[]{:S(2)}) collective-permute-start(f32[3,8,5376]{2,1,0:T(8,128)} %get-tuple-element.47), channel_id=1, source_target_pairs={{0,4},{4,8},{8,12},{12,16},{16,20},{20,24},{24,28},{28,32},{32,36}... | collective-permute-start | bytes 1548296 | tf_op jit(solution)/shard_map/ppermute | solution.py:695
  148.4 12.3 %collective-permute-start.5 = (f32[3,8,5376]{2,1,0:T(8,128)S(1)}, f32[3,8,5376]{2,1,0:T(8,128)S(1)}, u32[]{:S(2)}, u32[]{:S(2)}) collective-permute-start(f32[3,8,5376]{2,1,0:T(8,128)S(1)} %get-tuple-element.48), channel_id=1, source_target_pairs={{4,0},{8,4},{12,8},{16,12},{20,16},{24,20},{28,24},{32,28},{36,32}... | collective-permute-start | bytes 1548296 | tf_op jit(solution)/shard_map/ppermute | solution.py:696
  155.0 5.7 %copy-start = (bf16[9,256,256]{2,1,0:T(8,128)(2,1)S(1)}, bf16[9,256,256]{2,1,0:T(8,128)(2,1)}, u32[]{:S(2)}) copy-start(bf16[9,256,256]{2,1,0:T(8,128)(2,1)} %fusion.1.across_ref) | copy-start | bytes 3538948
  155.1 5.7 %copy-start.1 = (f32[32,4096]{1,0:T(8,128)S(1)}, f32[32,4096]{1,0:T(8,128)}, u32[]{:S(2)}) copy-start(f32[32,4096]{1,0:T(8,128)} %template_ref.3) | copy-start | bytes 1572868

commit v8 on v7

--- a/solution.py
+++ b/solution.py
@@ -12,7 +12,7 @@
 step = 108
 parts = 2
 whole = 58 << 20
-chunks = (5, 3)
+chunks = (4, 4)
 bf16 = jnp.bfloat16
 
 
@@ -692,9 +692,11 @@
     from_below = lax.ppermute(up, "patch", up_pairs)
     turn, total = lax.optimization_barrier((turn, total))
     warped, head, tail = warp_rows(early, late, turn, got[1], taps, shift, patch_rows)
+    head, tail, from_above, from_below = lax.optimization_barrier(
+        (head, tail, from_above, from_below)
+    )
     above = lax.ppermute(tail, "patch", down_pairs)
     below = lax.ppermute(head, "patch", up_pairs)
-    from_above, from_below, warped = lax.optimization_barrier((from_above, from_below, warped))
     difference, total = add_edges(weights, from_above, from_below, difference, total)
     difference, total = match_rows(
         early, weights, warped, above, below, down, across, coefs, template, total, difference

time: 182 us -> 177 us (0.973)
  waiting for transfers between devices: 28.6 us -> 24.3 us
  Pallas kernels: 78.4 us -> 75.9 us
    ppermute x2, waiting for transfers between devices: 28.3 us -> 14.4 us  [on_device(): lax.ppermute(packed, 'patch', pairs)]
    all_to_all x2, waiting for transfers between devices: 0.01 us -> 6.55 us  [on_device(): lax.all_to_all(block, 'patch', split_axis=0, concat_axis=0, tiled=True)]
    pallas_call x1, Pallas kernels: 27.1 us -> 22.3 us  [spread_rows(): pl.pallas_call(spread_kernel, out_shape=(jax.ShapeDtypeStruct((visits, pa...]
    pallas_call x1, Pallas kernels: 10.4 us -> 13.6 us  [match_rows(): pl.pallas_call(body, out_shape=(jax.ShapeDtypeStruct((visits, patch_rows,...]
    all_to_all x2, starting transfers between devices: 19 us -> 17.2 us  [on_device(): lax.all_to_all(block, 'patch', split_axis=0, concat_axis=0, tiled=True)]
  transfers between devices with their start and end apart: 8 -> 8, of which waited for: 2 -> 4; matrix products, arithmetic and copies ran while one was open for 15% -> 16% of each run, Pallas kernels for 29% -> 27%
where the time goes in v8:
time: 177 us; the launch traced here: 175 us
  Pallas kernels  75.9 us (43%)
  starting transfers between devices  42.1 us (24%)
  waiting for transfers between devices  24.3 us (14%)
  local copies, waits for them, and re-layouts  13.3 us (8%)
  other arithmetic  7.92 us (4%)
  matrix products  7.68 us (4%)
  between operations  3.76 us (2%)
    pallas_call x1, Pallas kernels, spread_rows(): pl.pallas_call(spread_kernel, out_shape=(jax.ShapeDtypeStruct((visits, pa...  22.3 us
    all_to_all x2, starting transfers between devices, on_device(): lax.all_to_all(block, 'patch', split_axis=0, concat_axis=0, tiled=True)  17.2 us
    pallas_call x2, Pallas kernels, warp_rows(): pl.pallas_call(functools.partial(warp_kernel, first), out_shape=(jax.Shap...  16.2 us
    ppermute x2, waiting for transfers between devices, on_device(): lax.ppermute(packed, 'patch', pairs)  14.4 us
    pallas_call x1, Pallas kernels, match_rows(): pl.pallas_call(body, out_shape=(jax.ShapeDtypeStruct((visits, patch_rows,...  13.6 us
    pallas_call x1, Pallas kernels, sum_visits(): pl.pallas_call(sum_kernel, out_shape=jax.ShapeDtypeStruct(shape, jnp.floa...  10.3 us
    pallas_call x2, Pallas kernels, pack_rows(): pl.pallas_call(functools.partial(pack_kernel, first), out_shape=jax.Shape...  9.26 us
    dot_general x3, matrix products, windowed_coefs(): jnp.einsum('qbg,gx->qbx', table, one_hot, precision=lax.Precision.HIGHEST)  7.68 us
  transfers between devices with their start and end apart: 8, of which 4 were waited for; matrix products, arithmetic and copies ran while one was open for 16% of the time, Pallas kernels for 27%

profile of v8, /device:TPU:8, one launch (start us, length us, event | category | flops | bytes accessed | tf_op | source)
XLA Modules:
  0.0 174.9 jit_solution(13636156640776441398)
XLA Ops:
  0.6 4.6 %pack_rows.3 = f32[32,4,64,128]{3,2,1,0:T(8,128)} custom-call(s32[8,32]{1,0:T(8,128)} %places_ref.3, f32[8,1024,128]{2,1,0:T(8,128)} %bitcast.159), custom_call_target="tpu_custom_call" | custom-call | bytes 12582912 | tf_op jit(solution)/shard_map/pack_rows/pallas_call | solution.py:39
  5.2 8.8 %all-to-all-start = ((f32[32,4,64,128]{3,2,1,0:T(8,128)}), f32[32,4,64,128]{3,2,1,0:T(8,128)}, u32[]{:S(2)}, u32[]{:S(2)}) async-start(f32[32,4,64,128]{3,2,1,0:T(8,128)} %pack_rows.3), calls=%async_computation | async-start | bytes 8388608 | tf_op jit(solution)/shard_map/all_to_all | solution.py:675
  14.0 0.1 reduce.42
  14.2 2.1 %collective-permute-start = (f32[6400]{0:T(1024)S(1)}, f32[6400]{0:T(1024)S(1)}, u32[]{:S(2)}, u32[]{:S(2)}) collective-permute-start(f32[6400]{0:T(1024)S(1)} %pad_maximum_fusion.2), channel_id=1, source_target_pairs={{0,4},{4,8},{8,12},{12,16},{16,20},{20,24},{24,28},{28,32},{32,36}... | collective-permute-start | bytes 76808 | tf_op jit(solution)/shard_map/ppermute | solution.py:669
  16.3 5.6 %collective-permute-start.1 = (f32[6400]{0:T(1024)S(1)}, f32[6400]{0:T(1024)S(1)}, u32[]{:S(2)}, u32[]{:S(2)}) collective-permute-start(f32[6400]{0:T(1024)S(1)} %pad_maximum_fusion.2), channel_id=1, source_target_pairs={{4,0},{8,4},{12,8},{16,12},{20,16},{24,20},{28,24},{32,28},{36,32}... | collective-permute-start | bytes 76808 | tf_op jit(solution)/shard_map/ppermute | solution.py:669
  21.9 0.2 slice_reduce_fusion.22
  22.2 0.1 broadcast_in_dim.1242
  22.3 0.1 broadcast_in_dim.1236
  22.4 0.5 slice_reduce_fusion.41
  23.0 0.1 broadcast_in_dim.1230
  23.1 0.1 broadcast_in_dim.1224
  23.3 0.1 broadcast_in_dim.1218
  23.4 0.1 broadcast_in_dim.1212
  23.6 0.1 broadcast_in_dim.1206
  23.8 0.1 broadcast_in_dim.1200
  23.9 0.1 broadcast_in_dim.1194
  24.1 0.1 broadcast_in_dim.1188
  24.2 0.1 broadcast_in_dim.1182
  24.4 0.1 broadcast_in_dim.1176
  24.5 0.1 broadcast_in_dim.1170
  24.7 0.1 broadcast_in_dim.1164
  24.8 0.1 broadcast_in_dim.1158
  25.0 0.1 broadcast_in_dim.1152
  25.1 0.1 broadcast_in_dim.1146
  25.4 0.1 broadcast_in_dim.1134
  28.8 0.2 reshape.1380
  29.2 0.9 reduce-precision_convert_fusion.2
  30.2 0.2 fusion.59
  30.4 1.9 %reduce-precision_convert_fusion.1 = (bf16[576,32]{1,0:T(8,128)(2,1)S(1)}, f32[576,32]{1,0:T(8,128)S(1)}) fusion(f32[576]{0:T(1024)S(1)} %broadcast_in_dim.1348, pred[64,32]{1,0:T(8,128)(4,1)S(1)} %get-tuple-element.130, f32[576]{0:T(1024)S(1)} %broadcast_in_dim.1343, pred[64,32]{1,0:T(8,128)(4,1)S(1)} %get-tuple-element.131, ...), kind=kLoop, calls=%fused_computation.17 | loop fusion | flops 423936 | bytes 201984 | tf_op jit(solution)/shard_map/convert_element_type | solution.py:587
  32.3 0.2 slice_reduce_fusion.1
  32.5 0.5 slice_reduce_fusion.20
  33.1 0.1 pad_maximum_fusion.down_ref
  33.2 0.2 fusion.38
  33.4 1.5 fusion.10
  35.0 1.2 fusion.1.across_ref
  36.2 2.6 %convolution_bitcast_fusion.coef_ref = f32[8,9,4864]{2,1,0:T(8,128)} fusion(s32[4864]{0:T(1024)S(1)} %pad_bitcast_fusion.2, f32[8,1,9,32]{3,1,2,0:T(1,128)S(1)} %copy-done.7), kind=kOutput, calls=%fused_computation | convolution fusion | flops 134635520 | bytes 1429504 | tf_op jit(solution)/shard_map/qbg,gx->qbx/dot_general | solution.py:628
  38.8 0.8 pad_maximum_fusion.1.down_ref
  39.6 4.7 %pack_rows.2 = f32[32,4,64,128]{3,2,1,0:T(8,128)} custom-call(s32[8,32]{1,0:T(8,128)} %places_ref.3, f32[8,1024,128]{2,1,0:T(8,128)} %bitcast.160), custom_call_target="tpu_custom_call" | custom-call | bytes 12582912 | tf_op jit(solution)/shard_map/pack_rows/pallas_call | solution.py:39
  44.3 1.2 slice.204
  48.2 0.3 pad.32.shift_ref
  48.5 1.3 pad.31.taps_ref
  49.9 0.6 dynamic_slice.3.weight_ref
  50.5 14.4 %collective-permute-done = f32[6400]{0:T(1024)S(1)} collective-permute-done((f32[6400]{0:T(1024)S(1)}, f32[6400]{0:T(1024)S(1)}, u32[]{:S(2)}, u32[]{:S(2)}) %collective-permute-start) | collective-permute-done | bytes 25632 | tf_op jit(solution)/shard_map/ppermute | solution.py:669
  64.9 8.5 %all-to-all-start.1 = ((f32[32,4,64,128]{3,2,1,0:T(8,128)}), f32[32,4,64,128]{3,2,1,0:T(8,128)}, u32[]{:S(2)}, u32[]{:S(2)}) async-start(f32[32,4,64,128]{3,2,1,0:T(8,128)} %pack_rows.2), calls=%async_computation.1 | async-start | bytes 8388608 | tf_op jit(solution)/shard_map/all_to_all | solution.py:675
  73.5 0.1 reshape.1383
  73.7 0.1 reshape.1385
  73.9 2.5 %fusion.5.coef_up_ref = f32[8,9,4864]{2,1,0:T(8,128)} fusion(f32[8,9,32]{2,1,0:T(8,128)S(1)} %reshape.1382, s32[4864]{0:T(1024)S(1)} %pad_bitcast_fusion.1), kind=kOutput, calls=%fused_computation.11 | convolution fusion | flops 134635520 | bytes 1429504 | tf_op jit(solution)/shard_map/qbg,gx->qbx/dot_general | solution.py:628
  76.4 2.6 %fusion.8.coef_dn_ref = f32[8,9,4864]{2,1,0:T(8,128)} fusion(f32[8,9,32]{2,1,0:T(8,128)S(1)} %reshape.1384, s32[4864]{0:T(1024)S(1)} %pad_bitcast_fusion), kind=kOutput, calls=%fused_computation.13 | convolution fusion | flops 134635520 | bytes 1429504 | tf_op jit(solution)/shard_map/qbg,gx->qbx/dot_general | solution.py:628
  79.0 8.1 %warp_rows.2 = (f32[4,32,4224]{2,1,0:T(8,128)}, f32[4,8,5376]{2,1,0:T(8,128)}, f32[4,8,5376]{2,1,0:T(8,128)}) custom-call(s32[1]{0:T(128)} %bitcast.53.turn_ref, f32[32,4,64,128]{3,2,1,0:T(8,128)} %all-to-all-done.got_ref, f32[8,8,4224]{2,1,0:T(8,128)} %pad.31.taps_ref, s32[8,1,4224]{2,1,0:T(1,128)S(1)} %pad.32.shift_ref), custom_call_target="tpu_custom_call" | custom-call | bytes 50331648 | tf_op jit(solution)/shard_map/warp_rows/pallas_call | solution.py:146
  87.1 22.3 %spread_rows.1 = (f32[8,32,4096]{2,1,0:T(8,128)}, f32[32,4096]{1,0:T(8,128)}, f32[4,8,5120]{2,1,0:T(8,128)}, f32[4,8,5120]{2,1,0:T(8,128)}) custom-call(f32[8]{0:T(128)} %dynamic_slice.3.weight_ref, f32[4,32,4224]{2,1,0:T(8,128)} %get-tuple-element.35.warped_ref, bf16[576,96]{1,0:T(8,128)(2,1)} %pad_maximum_fusion.1.down_ref, ...), custom_call_target="tpu_custom_call" | custom-call | bytes 100663296 | tf_op jit(solution)/shard_map/spread_rows/pallas_call | solution.py:379
  109.4 2.0 %collective-permute-start.2 = (f32[4,8,5120]{2,1,0:T(8,128)}, f32[4,8,5120]{2,1,0:T(8,128)S(1)}, u32[]{:S(2)}, u32[]{:S(2)}) collective-permute-start(f32[4,8,5120]{2,1,0:T(8,128)} %get-tuple-element.47), channel_id=1, source_target_pairs={{0,4},{4,8},{8,12},{12,16},{16,20},{20,24},{24,28},{28,32},{32,36}... | collective-permute-start | bytes 1966088 | tf_op jit(solution)/shard_map/ppermute | solution.py:691
  111.4 5.6 %collective-permute-start.3 = (f32[4,8,5120]{2,1,0:T(8,128)}, f32[4,8,5120]{2,1,0:T(8,128)S(1)}, u32[]{:S(2)}, u32[]{:S(2)}) collective-permute-start(f32[4,8,5120]{2,1,0:T(8,128)} %get-tuple-element.48), channel_id=1, source_target_pairs={{4,0},{8,4},{12,8},{16,12},{20,16},{24,20},{28,24},{32,28},{36,32}... | collective-permute-start | bytes 1966088 | tf_op jit(solution)/shard_map/ppermute | solution.py:692
  117.1 6.5 %all-to-all-done.1.got_ref = f32[32,4,64,128]{3,2,1,0:T(8,128)} async-done(((f32[32,4,64,128]{3,2,1,0:T(8,128)}), f32[32,4,64,128]{3,2,1,0:T(8,128)}, u32[]{:S(2)}, u32[]{:S(2)}) %all-to-all-start.1) | async-done | bytes 4194336 | tf_op jit(solution)/shard_map/all_to_all | solution.py:675
  123.6 8.1 %warp_rows.3 = (f32[4,32,4224]{2,1,0:T(8,128)}, f32[4,8,5376]{2,1,0:T(8,128)S(1)}, f32[4,8,5376]{2,1,0:T(8,128)}) custom-call(s32[1]{0:T(128)} %bitcast.53.turn_ref, f32[32,4,64,128]{3,2,1,0:T(8,128)} %all-to-all-done.1.got_ref, f32[8,8,4224]{2,1,0:T(8,128)} %pad.31.taps_ref, s32[8,1,4224]{2,1,0:T(1,128)S(1)} %pad.32.shift_ref), custom_call_target="tpu_custom_call" | custom-call | bytes 50331648 | tf_op jit(solution)/shard_map/warp_rows/pallas_call | solution.py:146
  131.7 0.8 copy-done.6
  132.5 1.9 %collective-permute-start.4 = (f32[4,8,5376]{2,1,0:T(8,128)}, f32[4,8,5376]{2,1,0:T(8,128)S(1)}, u32[]{:S(2)}, u32[]{:S(2)}) collective-permute-start(f32[4,8,5376]{2,1,0:T(8,128)} %get-tuple-element.49), channel_id=1, source_target_pairs={{0,4},{4,8},{8,12},{12,16},{16,20},{20,24},{24,28},{28,32},{32,36}... | collective-permute-start | bytes 2064392 | tf_op jit(solution)/shard_map/ppermute | solution.py:698
  134.4 7.6 %collective-permute-start.5 = (f32[4,8,5376]{2,1,0:T(8,128)S(1)}, f32[4,8,5376]{2,1,0:T(8,128)S(1)}, u32[]{:S(2)}, u32[]{:S(2)}) collective-permute-start(f32[4,8,5376]{2,1,0:T(8,128)S(1)} %get-tuple-element.50), channel_id=1, source_target_pairs={{4,0},{8,4},{12,8},{16,12},{20,16},{24,20},{28,24},{32,28},{36,32}... | collective-permute-start | bytes 2064392 | tf_op jit(solution)/shard_map/ppermute | solution.py:699
  142.1 0.7 reduce_sum.9
  142.7 4.2 %add_edges.1 = (f32[8,32,4096]{2,1,0:T(8,128)}, f32[32,4096]{1,0:T(8,128)S(1)}) custom-call(f32[8]{0:T(128)S(1)} %copy-done.2, f32[4,8,5120]{2,1,0:T(8,128)S(1)} %collective-permute-done.2.above_ref, f32[4,8,5120]{2,1,0:T(8,128)} %copy-done.6, f32[8,32,4096]{2,1,0:T(8,128)} %get-tuple-element.54.before_ref, ...), custom_call_target="tpu_custom_call", output_to_operand_aliasing={{0}: (3, {})} | custom-call | bytes 12582912 | tf_op jit(solution)/shard_map/add_edges/pallas_call | solution.py:451
  147.0 1.7 %collective-permute-done.4.above_ref = f32[4,8,5376]{2,1,0:T(8,128)S(1)} collective-permute-done((f32[4,8,5376]{2,1,0:T(8,128)}, f32[4,8,5376]{2,1,0:T(8,128)S(1)}, u32[]{:S(2)}, u32[]{:S(2)}) %collective-permute-start.4) | collective-permute-done | bytes 688160 | tf_op jit(solution)/shard_map/ppermute | solution.py:698
  148.7 1.5 collective-permute-done.5.below_ref
  150.3 13.6 %match_rows.1 = (f32[8,32,4096]{2,1,0:T(8,128)}, f32[32,4096]{1,0:T(8,128)S(1)}) custom-call(f32[8]{0:T(128)S(1)} %copy-done.2, f32[4,32,4224]{2,1,0:T(8,128)} %get-tuple-element.44.warped_ref, f32[4,8,5376]{2,1,0:T(8,128)S(1)} %collective-permute-done.4.above_ref, ...), custom_call_target="tpu_custom_call", output_to_operand_aliasing={{0}: (9, {})} | custom-call | bytes 83886080 | tf_op jit(solution)/shard_map/match_rows/pallas_call | solution.py:496
  163.9 10.3 %sum_visits.1 = f32[8,4096]{1,0:T(8,128)S(1)} custom-call(f32[32,4096]{1,0:T(8,128)S(1)} %get-tuple-element.59.total_ref, f32[1]{0:T(128)} %bitcast.60.scale_ref), custom_call_target="tpu_custom_call" | custom-call | tf_op jit(solution)/shard_map/sum_visits/pallas_call | solution.py:565
  174.2 0.7 copy.26
  (118 shorter events, 5.4 us)
Async XLA Ops:
  5.2 8.8 %copy-start.9 = (s32[1,4096]{1,0:T(1,128)S(1)}, s32[1,4096]{1,0:T(1,128)}, u32[]{:S(2)}) copy-start(s32[1,4096]{1,0:T(1,128)} %param.17) | copy-start | bytes 49156
  5.2 8.8 %copy-start.7 = (f32[8,1,9,32]{3,1,2,0:T(1,128)S(1)}, f32[8,1,9,32]{3,1,2,0:T(1,128)}, u32[]{:S(2)}) copy-start(f32[8,1,9,32]{3,1,2,0:T(1,128)} %param.16) | copy-start | bytes 27652
  5.2 16.7 %copy-start.3 = (f32[9,21]{1,0:T(8,128)S(1)}, f32[9,21]{1,0:T(8,128)}, u32[]{:S(2)}) copy-start(f32[9,21]{1,0:T(8,128)} %param.14) | copy-start | bytes 2272
  5.2 59.7 %all-to-all-start = ((f32[32,4,64,128]{3,2,1,0:T(8,128)}), f32[32,4,64,128]{3,2,1,0:T(8,128)}, u32[]{:S(2)}, u32[]{:S(2)}) async-start(f32[32,4,64,128]{3,2,1,0:T(8,128)} %pack_rows.3), calls=%async_computation | async-start | bytes 8388608 | tf_op jit(solution)/shard_map/all_to_all | solution.py:675
  14.0 18.3 %copy-start.4 = (f32[9,21]{1,0:T(8,128)S(1)}, f32[9,21]{1,0:T(8,128)}, u32[]{:S(2)}) copy-start(f32[9,21]{1,0:T(8,128)} %param.15) | copy-start | bytes 2272
  14.2 50.7 %collective-permute-start = (f32[6400]{0:T(1024)S(1)}, f32[6400]{0:T(1024)S(1)}, u32[]{:S(2)}, u32[]{:S(2)}) collective-permute-start(f32[6400]{0:T(1024)S(1)} %pad_maximum_fusion.2), channel_id=1, source_target_pairs={{0,4},{4,8},{8,12},{12,16},{16,20},{20,24},{24,28},{28,32},{32,36}... | collective-permute-start | bytes 76808 | tf_op jit(solution)/shard_map/ppermute | solution.py:669
  16.3 48.6 %collective-permute-start.1 = (f32[6400]{0:T(1024)S(1)}, f32[6400]{0:T(1024)S(1)}, u32[]{:S(2)}, u32[]{:S(2)}) collective-permute-start(f32[6400]{0:T(1024)S(1)} %pad_maximum_fusion.2), channel_id=1, source_target_pairs={{4,0},{8,4},{12,8},{16,12},{20,16},{24,20},{28,24},{32,28},{36,32}... | collective-permute-start | bytes 76808 | tf_op jit(solution)/shard_map/ppermute | solution.py:669
  39.6 8.5 %copy-start.8 = (s32[8,1,4096]{2,1,0:T(1,128)S(1)}, s32[8,1,4096]{2,1,0:T(1,128)}, u32[]{:S(2)}) copy-start(s32[8,1,4096]{2,1,0:T(1,128)} %param.13) | copy-start | bytes 393220
  39.6 8.9 %copy-start.5 = (f32[8,1,8,4096]{3,2,1,0:T(8,128)S(1)}, f32[8,1,8,4096]{3,2,1,0:T(8,128)}, u32[]{:S(2)}) copy-start(f32[8,1,8,4096]{3,2,1,0:T(8,128)} %param.12) | copy-start | bytes 3145732
  44.3 5.6 %copy-start.10 = (f32[32]{0:T(128)S(1)}, f32[32]{0:T(128)}, u32[]{:S(2)}) copy-start(f32[32]{0:T(128)} %param.19) | copy-start | bytes 388
  64.9 58.7 %all-to-all-start.1 = ((f32[32,4,64,128]{3,2,1,0:T(8,128)}), f32[32,4,64,128]{3,2,1,0:T(8,128)}, u32[]{:S(2)}, u32[]{:S(2)}) async-start(f32[32,4,64,128]{3,2,1,0:T(8,128)} %pack_rows.2), calls=%async_computation.1 | async-start | bytes 8388608 | tf_op jit(solution)/shard_map/all_to_all | solution.py:675
  109.4 22.3 %collective-permute-start.2 = (f32[4,8,5120]{2,1,0:T(8,128)}, f32[4,8,5120]{2,1,0:T(8,128)S(1)}, u32[]{:S(2)}, u32[]{:S(2)}) collective-permute-start(f32[4,8,5120]{2,1,0:T(8,128)} %get-tuple-element.47), channel_id=1, source_target_pairs={{0,4},{4,8},{8,12},{12,16},{16,20},{20,24},{24,28},{28,32},{32,36}... | collective-permute-start | bytes 1966088 | tf_op jit(solution)/shard_map/ppermute | solution.py:691
  111.4 20.3 %collective-permute-start.3 = (f32[4,8,5120]{2,1,0:T(8,128)}, f32[4,8,5120]{2,1,0:T(8,128)S(1)}, u32[]{:S(2)}, u32[]{:S(2)}) collective-permute-start(f32[4,8,5120]{2,1,0:T(8,128)} %get-tuple-element.48), channel_id=1, source_target_pairs={{4,0},{8,4},{12,8},{16,12},{20,16},{24,20},{28,24},{32,28},{36,32}... | collective-permute-start | bytes 1966088 | tf_op jit(solution)/shard_map/ppermute | solution.py:692
  117.0 25.7 %copy-start.1 = (f32[32,4096]{1,0:T(8,128)S(1)}, f32[32,4096]{1,0:T(8,128)}, u32[]{:S(2)}) copy-start(f32[32,4096]{1,0:T(8,128)} %get-tuple-element.55.sums_ref) | copy-start | bytes 1572868
  117.1 25.7 %copy-start.2 = (f32[8]{0:T(128)S(1)}, f32[8]{0:T(128)}, u32[]{:S(2)}) copy-start(f32[8]{0:T(128)} %dynamic_slice.3.weight_ref) | copy-start | bytes 100
  131.7 0.8 copy-start.6
  132.5 16.2 %collective-permute-start.4 = (f32[4,8,5376]{2,1,0:T(8,128)}, f32[4,8,5376]{2,1,0:T(8,128)S(1)}, u32[]{:S(2)}, u32[]{:S(2)}) collective-permute-start(f32[4,8,5376]{2,1,0:T(8,128)} %get-tuple-element.49), channel_id=1, source_target_pairs={{0,4},{4,8},{8,12},{12,16},{16,20},{20,24},{24,28},{28,32},{32,36}... | collective-permute-start | bytes 2064392 | tf_op jit(solution)/shard_map/ppermute | solution.py:698
  134.4 15.8 %collective-permute-start.5 = (f32[4,8,5376]{2,1,0:T(8,128)S(1)}, f32[4,8,5376]{2,1,0:T(8,128)S(1)}, u32[]{:S(2)}, u32[]{:S(2)}) collective-permute-start(f32[4,8,5376]{2,1,0:T(8,128)S(1)} %get-tuple-element.50), channel_id=1, source_target_pairs={{4,0},{8,4},{12,8},{16,12},{20,16},{24,20},{28,24},{32,28},{36,32}... | collective-permute-start | bytes 2064392 | tf_op jit(solution)/shard_map/ppermute | solution.py:699
  142.7 7.5 %copy-start = (f32[32,4096]{1,0:T(8,128)S(1)}, f32[32,4096]{1,0:T(8,128)}, u32[]{:S(2)}) copy-start(f32[32,4096]{1,0:T(8,128)} %template_ref.3) | copy-start | bytes 1572868

commit v9 on v8

--- a/solution.py
+++ b/solution.py
@@ -162,7 +162,7 @@
             pltpu.VMEM((2 * patch_rows, width + lane), bf16),
             pltpu.SemaphoreType.DMA((count,)),
         ],
-        compiler_params=pltpu.CompilerParams(vmem_limit_bytes=52 << 20),
+        compiler_params=pltpu.CompilerParams(vmem_limit_bytes=50 << 20),
         cost_estimate=pl.CostEstimate(flops=0, bytes_accessed=12 * count << 20, transcendentals=0),
         name="warp_rows",
     )(turn, got, taps, shift)
@@ -522,7 +522,7 @@
             pltpu.VMEM((span // lane * patch_rows, lane), jnp.float32),
         ],
         input_output_aliases=aliases,
-        compiler_params=pltpu.CompilerParams(vmem_limit_bytes=50 << 20),
+        compiler_params=pltpu.CompilerParams(vmem_limit_bytes=48 << 20),
         cost_estimate=pl.CostEstimate(flops=0, bytes_accessed=20 * count << 20, transcendentals=0),
         name="match_rows",
     )(weights, warped, above, below, down, across, coefs, template, before, *extra)

time: 177 us -> 175 us (0.989)
  waiting for transfers between devices: 24.3 us -> 26.6 us
  Pallas kernels: 75.9 us -> 73.8 us
  local copies, waits for them, and re-layouts: 13.3 us -> 11.5 us
    pallas_call x2, Pallas kernels: 16.2 us -> 14.3 us  [warp_rows(): pl.pallas_call(functools.partial(warp_kernel, first), out_shape=(jax.Shap...]
  transfers between devices with their start and end apart: 8 -> 8, of which waited for: 4 -> 5; matrix products, arithmetic and copies ran while one was open for 16% -> 15% of each run, Pallas kernels for 27% -> 26%
where the time goes in v9:
time: 175 us; the launch traced here: 173 us
  Pallas kernels  73.8 us (42%)
  starting transfers between devices  41.6 us (24%)
  waiting for transfers between devices  26.6 us (15%)
  local copies, waits for them, and re-layouts  11.5 us (7%)
  other arithmetic  7.87 us (4%)
  matrix products  7.68 us (4%)
  between operations  3.75 us (2%)
    pallas_call x1, Pallas kernels, spread_rows(): pl.pallas_call(spread_kernel, out_shape=(jax.ShapeDtypeStruct((visits, pa...  22.3 us
    all_to_all x2, starting transfers between devices, on_device(): lax.all_to_all(block, 'patch', split_axis=0, concat_axis=0, tiled=True)  17.2 us
    ppermute x2, waiting for transfers between devices, on_device(): lax.ppermute(packed, 'patch', pairs)  15.4 us
    pallas_call x2, Pallas kernels, warp_rows(): pl.pallas_call(functools.partial(warp_kernel, first), out_shape=(jax.Shap...  14.3 us
    pallas_call x1, Pallas kernels, match_rows(): pl.pallas_call(body, out_shape=(jax.ShapeDtypeStruct((visits, patch_rows,...  13.3 us
    pallas_call x1, Pallas kernels, sum_visits(): pl.pallas_call(sum_kernel, out_shape=jax.ShapeDtypeStruct(shape, jnp.floa...  10.2 us
    pallas_call x2, Pallas kernels, pack_rows(): pl.pallas_call(functools.partial(pack_kernel, first), out_shape=jax.Shape...  9.26 us
    dot_general x3, matrix products, windowed_coefs(): jnp.einsum('qbg,gx->qbx', table, one_hot, precision=lax.Precision.HIGHEST)  7.68 us
  transfers between devices with their start and end apart: 8, of which 5 were waited for; matrix products, arithmetic and copies ran while one was open for 15% of the time, Pallas kernels for 26%

profile of v9, /device:TPU:8, one launch (start us, length us, event | category | flops | bytes accessed | tf_op | source)
XLA Modules:
  0.0 172.8 jit_solution(8377542974476359588)
XLA Ops:
  0.6 4.6 %pack_rows.3 = f32[32,4,64,128]{3,2,1,0:T(8,128)} custom-call(s32[8,32]{1,0:T(8,128)} %places_ref.3, f32[8,1024,128]{2,1,0:T(8,128)} %bitcast.159), custom_call_target="tpu_custom_call" | custom-call | bytes 12582912 | tf_op jit(solution)/shard_map/pack_rows/pallas_call | solution.py:39
  5.2 8.8 %all-to-all-start = ((f32[32,4,64,128]{3,2,1,0:T(8,128)}), f32[32,4,64,128]{3,2,1,0:T(8,128)}, u32[]{:S(2)}, u32[]{:S(2)}) async-start(f32[32,4,64,128]{3,2,1,0:T(8,128)} %pack_rows.3), calls=%async_computation | async-start | bytes 8388608 | tf_op jit(solution)/shard_map/all_to_all | solution.py:675
  14.0 0.1 reduce.42
  14.2 2.1 %collective-permute-start = (f32[6400]{0:T(1024)S(1)}, f32[6400]{0:T(1024)S(1)}, u32[]{:S(2)}, u32[]{:S(2)}) collective-permute-start(f32[6400]{0:T(1024)S(1)} %pad_maximum_fusion.2), channel_id=1, source_target_pairs={{0,4},{4,8},{8,12},{12,16},{16,20},{20,24},{24,28},{28,32},{32,36}... | collective-permute-start | bytes 76808 | tf_op jit(solution)/shard_map/ppermute | solution.py:669
  16.3 5.6 %collective-permute-start.1 = (f32[6400]{0:T(1024)S(1)}, f32[6400]{0:T(1024)S(1)}, u32[]{:S(2)}, u32[]{:S(2)}) collective-permute-start(f32[6400]{0:T(1024)S(1)} %pad_maximum_fusion.2), channel_id=1, source_target_pairs={{4,0},{8,4},{12,8},{16,12},{20,16},{24,20},{28,24},{32,28},{36,32}... | collective-permute-start | bytes 76808 | tf_op jit(solution)/shard_map/ppermute | solution.py:669
  21.9 0.2 slice_reduce_fusion.22
  22.2 0.1 broadcast_in_dim.1242
  22.3 0.1 broadcast_in_dim.1236
  22.4 0.5 slice_reduce_fusion.41
  23.0 0.1 broadcast_in_dim.1230
  23.1 0.1 broadcast_in_dim.1224
  23.3 0.1 broadcast_in_dim.1218
  23.4 0.1 broadcast_in_dim.1212
  23.6 0.1 broadcast_in_dim.1206
  23.8 0.1 broadcast_in_dim.1200
  23.9 0.1 broadcast_in_dim.1194
  24.1 0.1 broadcast_in_dim.1188
  24.2 0.1 broadcast_in_dim.1182
  24.4 0.1 broadcast_in_dim.1176
  24.5 0.1 broadcast_in_dim.1170
  24.7 0.1 broadcast_in_dim.1164
  24.8 0.1 broadcast_in_dim.1158
  25.0 0.1 broadcast_in_dim.1152
  25.1 0.1 broadcast_in_dim.1146
  25.7 0.1 broadcast_in_dim.1122
  28.8 0.2 reshape.1380
  29.2 0.9 reduce-precision_convert_fusion.2
  30.2 0.2 fusion.59
  30.4 1.9 %reduce-precision_convert_fusion.1 = (bf16[576,32]{1,0:T(8,128)(2,1)S(1)}, f32[576,32]{1,0:T(8,128)S(1)}) fusion(f32[576]{0:T(1024)S(1)} %broadcast_in_dim.1348, pred[64,32]{1,0:T(8,128)(4,1)S(1)} %get-tuple-element.130, f32[576]{0:T(1024)S(1)} %broadcast_in_dim.1343, pred[64,32]{1,0:T(8,128)(4,1)S(1)} %get-tuple-element.131, ...), kind=kLoop, calls=%fused_computation.17 | loop fusion | flops 423936 | bytes 201984 | tf_op jit(solution)/shard_map/convert_element_type | solution.py:587
  32.3 0.2 slice_reduce_fusion.1
  32.5 0.5 slice_reduce_fusion.20
  33.1 0.1 pad_maximum_fusion.down_ref
  33.2 0.2 fusion.38
  33.4 1.5 fusion.10
  35.0 1.2 fusion.1.across_ref
  36.2 2.6 %convolution_bitcast_fusion.coef_ref = f32[8,9,4864]{2,1,0:T(8,128)} fusion(s32[4864]{0:T(1024)S(1)} %pad_bitcast_fusion.2, f32[8,1,9,32]{3,1,2,0:T(1,128)S(1)} %copy-done.7), kind=kOutput, calls=%fused_computation | convolution fusion | flops 134635520 | bytes 1429504 | tf_op jit(solution)/shard_map/qbg,gx->qbx/dot_general | solution.py:628
  38.8 0.8 pad_maximum_fusion.1.down_ref
  39.7 4.7 %pack_rows.2 = f32[32,4,64,128]{3,2,1,0:T(8,128)} custom-call(s32[8,32]{1,0:T(8,128)} %places_ref.3, f32[8,1024,128]{2,1,0:T(8,128)} %bitcast.160), custom_call_target="tpu_custom_call" | custom-call | bytes 12582912 | tf_op jit(solution)/shard_map/pack_rows/pallas_call | solution.py:39
  44.3 1.2 slice.204
  48.2 0.3 pad.32.shift_ref
  48.6 0.3 pad.31.taps_ref
  48.9 0.6 dynamic_slice.3.weight_ref
  49.5 15.4 %collective-permute-done = f32[6400]{0:T(1024)S(1)} collective-permute-done((f32[6400]{0:T(1024)S(1)}, f32[6400]{0:T(1024)S(1)}, u32[]{:S(2)}, u32[]{:S(2)}) %collective-permute-start) | collective-permute-done | bytes 25632 | tf_op jit(solution)/shard_map/ppermute | solution.py:669
  64.9 8.5 %all-to-all-start.1 = ((f32[32,4,64,128]{3,2,1,0:T(8,128)}), f32[32,4,64,128]{3,2,1,0:T(8,128)}, u32[]{:S(2)}, u32[]{:S(2)}) async-start(f32[32,4,64,128]{3,2,1,0:T(8,128)} %pack_rows.2), calls=%async_computation.1 | async-start | bytes 8388608 | tf_op jit(solution)/shard_map/all_to_all | solution.py:675
  73.5 0.1 reshape.1383
  73.7 0.1 reshape.1385
  73.9 2.5 %fusion.5.coef_up_ref = f32[8,9,4864]{2,1,0:T(8,128)} fusion(f32[8,9,32]{2,1,0:T(8,128)S(1)} %reshape.1382, s32[4864]{0:T(1024)S(1)} %pad_bitcast_fusion.1), kind=kOutput, calls=%fused_computation.11 | convolution fusion | flops 134635520 | bytes 1429504 | tf_op jit(solution)/shard_map/qbg,gx->qbx/dot_general | solution.py:628
  76.4 2.6 %fusion.8.coef_dn_ref = f32[8,9,4864]{2,1,0:T(8,128)} fusion(f32[8,9,32]{2,1,0:T(8,128)S(1)} %reshape.1384, s32[4864]{0:T(1024)S(1)} %pad_bitcast_fusion), kind=kOutput, calls=%fused_computation.13 | convolution fusion | flops 134635520 | bytes 1429504 | tf_op jit(solution)/shard_map/qbg,gx->qbx/dot_general | solution.py:628
  79.0 7.2 %warp_rows.2 = (f32[4,32,4224]{2,1,0:T(8,128)}, f32[4,8,5376]{2,1,0:T(8,128)}, f32[4,8,5376]{2,1,0:T(8,128)}) custom-call(s32[1]{0:T(128)} %bitcast.53.turn_ref, f32[32,4,64,128]{3,2,1,0:T(8,128)} %all-to-all-done.got_ref, f32[8,8,4224]{2,1,0:T(8,128)S(1)} %pad.31.taps_ref, s32[8,1,4224]{2,1,0:T(1,128)S(1)} %pad.32.shift_ref), custom_call_target="tpu_custom_call" | custom-call | bytes 50331648 | tf_op jit(solution)/shard_map/warp_rows/pallas_call | solution.py:146
  86.2 22.3 %spread_rows.1 = (f32[8,32,4096]{2,1,0:T(8,128)}, f32[32,4096]{1,0:T(8,128)}, f32[4,8,5120]{2,1,0:T(8,128)}, f32[4,8,5120]{2,1,0:T(8,128)}) custom-call(f32[8]{0:T(128)} %dynamic_slice.3.weight_ref, f32[4,32,4224]{2,1,0:T(8,128)} %get-tuple-element.35.warped_ref, bf16[576,96]{1,0:T(8,128)(2,1)} %pad_maximum_fusion.1.down_ref, ...), custom_call_target="tpu_custom_call" | custom-call | bytes 100663296 | tf_op jit(solution)/shard_map/spread_rows/pallas_call | solution.py:379
  108.5 2.1 %collective-permute-start.2 = (f32[4,8,5120]{2,1,0:T(8,128)}, f32[4,8,5120]{2,1,0:T(8,128)S(1)}, u32[]{:S(2)}, u32[]{:S(2)}) collective-permute-start(f32[4,8,5120]{2,1,0:T(8,128)} %get-tuple-element.47), channel_id=1, source_target_pairs={{0,4},{4,8},{8,12},{12,16},{16,20},{20,24},{24,28},{28,32},{32,36}... | collective-permute-start | bytes 1966088 | tf_op jit(solution)/shard_map/ppermute | solution.py:691
  110.5 5.6 %collective-permute-start.3 = (f32[4,8,5120]{2,1,0:T(8,128)}, f32[4,8,5120]{2,1,0:T(8,128)}, u32[]{:S(2)}, u32[]{:S(2)}) collective-permute-start(f32[4,8,5120]{2,1,0:T(8,128)} %get-tuple-element.48), channel_id=1, source_target_pairs={{4,0},{8,4},{12,8},{16,12},{20,16},{24,20},{28,24},{32,28},{36,32}... | collective-permute-start | bytes 1966088 | tf_op jit(solution)/shard_map/ppermute | solution.py:692
  116.2 7.5 %all-to-all-done.1.got_ref = f32[32,4,64,128]{3,2,1,0:T(8,128)} async-done(((f32[32,4,64,128]{3,2,1,0:T(8,128)}), f32[32,4,64,128]{3,2,1,0:T(8,128)}, u32[]{:S(2)}, u32[]{:S(2)}) %all-to-all-start.1) | async-done | bytes 4194336 | tf_op jit(solution)/shard_map/all_to_all | solution.py:675
  123.6 7.1 %warp_rows.3 = (f32[4,32,4224]{2,1,0:T(8,128)}, f32[4,8,5376]{2,1,0:T(8,128)S(1)}, f32[4,8,5376]{2,1,0:T(8,128)}) custom-call(s32[1]{0:T(128)} %bitcast.53.turn_ref, f32[32,4,64,128]{3,2,1,0:T(8,128)} %all-to-all-done.1.got_ref, f32[8,8,4224]{2,1,0:T(8,128)S(1)} %pad.31.taps_ref, s32[8,1,4224]{2,1,0:T(1,128)S(1)} %pad.32.shift_ref), custom_call_target="tpu_custom_call" | custom-call | bytes 50331648 | tf_op jit(solution)/shard_map/warp_rows/pallas_call | solution.py:146
  130.8 0.5 collective-permute-done.2.above_ref
  131.2 1.9 %collective-permute-start.4 = (f32[4,8,5376]{2,1,0:T(8,128)}, f32[4,8,5376]{2,1,0:T(8,128)S(1)}, u32[]{:S(2)}, u32[]{:S(2)}) collective-permute-start(f32[4,8,5376]{2,1,0:T(8,128)} %get-tuple-element.49), channel_id=1, source_target_pairs={{0,4},{4,8},{8,12},{12,16},{16,20},{20,24},{24,28},{28,32},{32,36}... | collective-permute-start | bytes 2064392 | tf_op jit(solution)/shard_map/ppermute | solution.py:698
  133.2 7.2 %collective-permute-start.5 = (f32[4,8,5376]{2,1,0:T(8,128)S(1)}, f32[4,8,5376]{2,1,0:T(8,128)S(1)}, u32[]{:S(2)}, u32[]{:S(2)}) collective-permute-start(f32[4,8,5376]{2,1,0:T(8,128)S(1)} %get-tuple-element.50), channel_id=1, source_target_pairs={{4,0},{8,4},{12,8},{16,12},{20,16},{24,20},{28,24},{32,28},{36,32}... | collective-permute-start | bytes 2064392 | tf_op jit(solution)/shard_map/ppermute | solution.py:699
  140.3 0.6 reduce_sum.9
  140.9 4.3 %add_edges.1 = (f32[8,32,4096]{2,1,0:T(8,128)}, f32[32,4096]{1,0:T(8,128)S(1)}) custom-call(f32[8]{0:T(128)S(1)} %copy-done.3, f32[4,8,5120]{2,1,0:T(8,128)S(1)} %collective-permute-done.2.above_ref, f32[4,8,5120]{2,1,0:T(8,128)} %collective-permute-done.3.below_ref, f32[8,32,4096]{2,1,0:T(8,128)} %get-tuple-element.54.before_ref, ...), custom_call_target="tpu_custom_call", output_to_operand_aliasing={{0}: (3, {})} | custom-call | bytes 12582912 | tf_op jit(solution)/shard_map/add_edges/pallas_call | solution.py:451
  145.3 1.7 collective-permute-done.4.above_ref
  147.0 1.5 collective-permute-done.5.below_ref
  148.5 13.3 %match_rows.1 = (f32[8,32,4096]{2,1,0:T(8,128)}, f32[32,4096]{1,0:T(8,128)S(1)}) custom-call(f32[8]{0:T(128)S(1)} %copy-done.3, f32[4,32,4224]{2,1,0:T(8,128)} %get-tuple-element.44.warped_ref, f32[4,8,5376]{2,1,0:T(8,128)S(1)} %collective-permute-done.4.above_ref, ...), custom_call_target="tpu_custom_call", output_to_operand_aliasing={{0}: (9, {})} | custom-call | bytes 83886080 | tf_op jit(solution)/shard_map/match_rows/pallas_call | solution.py:496
  161.9 10.2 %sum_visits.1 = f32[8,4096]{1,0:T(8,128)S(1)} custom-call(f32[32,4096]{1,0:T(8,128)S(1)} %get-tuple-element.59.total_ref, f32[1]{0:T(128)} %bitcast.60.scale_ref), custom_call_target="tpu_custom_call" | custom-call | tf_op jit(solution)/shard_map/sum_visits/pallas_call | solution.py:565
  172.1 0.7 copy.26
  (118 shorter events, 5.4 us)
Async XLA Ops:
  5.2 8.8 %copy-start.9 = (s32[1,4096]{1,0:T(1,128)S(1)}, s32[1,4096]{1,0:T(1,128)}, u32[]{:S(2)}) copy-start(s32[1,4096]{1,0:T(1,128)} %param.17) | copy-start | bytes 49156
  5.2 8.8 %copy-start.7 = (f32[8,1,9,32]{3,1,2,0:T(1,128)S(1)}, f32[8,1,9,32]{3,1,2,0:T(1,128)}, u32[]{:S(2)}) copy-start(f32[8,1,9,32]{3,1,2,0:T(1,128)} %param.16) | copy-start | bytes 27652
  5.2 16.7 %copy-start.4 = (f32[9,21]{1,0:T(8,128)S(1)}, f32[9,21]{1,0:T(8,128)}, u32[]{:S(2)}) copy-start(f32[9,21]{1,0:T(8,128)} %param.14) | copy-start | bytes 2272
  5.2 59.7 %all-to-all-start = ((f32[32,4,64,128]{3,2,1,0:T(8,128)}), f32[32,4,64,128]{3,2,1,0:T(8,128)}, u32[]{:S(2)}, u32[]{:S(2)}) async-start(f32[32,4,64,128]{3,2,1,0:T(8,128)} %pack_rows.3), calls=%async_computation | async-start | bytes 8388608 | tf_op jit(solution)/shard_map/all_to_all | solution.py:675
  14.0 18.3 %copy-start.5 = (f32[9,21]{1,0:T(8,128)S(1)}, f32[9,21]{1,0:T(8,128)}, u32[]{:S(2)}) copy-start(f32[9,21]{1,0:T(8,128)} %param.15) | copy-start | bytes 2272
  14.2 50.7 %collective-permute-start = (f32[6400]{0:T(1024)S(1)}, f32[6400]{0:T(1024)S(1)}, u32[]{:S(2)}, u32[]{:S(2)}) collective-permute-start(f32[6400]{0:T(1024)S(1)} %pad_maximum_fusion.2), channel_id=1, source_target_pairs={{0,4},{4,8},{8,12},{12,16},{16,20},{20,24},{24,28},{28,32},{32,36}... | collective-permute-start | bytes 76808 | tf_op jit(solution)/shard_map/ppermute | solution.py:669
  16.3 48.6 %collective-permute-start.1 = (f32[6400]{0:T(1024)S(1)}, f32[6400]{0:T(1024)S(1)}, u32[]{:S(2)}, u32[]{:S(2)}) collective-permute-start(f32[6400]{0:T(1024)S(1)} %pad_maximum_fusion.2), channel_id=1, source_target_pairs={{4,0},{8,4},{12,8},{16,12},{20,16},{24,20},{28,24},{32,28},{36,32}... | collective-permute-start | bytes 76808 | tf_op jit(solution)/shard_map/ppermute | solution.py:669
  39.6 8.5 %copy-start.8 = (s32[8,1,4096]{2,1,0:T(1,128)S(1)}, s32[8,1,4096]{2,1,0:T(1,128)}, u32[]{:S(2)}) copy-start(s32[8,1,4096]{2,1,0:T(1,128)} %param.13) | copy-start | bytes 393220
  39.7 8.9 %copy-start.6 = (f32[8,1,8,4096]{3,2,1,0:T(8,128)S(1)}, f32[8,1,8,4096]{3,2,1,0:T(8,128)}, u32[]{:S(2)}) copy-start(f32[8,1,8,4096]{3,2,1,0:T(8,128)} %param.12) | copy-start | bytes 3145732
  44.3 4.6 %copy-start.10 = (f32[32]{0:T(128)S(1)}, f32[32]{0:T(128)}, u32[]{:S(2)}) copy-start(f32[32]{0:T(128)} %param.19) | copy-start | bytes 388
  64.9 58.7 %all-to-all-start.1 = ((f32[32,4,64,128]{3,2,1,0:T(8,128)}), f32[32,4,64,128]{3,2,1,0:T(8,128)}, u32[]{:S(2)}, u32[]{:S(2)}) async-start(f32[32,4,64,128]{3,2,1,0:T(8,128)} %pack_rows.2), calls=%async_computation.1 | async-start | bytes 8388608 | tf_op jit(solution)/shard_map/all_to_all | solution.py:675
  108.5 22.8 %collective-permute-start.2 = (f32[4,8,5120]{2,1,0:T(8,128)}, f32[4,8,5120]{2,1,0:T(8,128)S(1)}, u32[]{:S(2)}, u32[]{:S(2)}) collective-permute-start(f32[4,8,5120]{2,1,0:T(8,128)} %get-tuple-element.47), channel_id=1, source_target_pairs={{0,4},{4,8},{8,12},{12,16},{16,20},{20,24},{24,28},{28,32},{32,36}... | collective-permute-start | bytes 1966088 | tf_op jit(solution)/shard_map/ppermute | solution.py:691
  110.5 20.7 %collective-permute-start.3 = (f32[4,8,5120]{2,1,0:T(8,128)}, f32[4,8,5120]{2,1,0:T(8,128)}, u32[]{:S(2)}, u32[]{:S(2)}) collective-permute-start(f32[4,8,5120]{2,1,0:T(8,128)} %get-tuple-element.48), channel_id=1, source_target_pairs={{4,0},{8,4},{12,8},{16,12},{20,16},{24,20},{28,24},{32,28},{36,32}... | collective-permute-start | bytes 1966088 | tf_op jit(solution)/shard_map/ppermute | solution.py:692
  116.1 24.8 %copy-start.2 = (f32[32,4096]{1,0:T(8,128)S(1)}, f32[32,4096]{1,0:T(8,128)}, u32[]{:S(2)}) copy-start(f32[32,4096]{1,0:T(8,128)} %get-tuple-element.55.sums_ref) | copy-start | bytes 1572868
  116.1 24.8 %copy-start.3 = (f32[8]{0:T(128)S(1)}, f32[8]{0:T(128)}, u32[]{:S(2)}) copy-start(f32[8]{0:T(128)} %dynamic_slice.3.weight_ref) | copy-start | bytes 100
  131.2 15.8 %collective-permute-start.4 = (f32[4,8,5376]{2,1,0:T(8,128)}, f32[4,8,5376]{2,1,0:T(8,128)S(1)}, u32[]{:S(2)}, u32[]{:S(2)}) collective-permute-start(f32[4,8,5376]{2,1,0:T(8,128)} %get-tuple-element.49), channel_id=1, source_target_pairs={{0,4},{4,8},{8,12},{12,16},{16,20},{20,24},{24,28},{28,32},{32,36}... | collective-permute-start | bytes 2064392 | tf_op jit(solution)/shard_map/ppermute | solution.py:698
  133.2 15.4 %collective-permute-start.5 = (f32[4,8,5376]{2,1,0:T(8,128)S(1)}, f32[4,8,5376]{2,1,0:T(8,128)S(1)}, u32[]{:S(2)}, u32[]{:S(2)}) collective-permute-start(f32[4,8,5376]{2,1,0:T(8,128)S(1)} %get-tuple-element.50), channel_id=1, source_target_pairs={{4,0},{8,4},{12,8},{16,12},{20,16},{24,20},{28,24},{32,28},{36,32}... | collective-permute-start | bytes 2064392 | tf_op jit(solution)/shard_map/ppermute | solution.py:699
  140.9 7.6 %copy-start = (bf16[9,256,256]{2,1,0:T(8,128)(2,1)S(1)}, bf16[9,256,256]{2,1,0:T(8,128)(2,1)}, u32[]{:S(2)}) copy-start(bf16[9,256,256]{2,1,0:T(8,128)(2,1)} %fusion.1.across_ref) | copy-start | bytes 3538948
  140.9 7.6 %copy-start.1 = (f32[32,4096]{1,0:T(8,128)S(1)}, f32[32,4096]{1,0:T(8,128)}, u32[]{:S(2)}) copy-start(f32[32,4096]{1,0:T(8,128)} %template_ref.3) | copy-start | bytes 1572868
